TPU v7x, 32 devices: a whole 2x2x4 slice. The times are simulated.
32 devices in a mesh: scene: 4 (over x, core), seq: 8 (over z, y).
Axes of the slice: x: 2, y: 2, z: 4, core: 2. Of those that a mesh axis runs over, the one named last changes fastest.
Arguments:
- tokens: bfloat16 [10240, 768], P(('scene', 'seq')), may hold values from -6 to 6
- scene_tokens: int32 [4], P('scene'), may hold values from 128 to 320, as said below
- cotangent: bfloat16 [10240, 768], P(('scene', 'seq')), may hold values from -6 to 6
- qkv_master: float32 [768, 2304], P(('scene', 'seq')), may hold values from -0.21875 to 0.21875
- out_master: float32 [768, 768], P(('scene', 'seq')), may hold values from -6 to 6
- up_master: float32 [768, 3072], P(('scene', 'seq')), may hold values from -0.21875 to 0.21875
- down_master: float32 [3072, 768], P(('scene', 'seq')), may hold values from -0.109375 to 0.109375
- gain_one: float32 [768], replicated, may hold values from 0.5 to 1.5
- gain_two: float32 [768], replicated, may hold values from 0.5 to 1.5
Outputs:
- mixed: bfloat16 [10240, 768], P(('scene', 'seq'))
- input_grad: float32 [10240, 768], P(('scene', 'seq'))
- qkv_grad: float32 [768, 2304], P(('scene', 'seq'))
- out_grad: float32 [768, 768], P(('scene', 'seq'))
- up_grad: float32 [768, 3072], P(('scene', 'seq'))
- down_grad: float32 [3072, 768], P(('scene', 'seq'))
- gain_one_grad: float32 [768], P(('scene', 'seq'))
- gain_two_grad: float32 [768], P(('scene', 'seq'))
Inputs may be any that keep to these rules, and one draw needn't show every extreme that they name: Slots 0 to scene_tokens[s] - 1 of every device of scene s's group hold that scene's tokens, the others are padding; one scene, drawn from the seed, has all 320 slots of every device live.
All inputs are finite; a program needn't handle non-finite values.
Results may differ from a plain program's by a relative error of at most 0.02.
Values may be sent and summed in bfloat16 or wider, within the bound.
No kernel may reach another device: no remote copies, remote signals or barrier semaphores. Data moves between devices by JAX's collectives and lax.ppermute only.
A program may use at most 512 MiB of HBM per device.

v0:
```python
import functools
import math

import jax
import jax.numpy as jnp
from jax import lax
from jax.experimental import pallas as pl
from jax.experimental.pallas import tpu as pltpu
from jax.sharding import Mesh
from jax.sharding import PartitionSpec as P

HEADS = 12
HEAD = 64
LANES = 128
NEG_BIG = -1e30
EPS = 1e-05
SCALE = 0.125
EXP_SCALE = SCALE * math.log2(math.e)
VMEM_LIMIT = 60 * 1024 * 1024
GELU_A = math.sqrt(2.0 / math.pi)
GELU_B = 0.044715
F32 = jnp.float32
BF16 = jnp.bfloat16
ALL = ("a", "c", "g", "r")


def nt(left, right):
    return lax.dot_general(left, right, (((1,), (1,)), ((), ())), preferred_element_type=F32)


def nn(left, right):
    return lax.dot_general(left, right, (((1,), (0,)), ((), ())), preferred_element_type=F32)


def tn(left, right):
    return lax.dot_general(left, right, (((0,), (0,)), ((), ())), preferred_element_type=F32)


def three_parts(value):
    first = value.astype(BF16)
    rest = value - first.astype(F32)
    second = rest.astype(BF16)
    third = (rest - second.astype(F32)).astype(BF16)
    return first, second, third


def block_rows(rows):
    return 256 if rows % 256 == 0 else rows


def attention_forward_kernel(n_own, live_ref, *refs):
    n_pieces = len(refs) - 6
    pieces, weight = refs[:n_pieces], refs[n_pieces]
    out_ref, query_ref, key_ref, value_ref, out_scr = refs[n_pieces + 1 :]
    rows = pieces[0].shape[0]
    half = rows // 2
    lane = lax.broadcasted_iota(jnp.int32, (rows, HEAD), 1)
    slot = lax.broadcasted_iota(jnp.int32, (rows, HEAD), 0)
    bias = jnp.where(slot < live_ref[0], 0.0, NEG_BIG)
    key_extra = jnp.where(lane == 0, bias, jnp.where(lane < 4, 1.0, 0.0)).astype(BF16)
    value_extra = jnp.where(lane < 3, 1.0, 0.0).astype(BF16)
    query_extra = jnp.where(lane == 0, 1.0, 0.0).astype(BF16)
    for index in range(n_pieces):
        made = nn(pieces[index][...], weight[0]).astype(BF16)
        here = slice(index * rows, (index + 1) * rows)
        key_ref[0, here, :] = jnp.concatenate([made[:, HEAD : 2 * HEAD], key_extra], axis=1)
        value_ref[0, here, :] = jnp.concatenate([made[:, 2 * HEAD :], value_extra], axis=1)
        if index < n_own:
            query_ref[0, here, :] = jnp.concatenate([made[:, :HEAD], query_extra], axis=1)

    size = block_rows(rows * n_own)
    blocks = rows * n_own // size
    full = lax.broadcasted_iota(jnp.int32, (size, LANES), 1)
    keys = key_ref[0]
    values = value_ref[0]
    scores = nt(query_ref[0, :size], keys)
    for block in range(blocks):
        here = slice(block * size, (block + 1) * size)
        later = None
        if block + 1 < blocks:
            later = nt(query_ref[0, (block + 1) * size : (block + 2) * size], keys)
        highest = jnp.max(scores, axis=1, keepdims=True)
        weights = jnp.exp2((scores - highest) * EXP_SCALE).astype(BF16)
        summed = nn(weights, values)
        total = summed[:, HEAD : HEAD + 1]
        out_scr[here, :] = summed / total
        first, second, third = three_parts(-(highest + jnp.log2(total) * (1.0 / EXP_SCALE)))
        query_ref[0, here, :] = jnp.where(
            full == HEAD + 1,
            first,
            jnp.where(
                full == HEAD + 2, second, jnp.where(full == HEAD + 3, third, query_ref[0, here, :])
            ),
        )
        scores = later
    for index in range(n_own):
        base = index * rows
        upper = out_scr[base : base + half, :HEAD]
        lower = out_scr[base + half : base + rows, :HEAD]
        out_ref[index, 0] = jnp.concatenate([upper, lower], axis=1).astype(BF16)


def attention_forward(live, pieces, weight, n_own):
    heads = weight.shape[0]
    rows, width = pieces[0].shape
    n_keys = rows * len(pieces)
    n_queries = rows * n_own
    half = rows // 2
    per_head = lambda n: pl.BlockSpec((1, n, LANES), lambda h: (h, 0, 0))
    return pl.pallas_call(
        functools.partial(attention_forward_kernel, n_own),
        grid=(heads,),
        in_specs=[pl.BlockSpec(memory_space=pltpu.SMEM)]
        + [pl.BlockSpec((rows, width), lambda h: (0, 0), pipeline_mode=pl.Buffered(1)) for _ in pieces]
        + [pl.BlockSpec((1, width, 3 * HEAD), lambda h: (h, 0, 0))],
        out_specs=[
            pl.BlockSpec((n_own, 1, half, LANES), lambda h: (0, h, 0, 0)),
            per_head(n_queries),
            per_head(n_keys),
            per_head(n_keys),
        ],
        out_shape=[
            jax.ShapeDtypeStruct((n_own, heads, half, LANES), BF16),
            jax.ShapeDtypeStruct((heads, n_queries, LANES), BF16),
            jax.ShapeDtypeStruct((heads, n_keys, LANES), BF16),
            jax.ShapeDtypeStruct((heads, n_keys, LANES), BF16),
        ],
        scratch_shapes=[pltpu.VMEM((n_queries, LANES), F32)],
        compiler_params=pltpu.CompilerParams(
            dimension_semantics=("arbitrary",), vmem_limit_bytes=VMEM_LIMIT
        ),
        name="attention_forward",
    )(live, *pieces, weight)


def attention_backward_kernel(rows, n_own, out_ref, query_ref, key_ref, value_ref, *refs):
    grads = refs[:n_own]
    own_ref, send_ref, grad_query_ref, grad_scr, low_scr, key_scr, query_scr, acc_scr = refs[n_own:]
    half = rows // 2
    lane = lax.broadcasted_iota(jnp.int32, (rows, HEAD), 1)
    for index in range(n_own):
        packed = grads[index][0]
        grad = jnp.concatenate([packed[:, :HEAD], packed[:, HEAD:]], axis=0)
        packed_out = out_ref[index, 0]
        attended = jnp.concatenate([packed_out[:, :HEAD], packed_out[:, HEAD:]], axis=0)
        delta = jnp.sum(grad.astype(F32) * attended.astype(F32), axis=1, keepdims=True)
        first, second, third = three_parts(-delta)
        zeros = jnp.zeros_like(grad)
        extra = jnp.where(
            lane == 0, first, jnp.where(lane == 1, second, jnp.where(lane == 2, third, zeros))
        )
        here = slice(index * rows, (index + 1) * rows)
        grad_scr[here, :] = jnp.concatenate([grad, extra], axis=1)
        low_scr[here, :] = jnp.concatenate([zeros, grad], axis=1)
    key_scr[...] = key_ref[0].T

    size = block_rows(rows * n_own)
    blocks = rows * n_own // size
    keys = key_ref[0]
    values = value_ref[0]
    full = lax.broadcasted_iota(jnp.int32, (size, LANES), 1)

    def products(block):
        here = slice(block * size, (block + 1) * size)
        return nt(keys, query_ref[0, here, :]), nt(values, grad_scr[here, :])

    scores, change = products(0)
    for block in range(blocks):
        here = slice(block * size, (block + 1) * size)
        later = products(block + 1) if block + 1 < blocks else (None, None)
        weights = jnp.exp2(scores * EXP_SCALE)
        dscore = (weights * change).astype(BF16)
        query = query_ref[0, here, :]
        plain = jnp.where(full < HEAD, query * SCALE, jnp.zeros_like(query))
        terms = nn(
            jnp.concatenate([weights.astype(BF16), dscore], axis=1),
            jnp.concatenate([low_scr[here, :], plain], axis=0),
        )
        if block == 0:
            acc_scr[...] = terms
        else:
            acc_scr[...] += terms
        query_scr[here, :] = nn(key_scr[...], dscore).T * SCALE
        scores, change = later
    for index in range(n_own):
        base = index * rows
        upper = query_scr[base : base + half, :HEAD]
        lower = query_scr[base + half : base + rows, :HEAD]
        grad_query_ref[index] = jnp.concatenate([upper, lower], axis=1).astype(BF16)
        own_ref[index] = acc_scr[base : base + rows, :]
    for index in range(send_ref.shape[0]):
        base = (n_own + index) * rows
        send_ref[index] = acc_scr[base : base + rows, :].astype(BF16)


def attention_backward(out, query, key, value, grads, head):
    n_own, _, half, _ = out.shape
    rows = 2 * half
    n_queries, n_keys = query.shape[1], key.shape[1]
    n_send = n_keys // rows - n_own
    per_head = lambda n: pl.BlockSpec((1, n, LANES), lambda i: (head, 0, 0))
    stacked = lambda k, n: pl.BlockSpec((k, 1, n, LANES), lambda i: (0, head, 0, 0))
    vmem = pl.BlockSpec(memory_space=pltpu.VMEM)
    return pl.pallas_call(
        functools.partial(attention_backward_kernel, rows, n_own),
        grid=(1,),
        in_specs=[stacked(n_own, half), per_head(n_queries), per_head(n_keys), per_head(n_keys)]
        + [per_head(half) for _ in grads],
        out_specs=[vmem, vmem, vmem],
        out_shape=[
            jax.ShapeDtypeStruct((n_own, rows, LANES), F32),
            jax.ShapeDtypeStruct((n_send, rows, LANES), BF16),
            jax.ShapeDtypeStruct((n_own, half, LANES), BF16),
        ],
        scratch_shapes=[
            pltpu.VMEM((n_queries, LANES), BF16),
            pltpu.VMEM((n_queries, LANES), BF16),
            pltpu.VMEM((LANES, n_keys), BF16),
            pltpu.VMEM((n_queries, LANES), F32),
            pltpu.VMEM((n_keys, LANES), F32),
        ],
        compiler_params=pltpu.CompilerParams(
            dimension_semantics=("arbitrary",), vmem_limit_bytes=VMEM_LIMIT
        ),
        name="attention_backward",
    )(out, query, key, value, *grads)


def unpack_rows(packed):
    heads = packed.shape[0]
    return jnp.concatenate(
        [
            jnp.concatenate([packed[h, :, :HEAD], packed[h, :, HEAD:]], axis=0)
            for h in range(heads)
        ],
        axis=1,
    )


def middle_kernel(sizes, scalar_ref, *refs):
    n_g, wide, width, rows, n_a, chunks = sizes
    refs = list(refs)

    def take(count):
        taken = refs[:count]
        del refs[:count]
        return taken

    token_ref, cotangent_ref, gain_ref = take(3)
    pieces = take(n_g)
    (weight_hbm,) = take(1)
    mixed_ref, resid_ref = take(2)
    grads = take(n_g)
    grad_hbm = [take(2 * n_a) for _ in chunks]
    weight_scr, made_scr, attended_scr, in_sem, out_sem = refs
    half = rows // 2
    part = width // n_g
    heads = part // HEAD
    block = width // (2 * n_a)
    here_a, here_c = scalar_ref[3], scalar_ref[2]

    def row_block(step_a, step_c):
        at_a = here_a + step_a
        at_a = jnp.where(at_a >= n_a, at_a - n_a, at_a)
        at_c = jnp.where(here_c + step_c >= 2, 0, here_c + step_c)
        return pl.ds(pl.multiple_of((at_a * 2 + at_c) * block, block), block)

    def chunk_of(index):
        first = 0
        for number, count in enumerate(chunks):
            if index < first + count:
                return number, pl.ds((index - first) * width, width)
            first += count

    def fetch(index):
        return [
            pltpu.make_async_copy(
                weight_hbm.at[:, pl.ds(index * width, width)],
                weight_scr.at[index],
                in_sem.at[index],
            )
        ]

    def flush(index):
        number, columns = chunk_of(index)
        return [
            pltpu.make_async_copy(
                made_scr.at[index, row_block(step_a, step_c)],
                grad_hbm[number][step_c * n_a + step_a].at[:, columns],
                out_sem.at[index, step_c * n_a + step_a],
            )
            for step_c in range(2)
            for step_a in range(n_a)
        ]

    def start(copies):
        for copy in copies:
            copy.start()

    def wait(copies):
        for copy in copies:
            copy.wait()

    count = 1 + 2 * wide
    for index in range(count):
        start(fetch(index))

    def places(k):
        at = scalar_ref[1] - k
        at = jnp.where(at < 0, at + n_g, at)
        return pl.ds(pl.multiple_of(at * part, part), part)

    resid = token_ref[...].astype(F32)
    for k in range(n_g):
        attended_scr[k] = unpack_rows(pieces[k][...])
    wait(fetch(0))
    for k in range(n_g):
        resid = resid + nn(attended_scr[k], weight_scr[0, places(k), :])
    gain = gain_ref[...]
    mean = jnp.mean(resid, axis=1, keepdims=True)
    centered = resid - mean
    inverse = lax.rsqrt(jnp.mean(centered * centered, axis=1, keepdims=True) + EPS)
    scaled = centered * inverse
    normed = (scaled * gain).astype(BF16)
    slot = lax.broadcasted_iota(jnp.int32, (rows, width), 0)
    grad_low = jnp.where(
        slot < scalar_ref[0], cotangent_ref[...].astype(F32), 0.0
    ).astype(BF16)
    normed_turned = normed.T
    added = None
    grad_normed = None
    for q in range(wide):
        up_at, down_at = 1 + 2 * q, 2 + 2 * q
        wait(fetch(up_at))
        upper = nn(normed, weight_scr[up_at])
        wait(fetch(down_at))
        grad_active = nt(grad_low, weight_scr[down_at])
        square = upper * upper
        inner = jnp.tanh((GELU_A * upper) * (1.0 + GELU_B * square))
        onward = 0.5 * (1.0 + inner)
        active = (upper * onward).astype(BF16)
        slope = onward + (0.5 * GELU_A) * upper * (1.0 - inner * inner) * (
            1.0 + (3.0 * GELU_B) * square
        )
        grad_upper = (grad_active * slope).astype(BF16)
        more = nn(active, weight_scr[down_at])
        added = more if added is None else added + more
        made_scr[down_at] = tn(active, grad_low).astype(BF16)
        start(flush(down_at))
        made_scr[up_at] = nn(normed_turned, grad_upper).astype(BF16)
        start(flush(up_at))
        more = nt(grad_upper, weight_scr[up_at])
        grad_normed = more if grad_normed is None else grad_normed + more
    mixed_ref[...] = (resid + added).astype(BF16)
    grad_scaled = grad_normed * gain
    first = jnp.mean(grad_scaled, axis=1, keepdims=True)
    second = jnp.mean(grad_scaled * scaled, axis=1, keepdims=True)
    grad_resid = grad_low.astype(F32) + inverse * (grad_scaled - first - scaled * second)
    resid_ref[...] = grad_resid
    branch = grad_resid.astype(BF16)
    for k in range(n_g):
        grad_block = nt(branch, weight_scr[0, places(k), :])
        for h in range(heads):
            here = slice(h * HEAD, (h + 1) * HEAD)
            grads[k][h] = jnp.concatenate(
                [grad_block[:half, here], grad_block[half:, here]], axis=1
            ).astype(BF16)
    for k in range(n_g):
        made_scr[0, places(k), :] = tn(attended_scr[k], branch).astype(BF16)
    start(flush(0))
    for index in range(count):
        wait(flush(index))


def middle(scalars, tokens, cotangent, gain, pieces, weights, n_a):
    rows, width = tokens.shape
    n_g = len(pieces)
    count = weights.shape[1] // width
    wide = (count - 1) // 2
    chunks = (1 + 2 * (wide // 2), 2 * (wide - wide // 2))
    vmem = pl.BlockSpec(memory_space=pltpu.VMEM)
    anywhere = pl.BlockSpec(memory_space=pl.ANY)
    flat = [
        jax.ShapeDtypeStruct((width // (2 * n_a), chunk * width), BF16)
        for chunk in chunks
        for _ in range(2 * n_a)
    ]
    return pl.pallas_call(
        functools.partial(middle_kernel, (n_g, wide, width, rows, n_a, chunks)),
        in_specs=[pl.BlockSpec(memory_space=pltpu.SMEM)] + [vmem] * (3 + n_g) + [anywhere],
        out_specs=[vmem] * (2 + n_g) + [anywhere] * len(flat),
        out_shape=[
            jax.ShapeDtypeStruct((rows, width), BF16),
            jax.ShapeDtypeStruct((rows, width), F32),
        ]
        + [jax.ShapeDtypeStruct(piece.shape, BF16) for piece in pieces]
        + flat,
        scratch_shapes=[
            pltpu.VMEM((count, width, width), BF16),
            pltpu.VMEM((count, width, width), BF16),
            pltpu.VMEM((n_g, rows, width // n_g), BF16),
            pltpu.SemaphoreType.DMA((count,)),
            pltpu.SemaphoreType.DMA((count, 2 * n_a)),
        ],
        compiler_params=pltpu.CompilerParams(vmem_limit_bytes=VMEM_LIMIT),
        name="middle",
    )(scalars, tokens, cotangent, gain, *pieces, weights)


def combine_kernel(rows, n_terms, own_ref, query_ref, *refs):
    terms, outs = refs[:n_terms], refs[n_terms:]
    for k, out_ref in enumerate(outs):
        total = own_ref[k]
        for term in terms:
            total = total + term[k].astype(F32)
        out_ref[:rows, :] = total.astype(BF16)
        out_ref[rows:, :] = query_ref[k]


def combine(own, grad_query, terms):
    n_g, rows, _ = own.shape
    vmem = pl.BlockSpec(memory_space=pltpu.VMEM)
    shape = (rows + grad_query.shape[1], LANES)
    return pl.pallas_call(
        functools.partial(combine_kernel, rows, len(terms)),
        in_specs=[vmem] * (2 + len(terms)),
        out_specs=[vmem] * n_g,
        out_shape=[jax.ShapeDtypeStruct(shape, BF16)] * n_g,
        compiler_params=pltpu.CompilerParams(vmem_limit_bytes=VMEM_LIMIT),
        name="combine",
    )(own, grad_query, *terms)


def unpack_grads(pieces, rows):
    parts = []
    for piece in pieces:
        packed = piece[rows:, :]
        parts.append(jnp.concatenate([packed[:, :HEAD], packed[:, HEAD:]], axis=0))
        parts.append(piece[:rows, :])
    return jnp.concatenate(parts, axis=1)


def group_grad_kernel(n_g, n_a, scalar_ref, *refs):
    inputs, pieces = refs[:n_g], refs[n_g:-3]
    mine_ref, other_ref, scr = refs[-3:]
    heads = len(pieces) // n_g
    rows = inputs[0].shape[0]
    left = jnp.concatenate([ref[...] for ref in inputs], axis=0)
    right = [
        unpack_grads([ref[...] for ref in pieces[k * heads : (k + 1) * heads]], rows)
        for k in range(n_g)
    ]
    right = jnp.concatenate(right, axis=0)
    scr[...] = tn(left, right)
    block = mine_ref.shape[1]
    n_c = scr.shape[0] // (n_a * block)
    for a in range(n_a):
        mine = pl.ds(pl.multiple_of((a * n_c + scalar_ref[2]) * block, block), block)
        other = pl.ds(pl.multiple_of((a * n_c + n_c - 1 - scalar_ref[2]) * block, block), block)
        mine_ref[a] = scr[mine, :]
        other_ref[a] = scr[other, :].astype(BF16)


def group_grad(scalars, inputs, pieces, n_a, n_c):
    rows, width = inputs[0].shape
    n_g = len(pieces)
    heads = len(pieces[0])
    columns = heads * 3 * HEAD
    block = width // (n_a * n_c)
    vmem = pl.BlockSpec(memory_space=pltpu.VMEM)
    return pl.pallas_call(
        functools.partial(group_grad_kernel, n_g, n_a),
        in_specs=[pl.BlockSpec(memory_space=pltpu.SMEM)] + [vmem] * (n_g * (1 + heads)),
        out_specs=[vmem] * 2,
        out_shape=[
            jax.ShapeDtypeStruct((n_a, block, columns), F32),
            jax.ShapeDtypeStruct((n_a, block, columns), BF16),
        ],
        scratch_shapes=[pltpu.VMEM((width, columns), F32)],
        compiler_params=pltpu.CompilerParams(vmem_limit_bytes=VMEM_LIMIT),
        name="group_grad",
    )(scalars, *inputs, *(piece for some in pieces for piece in some))


def input_grad_kernel(n_g, scalar_ref, token_ref, resid_ref, gain_ref, weight_ref, *refs):
    pieces, (out_ref, scr) = refs[:-2], refs[-2:]
    heads = len(pieces) // n_g
    rows, width = token_ref.shape
    padded = scr.shape[2]
    for k in range(n_g):
        at = scalar_ref[1] - k
        at = jnp.where(at < 0, at + n_g, at)
        made = unpack_grads([ref[...] for ref in pieces[k * heads : (k + 1) * heads]], rows)
        pad = jnp.zeros((rows, padded - made.shape[1]), BF16)
        scr[at] = jnp.concatenate([made, pad], axis=1)
    grad = nt(scr[0], weight_ref[:, :padded])
    for k in range(1, n_g):
        grad = grad + nt(scr[k], weight_ref[:, k * padded : (k + 1) * padded])
    values = token_ref[...].astype(F32)
    mean = jnp.mean(values, axis=1, keepdims=True)
    centered = values - mean
    inverse = lax.rsqrt(jnp.mean(centered * centered, axis=1, keepdims=True) + EPS)
    scaled = centered * inverse
    grad_scaled = grad * gain_ref[...]
    first = jnp.mean(grad_scaled, axis=1, keepdims=True)
    second = jnp.mean(grad_scaled * scaled, axis=1, keepdims=True)
    out_ref[...] = resid_ref[...] + inverse * (grad_scaled - first - scaled * second)


def input_gradient(scalars, tokens, grad_resid, gain, weight, pieces):
    rows, width = tokens.shape
    n_g = len(pieces)
    flat = [piece for some in pieces for piece in some]
    vmem = pl.BlockSpec(memory_space=pltpu.VMEM)
    return pl.pallas_call(
        functools.partial(input_grad_kernel, n_g),
        in_specs=[pl.BlockSpec(memory_space=pltpu.SMEM)] + [vmem] * (4 + len(flat)),
        out_specs=vmem,
        out_shape=jax.ShapeDtypeStruct((rows, width), F32),
        scratch_shapes=[pltpu.VMEM((n_g, rows, weight.shape[1] // n_g), BF16)],
        compiler_params=pltpu.CompilerParams(vmem_limit_bytes=VMEM_LIMIT),
        name="input_gradient",
    )(scalars, tokens, grad_resid, gain, weight, *flat)


def norm_rows(values, gain_vector):
    mean_value = jnp.mean(values, axis=-1, keepdims=True)
    centered = values - mean_value
    variance = jnp.mean(centered * centered, axis=-1, keepdims=True)
    return centered * lax.rsqrt(variance + EPS) * gain_vector


def shift(value, axis, step):
    n = lax.axis_size(axis)
    return lax.ppermute(value, axis, [(i, (i + step) % n) for i in range(n)])


def gather(value, axis):
    n = lax.axis_size(axis)
    if n == 1:
        return value[None]
    if n == 2:
        other = shift(value, axis, 1)
        first = lax.axis_index(axis) == 0
        return jnp.stack([jnp.where(first, value, other), jnp.where(first, other, value)])
    return lax.all_gather(value, axis, axis=0)


def after(value, *others):
    return lax.optimization_barrier((value,) + others)[0]


def add_high(*terms):
    total = terms[0].astype(F32)
    for term in terms[1:]:
        total = total + term.astype(F32)
    return total


def add_low(*terms):
    return add_high(*terms).astype(BF16)


def halves(value, axis, dim):
    n = lax.axis_size(axis)
    me = lax.axis_index(axis)
    mine = lax.dynamic_index_in_dim(value, me, dim, keepdims=False)
    others = [
        lax.dynamic_index_in_dim(value, (me + j) % n, dim, keepdims=False).astype(BF16)
        for j in range(1, n)
    ]
    return mine, others


def sum_halves(mine, others, axis):
    return add_high(mine, *(shift(other, axis, j) for j, other in enumerate(others, 1)))


def scatter_sum(value, axis, dim):
    return sum_halves(*halves(value, axis, dim), axis)


def on_device(
    tokens,
    scene_tokens,
    cotangent,
    qkv_master,
    out_master,
    up_master,
    down_master,
    gain_one,
    gain_two,
):
    rows, width = tokens.shape
    hidden = up_master.shape[1]
    n_a, n_c, n_g, n_r = (lax.axis_size(axis) for axis in ALL)
    share = qkv_master.shape[0]
    wide = hidden // width
    heads = HEADS // n_g
    live_count = scene_tokens[0]

    normed_low = norm_rows(tokens.astype(F32), gain_one).astype(BF16)
    qkv_low = qkv_master.astype(BF16)
    parts = qkv_low.reshape(share, 3, n_g, heads, HEAD).transpose(2, 0, 3, 1, 4)
    parts = parts.reshape(n_g, share, heads * 3 * HEAD)
    own_pieces = [normed_low] * n_g
    for k in {1, n_g - 1}:
        own_pieces[k] = shift(normed_low, "g", -k)
    ready = [own_pieces[1], own_pieces[n_g - 1]]
    others = {(j, 0): shift(normed_low, "r", -j) for j in range(1, n_r)}
    ready += others.values()
    parts = lax.all_to_all(parts, "g", 0, 0)
    ready.append(parts)
    for k in range(2, n_g - 1):
        own_pieces[k] = shift(after(own_pieces[k - 1], *ready), "g", -1)
    for k in sorted(range(1, n_g), key=lambda k: min(k, n_g - k)):
        for j in range(1, n_r):
            others[j, k] = shift(after(own_pieces[k], *ready), "r", -j)
    pieces = own_pieces + [others[at] for at in sorted(others)]

    n_all = n_a * n_c * n_g * n_r
    up_low = up_master.astype(BF16)
    up_turned = (
        up_low.reshape(share, n_all, wide, share).transpose(0, 2, 1, 3).reshape(share, wide, width)
    )
    down_turned = down_master.astype(BF16).reshape(wide, share, width)
    blocks = [out_master.astype(BF16)]
    for q in range(wide):
        blocks += [up_turned[:, q], down_turned[q]]
    weights = lax.all_gather(jnp.concatenate(blocks, axis=1), ALL, axis=0, tiled=True)

    parts = gather(gather(gather(after(parts, *ready), "r"), "c"), "a")
    parts = parts.reshape(n_a, n_c, n_r, n_g, share, heads, 3 * HEAD)
    group_weight = parts.transpose(5, 0, 1, 3, 2, 4, 6).reshape(heads, width, 3 * HEAD)

    scalars = jnp.stack(
        [live_count, lax.axis_index("g"), lax.axis_index("c"), lax.axis_index("a")]
    )
    out, query, key, value = attention_forward(scene_tokens, pieces, group_weight, n_g)
    back = [out[0]] + [shift(out[k], "g", k) for k in range(1, n_g)]
    made = middle(scalars, tokens, cotangent, gain_two[None], back, weights, n_a)
    mixed, grad_resid, sends = made[0], made[1], made[2 : 2 + n_g]
    grad_blocks = [made[2 + n_g : 2 + n_g + n_a * n_c], made[2 + n_g + n_a * n_c :]]

    terms = [[(block, shift(there, "c", 1)) for block, there in zip(some[:n_a], some[n_a:])] for some in grad_blocks]
    far = [add_low(*pair) for pair in terms[0][1:]]
    near = jnp.stack([add_high(*pair).reshape(n_g, n_r, share, -1) for pair in terms[1]])
    mine, other = halves(near, "r", 2)

    columns = heads * 3 * HEAD
    padded = -(-columns // LANES) * LANES
    turned = qkv_low.reshape(share, 3, n_g, heads, HEAD).transpose(0, 2, 3, 1, 4)
    turned = jnp.pad(turned.reshape(share, n_g, columns), ((0, 0), (0, 0), (0, padded - columns)))
    turned = after(turned.reshape(share, n_g * padded), *ready)
    qkv_weight = lax.all_gather(turned, ALL, axis=0, tiled=True)

    grads = [sends[0]] + [shift(sends[k], "g", -k) for k in range(1, n_g)]
    gate = [*far, *other]
    far = [shift(block, "a", k) for k, block in enumerate(far, 1)]
    other = [shift(block, "r", j) for j, block in enumerate(other, 1)]

    made = []
    grad_pieces = []
    whole = []

    def finish(head):
        own, across, grad_query = made[head]
        own = after(own, made[min(head + 1, heads - 1)][0])
        if head >= 2:
            own = after(own, *whole[head - 2])
        done = combine(own, grad_query, across)
        grad_pieces.append(done)
        whole.append([done[0]] + [shift(done[k], "g", k) for k in range(1, n_g)])

    for head in range(heads):
        if head == 1:
            gate = [made[0][0]]
        if head >= 2:
            finish(head - 2)
            gate = [*grad_pieces[head - 2], qkv_weight]
        if head == 2:
            first = add_high(*terms[0][0], *(after(block, made[1][0], *made[0][1]) for block in far))
            first, send = halves(first.reshape(n_g, n_r, share, -1), "r", 1)
            gate += send
            send = [shift(block, "r", j) for j, block in enumerate(send, 1)]
        gated = [after(grads[0], *gate)] + grads[1:]
        own, across, grad_query = attention_backward(out, query, key, value, gated, head)
        across = [
            shift(across[(j - 1) * n_g : j * n_g] if n_r > 2 else across, "r", j)
            for j in range(1, n_r)
        ]
        made.append((own, across, grad_query))
    finish(heads - 2)
    first = add_high(first, *(after(block, *made[-1][1]) for block in send)).astype(BF16)
    near = add_high(mine, *(after(block, *made[-1][1]) for block in other))
    second = add_low(near[0], *(shift(near[k].astype(BF16), "a", k) for k in range(1, n_a)))
    finish(heads - 1)
    first = lax.all_to_all(after(first, *whole[-2], *whole[-1]), "g", 0, 0)
    grad_pieces = [[some[k] for some in grad_pieces] for k in range(n_g)]
    whole = [[some[k] for some in whole] for k in range(n_g)]

    mine, theirs = group_grad(scalars, own_pieces, grad_pieces, n_a, n_c)
    qkv_grad = add_high(mine, shift(theirs, "c", 1))
    qkv_grad = qkv_grad.reshape(n_a, n_g, n_r, share, columns)
    qkv_grad = scatter_sum(scatter_sum(qkv_grad, "a", 0), "r", 1)
    last = [some[-1] for some in whole[1:]]
    second = jnp.concatenate([qkv_grad.astype(BF16), second], axis=2)
    second = lax.all_to_all(after(second, *last), "g", 0, 0)

    input_grad = input_gradient(scalars, tokens, grad_resid, gain_one[None], qkv_weight, whole)

    qkv_share = (
        second[:, :, :columns]
        .astype(F32)
        .reshape(n_g, share, heads, 3, HEAD)
        .transpose(1, 3, 0, 2, 4)
        .reshape(share, 3 * width)
    )
    shares = []
    for total in (first, second[:, :, columns:]):
        total = jnp.sum(total.astype(F32), axis=0)
        shares += [
            total[:, at * width : (at + 1) * width] for at in range(total.shape[1] // width)
        ]
    out_share = shares[0]
    up_turned_share = jnp.stack(shares[1::2], axis=1)
    up_share = (
        up_turned_share.reshape(share, wide, n_all, share)
        .transpose(0, 2, 1, 3)
        .reshape(share, hidden)
    )
    down_share = jnp.concatenate(shares[2::2], axis=0)

    place = lax.axis_index(ALL) * share
    own_gain_one = lax.dynamic_slice_in_dim(gain_one, place, share)
    own_gain_two = lax.dynamic_slice_in_dim(gain_two, place, share)
    first_share = jnp.sum(qkv_low.astype(F32) * qkv_share, axis=1) / own_gain_one
    second_share = jnp.sum(up_turned.astype(F32) * up_turned_share, axis=(1, 2)) / own_gain_two
    return (
        mixed,
        input_grad,
        qkv_share,
        out_share,
        up_share,
        down_share,
        first_share,
        second_share,
    )


def solution(mesh):
    n_scene, n_seq = mesh.devices.shape
    n_g = math.gcd(HEADS, n_seq)
    inner = Mesh(mesh.devices.reshape(n_scene // 2, 2, n_g, n_seq // n_g), ALL)
    split = P(ALL, None)
    in_specs = (split, P(("a", "c")), split, split, split, split, split, P(), P())
    out_specs = (split, split, split, split, split, split, P(ALL), P(ALL))
    return jax.shard_map(
        on_device, mesh=inner, in_specs=in_specs, out_specs=out_specs, check_vma=False
    )
```

profile of v0, /device:TPU:0, one launch (start us, length us, event | category | flops | bytes accessed | tf_op | source)
XLA Modules:
  0.0 341.5 jit_solution(17000419088318478490)
XLA Ops:
  8.2 1.2 reshape.109
  9.6 1.2 reshape.110
  12.6 5.1 %collective-permute-start = (bf16[320,768]{1,0:T(8,128)(2,1)S(1)}, bf16[320,768]{1,0:T(8,128)(2,1)S(1)}, u32[]{:S(2)}, u32[]{:S(2)}) collective-permute-start(bf16[320,768]{1,0:T(8,128)(2,1)S(1)} %fusion.14.refs_0_), channel_id=1, source_target_pairs={{0,6},{2,0},{4,2},{6,4},{1,7},{3,1},{5,3},{7,5},{8,14},{10,8},{12,... | collective-permute-start | bytes 1474568 | tf_op jit(solution)/shard_map/ppermute | solution.py:535
  17.7 1.5 collective-permute-start.2
  19.8 28.2 %all_to_all.15 = bf16[4,24,576]{2,1,0:T(8,128)(2,1)S(1)} all-to-all(bf16[4,24,576]{2,1,0:T(8,128)(2,1)S(1)} %reshape.107), channel_id=1, replica_groups=mesh['a'=2,'c'=2,'g'=4,'r'=2] {'g'}, dimensions={0} | all-to-all | bytes 221184 | tf_op jit(solution)/shard_map/all_to_all | solution.py:612
  48.1 1.6 collective-permute-start.7
  49.6 4.9 %collective-permute-done.7 = bf16[4,24,576]{2,1,0:T(8,128)(2,1)S(1)} collective-permute-done((bf16[4,24,576]{2,1,0:T(8,128)(2,1)S(1)}, bf16[4,24,576]{2,1,0:T(8,128)(2,1)S(1)}, u32[]{:S(2)}, u32[]{:S(2)}) %collective-permute-start.7) | collective-permute-done | bytes 110624 | tf_op jit(solution)/shard_map/ppermute | solution.py:535
  55.8 4.1 %collective-permute-start.3 = (bf16[320,768]{1,0:T(8,128)(2,1)S(1)}, bf16[320,768]{1,0:T(8,128)(2,1)}, u32[]{:S(2)}, u32[]{:S(2)}) collective-permute-start(bf16[320,768]{1,0:T(8,128)(2,1)S(1)} %collective-permute-done.refs_1_), channel_id=1, source_target_pairs={{0,6},{2,0},{4,2},{6,4},{1,7},{3,1},{5,3},{7,5},{8,14},{10,8},{12,... | collective-permute-start | bytes 1474568 | tf_op jit(solution)/shard_map/ppermute | solution.py:535
  60.0 1.5 collective-permute-start.9
  61.6 2.5 collective-permute-start.4
  64.1 13.9 %collective-permute-done.3.refs_2_ = bf16[320,768]{1,0:T(8,128)(2,1)} collective-permute-done((bf16[320,768]{1,0:T(8,128)(2,1)S(1)}, bf16[320,768]{1,0:T(8,128)(2,1)}, u32[]{:S(2)}, u32[]{:S(2)}) %collective-permute-start.3) | collective-permute-done | bytes 491552 | tf_op jit(solution)/shard_map/ppermute | solution.py:535
  78.0 1.6 collective-permute-start.5
  81.1 1.2 maximum_bitcast_fusion
  82.4 1.2 copy.22
  83.6 4.1 %collective-permute-done.6.refs_7_ = bf16[320,768]{1,0:T(8,128)(2,1)} collective-permute-done((bf16[320,768]{1,0:T(8,128)(2,1)S(1)}, bf16[320,768]{1,0:T(8,128)(2,1)}, u32[]{:S(2)}, u32[]{:S(2)}) %collective-permute-start.6) | collective-permute-done | bytes 491552 | tf_op jit(solution)/shard_map/ppermute | solution.py:535
  87.7 20.1 %collective-permute-done.5.refs_6_ = bf16[320,768]{1,0:T(8,128)(2,1)} collective-permute-done((bf16[320,768]{1,0:T(8,128)(2,1)}, bf16[320,768]{1,0:T(8,128)(2,1)}, u32[]{:S(2)}, u32[]{:S(2)}) %collective-permute-start.5) | collective-permute-done | bytes 491552 | tf_op jit(solution)/shard_map/ppermute | solution.py:535
  107.8 19.6 %attention_forward.1 = (bf16[4,3,160,128]{3,2,1,0:T(8,128)(2,1)}, bf16[3,1280,128]{2,1,0:T(8,128)(2,1)}, bf16[3,2560,128]{2,1,0:T(8,128)(2,1)}, bf16[3,2560,128]{2,1,0:T(8,128)(2,1)}) custom-call(s32[1]{0:T(128)S(6)} %copy.55.live_ref, bf16[320,768]{1,0:T(8,128)(2,1)} %copy-done.8, bf16[320,768]{1,0:T(8,128)(2,1)} %copy-done.9, ...), custom_call_target="tpu_custom_call" | custom-call | tf_op jit(solution)/shard_map/attention_forward/pallas_call | solution.py:110
  127.5 1.8 slice_bitcast_fusion.1
  129.2 4.3 %collective-permute-start.12 = (bf16[3,160,128]{2,1,0:T(8,128)(2,1)S(1)}, bf16[3,160,128]{2,1,0:T(8,128)(2,1)S(1)}, u32[]{:S(2)}, u32[]{:S(2)}) collective-permute-start(bf16[3,160,128]{2,1,0:T(8,128)(2,1)S(1)} %get-tuple-element.128), channel_id=1, source_target_pairs={{0,6},{2,0},{4,2},{6,4},{1,7},{3,1},{5,3},{7,5},{8,14},{10,8},{12,... | collective-permute-start | bytes 368648 | tf_op jit(solution)/shard_map/ppermute | solution.py:535
  134.8 1.3 collective-permute-done.10.refs_4_
  136.1 2.9 collective-permute-done.11.refs_5_
  139.6 22.6 %middle.1 = (bf16[320,768]{1,0:T(8,128)(2,1)}, f32[320,768]{1,0:T(8,128)}, bf16[3,160,128]{2,1,0:T(8,128)(2,1)}, bf16[3,160,128]{2,1,0:T(8,128)(2,1)}, bf16[3,16...) custom-call(s32[4]{0:T(128)} %pad_add_fusion.scalar_ref, ...), custom_call_target="tpu_custom_call" | custom-call | tf_op jit(solution)/shard_map/middle/pallas_call | solution.py:388
  162.9 2.3 collective-permute-start.16
  166.3 1.8 collective-permute-start.18
  168.1 1.7 convert_add_fusion.2
  169.9 2.9 add_convert_fusion
  173.4 1.2 copy-done
  174.7 4.1 %collective-permute-done.17.refs_2_ = bf16[3,160,128]{2,1,0:T(8,128)(2,1)S(1)} collective-permute-done((bf16[3,160,128]{2,1,0:T(8,128)(2,1)}, bf16[3,160,128]{2,1,0:T(8,128)(2,1)S(1)}, u32[]{:S(2)}, u32[]{:S(2)}) %collective-permute-start.17) | collective-permute-done | bytes 122912 | tf_op jit(solution)/shard_map/ppermute | solution.py:535
  179.4 10.2 %attention_backward.3 = (f32[4,320,128]{2,1,0:T(8,128)}, bf16[4,320,128]{2,1,0:T(8,128)(2,1)}, bf16[4,160,128]{2,1,0:T(8,128)(2,1)}) custom-call(bf16[4,3,160,128]{3,2,1,0:T(8,128)(2,1)} %get-tuple-element.70.out_ref, bf16[3,1280,128]{2,1,0:T(8,128)(2,1)} %get-tuple-element.74.query_ref, bf16[3,2560,128]{2,1,0:T(8,128)(2,1)} %get-tuple-element.75.key_ref, ...), custom_call_target="tpu_custom_call" | custom-call | tf_op jit(solution)/shard_map/attention_backward/pallas_call | solution.py:204
  189.6 2.0 collective-permute-start.19
  191.6 10.4 %attention_backward.4 = (f32[4,320,128]{2,1,0:T(8,128)}, bf16[4,320,128]{2,1,0:T(8,128)(2,1)}, bf16[4,160,128]{2,1,0:T(8,128)(2,1)}) custom-call(bf16[4,3,160,128]{3,2,1,0:T(8,128)(2,1)} %get-tuple-element.70.out_ref, bf16[3,1280,128]{2,1,0:T(8,128)(2,1)} %get-tuple-element.74.query_ref, bf16[3,2560,128]{2,1,0:T(8,128)(2,1)} %get-tuple-element.75.key_ref, ...), custom_call_target="tpu_custom_call" | custom-call | tf_op jit(solution)/shard_map/attention_backward/pallas_call | solution.py:204
  202.1 2.0 collective-permute-start.22
  204.8 2.1 combine.3
  206.8 8.0 %collective-permute-done.21 = bf16[192,3840]{1,0:T(8,128)(2,1)} collective-permute-done((bf16[192,3840]{1,0:T(8,128)(2,1)}, bf16[192,3840]{1,0:T(8,128)(2,1)}, u32[]{:S(2)}, u32[]{:S(2)}) %collective-permute-start.21) | collective-permute-done | bytes 1474592 | tf_op jit(solution)/shard_map/ppermute | solution.py:535
  214.9 2.7 convert_add_fusion
  217.6 1.6 copy-done.2
  220.2 10.6 %attention_backward.5 = (f32[4,320,128]{2,1,0:T(8,128)}, bf16[4,320,128]{2,1,0:T(8,128)(2,1)}, bf16[4,160,128]{2,1,0:T(8,128)(2,1)}) custom-call(bf16[4,3,160,128]{3,2,1,0:T(8,128)(2,1)} %get-tuple-element.70.out_ref, bf16[3,1280,128]{2,1,0:T(8,128)(2,1)} %get-tuple-element.74.query_ref, bf16[3,2560,128]{2,1,0:T(8,128)(2,1)} %get-tuple-element.75.key_ref, ...), custom_call_target="tpu_custom_call" | custom-call | tf_op jit(solution)/shard_map/attention_backward/pallas_call | solution.py:204
  230.8 2.5 collective-permute-start.26
  234.2 1.7 collective-permute-start.24
  235.9 5.6 %collective-permute-done.23.refs_3_ = bf16[480,128]{1,0:T(8,128)(2,1)} collective-permute-done((bf16[480,128]{1,0:T(8,128)(2,1)S(1)}, bf16[480,128]{1,0:T(8,128)(2,1)}, u32[]{:S(2)}, u32[]{:S(2)}) %collective-permute-start.23) | collective-permute-done | bytes 122912 | tf_op jit(solution)/shard_map/ppermute | solution.py:535
  241.5 3.8 %collective-permute-done.24.refs_6_ = bf16[480,128]{1,0:T(8,128)(2,1)} collective-permute-done((bf16[480,128]{1,0:T(8,128)(2,1)}, bf16[480,128]{1,0:T(8,128)(2,1)}, u32[]{:S(2)}, u32[]{:S(2)}) %collective-permute-start.24) | collective-permute-done | bytes 122912 | tf_op jit(solution)/shard_map/ppermute | solution.py:535
  246.7 2.0 combine.4
  248.7 1.2 collective-permute-start.27
  249.9 1.2 collective-permute-start.29
  251.1 1.5 collective-permute-start.31
  252.6 2.0 combine.5
  254.6 5.5 %group_grad.1 = (f32[2,192,576]{2,1,0:T(8,128)}, bf16[2,192,576]{2,1,0:T(8,128)(2,1)}) custom-call(s32[4]{0:T(128)} %pad_add_fusion.scalar_ref, bf16[320,768]{1,0:T(8,128)(2,1)} %copy-done.8, bf16[320,768]{1,0:T(8,128)(2,1)} %copy-done.9, bf16[320,768]{1,0:T(8,128)(2,1)} %collective-permute-done.3.refs_2_, bf16[320,768]{1,0:T(8,128)(2,1)} %copy-done.10, ...), custom_call_target="tpu_custom_call" | custom-call | tf_op jit(solution)/shard_map/group_grad/pallas_call | solution.py:471
  260.3 1.9 fusion.2
  263.8 1.7 collective-permute-start.30
  266.4 2.7 collective-permute-start.32
  269.4 1.7 collective-permute-start.34
  271.1 2.1 fusion.6
  273.3 2.8 collective-permute-done.30.refs_8_
  276.7 5.0 %all-to-all-start.2 = ((bf16[4,24,3840]{2,1,0:T(8,128)(2,1)}), bf16[4,24,3840]{2,1,0:T(8,128)(2,1)}, u32[]{:S(2)}, u32[]{:S(2)}) async-start(bf16[4,24,3840]{2,1,0:T(8,128)(2,1)} %fusion.6), calls=%async_computation.2 | async-start | bytes 1474560 | tf_op jit(solution)/shard_map/all_to_all | solution.py:698
  281.6 7.9 %collective-permute-done.34 = bf16[4,2,24,576]{3,2,0,1:T(8,128)(2,1)} collective-permute-done((bf16[4,2,24,576]{3,2,0,1:T(8,128)(2,1)}, bf16[4,2,24,576]{3,2,0,1:T(8,128)(2,1)}, u32[]{:S(2)}, u32[]{:S(2)}) %collective-permute-start.34) | collective-permute-done | bytes 221216 | tf_op jit(solution)/shard_map/ppermute | solution.py:535
  291.2 1.2 fusion.9
  292.4 3.1 collective-permute-done.35
  296.6 4.0 %all-to-all-done.2 = bf16[4,24,3840]{2,1,0:T(8,128)(2,1)} async-done(((bf16[4,24,3840]{2,1,0:T(8,128)(2,1)}), bf16[4,24,3840]{2,1,0:T(8,128)(2,1)}, u32[]{:S(2)}, u32[]{:S(2)}) %all-to-all-start.2) | async-done | bytes 737312 | tf_op jit(solution)/shard_map/all_to_all | solution.py:698
  300.6 3.7 %all-to-all-start.1 = ((bf16[4,24,3648]{2,1,0:T(8,128)(2,1)}), bf16[4,24,3648]{2,1,0:T(8,128)(2,1)S(1)}, u32[]{:S(2)}, u32[]{:S(2)}) async-start(bf16[4,24,3648]{2,1,0:T(8,128)(2,1)} %pad_maximum_fusion.1), calls=%async_computation.1 | async-start | bytes 1425408 | tf_op jit(solution)/shard_map/all_to_all | solution.py:708
  304.9 6.2 %input_gradient.1 = f32[320,768]{1,0:T(8,128)} custom-call(s32[4]{0:T(128)} %pad_add_fusion.scalar_ref, bf16[320,768]{1,0:T(8,128)(2,1)} %token_ref.1, f32[320,768]{1,0:T(8,128)} %get-tuple-element.72.resid_ref, f32[1,768]{1,0:T(1,128)} %broadcast_in_dim.10.gain_ref, bf16[768,2560]{1,0:T(8,128)(2,1)} %all-gather.5.cloned.1.call-done.weight_ref, ...), custom_call_target="tpu_custom_call" | custom-call | tf_op jit(solution)/shard_map/input_gradient/pallas_call | solution.py:515
  311.1 1.3 convert_reduce_fusion
  314.3 8.0 %all-to-all-done.1 = bf16[4,24,3648]{2,1,0:T(8,128)(2,1)S(1)} async-done(((bf16[4,24,3648]{2,1,0:T(8,128)(2,1)}), bf16[4,24,3648]{2,1,0:T(8,128)(2,1)S(1)}, u32[]{:S(2)}, u32[]{:S(2)}) %all-to-all-start.1) | async-done | bytes 700448 | tf_op jit(solution)/shard_map/all_to_all | solution.py:708
  325.2 3.7 %multiply_reduce_fusion = (f32[24]{0:T(128)S(1)}, f32[24,32,4,24]{3,2,1,0:T(4,128)S(1)}) fusion(f32[24,1,32,24]{3,1,2,0:T(1,128)} %bitcast.117, f32[24,1,32,24]{3,1,2,0:T(1,128)} %bitcast.116, f32[24,1,32,24]{3,1,2,0:T(1,128)} %bitcast.115, f32[24,1,32,24]{3,1,2,0:T(1,128)S(1)} %bitcast.114, bf16[24,32,4,24]{3,2,1,0:T(4,128)(2,1)S(1)} %copy-done.7), kind=kLoop, calls=%fused_computation.16 | loop fusion | flops 442344 | bytes 737376 | tf_op jit(solution)/shard_map/reduce_sum | solution.py:738
  328.9 2.6 reshape.118
  (193 shorter events, 29.3 us)
Async XLA Ops:
  7.2 131.8 %all-gather.3.cloned.1.call-start = ((), (), s32[]{:S(2)}) async-start(), calls=%async_computation.3 | async-start | bytes 10948608 | tf_op jit(solution)/shard_map/all_gather | solution.py:630
  10.9 8.3 %copy-start.18 = (f32[24,2304]{1,0:T(8,128)S(1)}, f32[24,2304]{1,0:T(8,128)}, u32[]{:S(2)}) copy-start(f32[24,2304]{1,0:T(8,128)} %param.12) | copy-start | bytes 663556
  11.8 208.4 %all-gather.5.cloned.1.call-start = ((), (), s32[]{:S(2)}) async-start(), calls=%async_computation.4 | async-start | bytes 4055040 | tf_op jit(solution)/shard_map/all_gather | solution.py:655
  12.6 42.3 %copy-start.8 = (bf16[320,768]{1,0:T(8,128)(2,1)}, bf16[320,768]{1,0:T(8,128)(2,1)S(1)}, u32[]{:S(2)}) copy-start(bf16[320,768]{1,0:T(8,128)(2,1)S(1)} %fusion.14.refs_0_) | copy-start | bytes 1474564
  12.6 35.4 %collective-permute-start = (bf16[320,768]{1,0:T(8,128)(2,1)S(1)}, bf16[320,768]{1,0:T(8,128)(2,1)S(1)}, u32[]{:S(2)}, u32[]{:S(2)}) collective-permute-start(bf16[320,768]{1,0:T(8,128)(2,1)S(1)} %fusion.14.refs_0_), channel_id=1, source_target_pairs={{0,6},{2,0},{4,2},{6,4},{1,7},{3,1},{5,3},{7,5},{8,14},{10,8},{12,... | collective-permute-start | bytes 1474568 | tf_op jit(solution)/shard_map/ppermute | solution.py:535
  17.7 30.4 %collective-permute-start.1 = (bf16[320,768]{1,0:T(8,128)(2,1)S(1)}, bf16[320,768]{1,0:T(8,128)(2,1)S(1)}, u32[]{:S(2)}, u32[]{:S(2)}) collective-permute-start(bf16[320,768]{1,0:T(8,128)(2,1)S(1)} %fusion.14.refs_0_), channel_id=1, source_target_pairs={{0,2},{2,4},{4,6},{6,0},{1,3},{3,5},{5,7},{7,1},{8,10},{10,12},{12... | collective-permute-start | bytes 1474568 | tf_op jit(solution)/shard_map/ppermute | solution.py:535
  17.7 30.4 %collective-permute-start.2 = (bf16[320,768]{1,0:T(8,128)(2,1)S(1)}, bf16[320,768]{1,0:T(8,128)(2,1)S(1)}, u32[]{:S(2)}, u32[]{:S(2)}) collective-permute-start(bf16[320,768]{1,0:T(8,128)(2,1)S(1)} %fusion.14.refs_0_), channel_id=1, source_target_pairs={{0,1},{1,0},{2,3},{3,2},{4,5},{5,4},{6,7},{7,6},{8,9},{9,8},{10,11... | collective-permute-start | bytes 1474568 | tf_op jit(solution)/shard_map/ppermute | solution.py:535
  48.0 13.5 %copy-start.9 = (bf16[320,768]{1,0:T(8,128)(2,1)}, bf16[320,768]{1,0:T(8,128)(2,1)S(1)}, u32[]{:S(2)}) copy-start(bf16[320,768]{1,0:T(8,128)(2,1)S(1)} %collective-permute-done.refs_1_) | copy-start | bytes 1474564
  48.0 16.0 %copy-start.10 = (bf16[320,768]{1,0:T(8,128)(2,1)}, bf16[320,768]{1,0:T(8,128)(2,1)S(1)}, u32[]{:S(2)}) copy-start(bf16[320,768]{1,0:T(8,128)(2,1)S(1)} %collective-permute-done.1.refs_3_) | copy-start | bytes 1474564
  48.1 6.4 %collective-permute-start.7 = (bf16[4,24,576]{2,1,0:T(8,128)(2,1)S(1)}, bf16[4,24,576]{2,1,0:T(8,128)(2,1)S(1)}, u32[]{:S(2)}, u32[]{:S(2)}) collective-permute-start(bf16[4,24,576]{2,1,0:T(8,128)(2,1)S(1)} %all_to_all.15), channel_id=1, source_target_pairs={{0,1},{1,0},{2,3},{3,2},{4,5},{5,4},{6,7},{7,6},{8,9},{9,8},{10,11... | collective-permute-start | bytes 331784 | tf_op jit(solution)/shard_map/ppermute | solution.py:535
  54.6 5.3 %collective-permute-start.8 = (bf16[2,4,24,576]{3,2,1,0:T(8,128)(2,1)S(1)}, bf16[2,4,24,576]{3,2,1,0:T(8,128)(2,1)S(1)}, u32[]{:S(2)}, u32[]{:S(2)}) collective-permute-start(bf16[2,4,24,576]{3,2,1,0:T(8,128)(2,1)S(1)} %pad_maximum_fusion.4), channel_id=1, source_target_pairs={{0,8},{8,0},{1,9},{9,1},{2,10},{10,2},{3,11},{11,3},{4,12},{12,4},... | collective-permute-start | bytes 663560 | tf_op jit(solution)/shard_map/ppermute | solution.py:535
  55.8 22.3 %collective-permute-start.3 = (bf16[320,768]{1,0:T(8,128)(2,1)S(1)}, bf16[320,768]{1,0:T(8,128)(2,1)}, u32[]{:S(2)}, u32[]{:S(2)}) collective-permute-start(bf16[320,768]{1,0:T(8,128)(2,1)S(1)} %collective-permute-done.refs_1_), channel_id=1, source_target_pairs={{0,6},{2,0},{4,2},{6,4},{1,7},{3,1},{5,3},{7,5},{8,14},{10,8},{12,... | collective-permute-start | bytes 1474568 | tf_op jit(solution)/shard_map/ppermute | solution.py:535
  60.0 20.3 %collective-permute-start.9 = (bf16[2,2,4,24,576]{4,3,2,1,0:T(8,128)(2,1)S(1)}, bf16[2,2,4,24,576]{4,3,2,1,0:T(8,128)(2,1)S(1)}, u32[]{:S(2)}, u32[]{:S(2)}) collective-permute-start(bf16[2,2,4,24,576]{4,3,2,1,0:T(8,128)(2,1)S(1)} %pad_maximum_fusion.2), channel_id=1, source_target_pairs={{0,16},{16,0},{1,17},{17,1},{2,18},{18,2},{3,19},{19,3},{4,20},{20... | collective-permute-start | bytes 1327112 | tf_op jit(solution)/shard_map/ppermute | solution.py:535
  61.6 22.1 %collective-permute-start.4 = (bf16[320,768]{1,0:T(8,128)(2,1)S(1)}, bf16[320,768]{1,0:T(8,128)(2,1)}, u32[]{:S(2)}, u32[]{:S(2)}) collective-permute-start(bf16[320,768]{1,0:T(8,128)(2,1)S(1)} %collective-permute-done.refs_1_), channel_id=1, source_target_pairs={{0,1},{1,0},{2,3},{3,2},{4,5},{5,4},{6,7},{7,6},{8,9},{9,8},{10,11... | collective-permute-start | bytes 1474568 | tf_op jit(solution)/shard_map/ppermute | solution.py:535
  64.0 23.6 %collective-permute-start.6 = (bf16[320,768]{1,0:T(8,128)(2,1)S(1)}, bf16[320,768]{1,0:T(8,128)(2,1)}, u32[]{:S(2)}, u32[]{:S(2)}) collective-permute-start(bf16[320,768]{1,0:T(8,128)(2,1)S(1)} %collective-permute-done.1.refs_3_), channel_id=1, source_target_pairs={{0,1},{1,0},{2,3},{3,2},{4,5},{5,4},{6,7},{7,6},{8,9},{9,8},{10,11... | collective-permute-start | bytes 1474568 | tf_op jit(solution)/shard_map/ppermute | solution.py:535
  78.0 29.8 %collective-permute-start.5 = (bf16[320,768]{1,0:T(8,128)(2,1)}, bf16[320,768]{1,0:T(8,128)(2,1)}, u32[]{:S(2)}, u32[]{:S(2)}) collective-permute-start(bf16[320,768]{1,0:T(8,128)(2,1)} %collective-permute-done.3.refs_2_), channel_id=1, source_target_pairs={{0,1},{1,0},{2,3},{3,2},{4,5},{5,4},{6,7},{7,6},{8,9},{9,8},{10,11... | collective-permute-start | bytes 1474568 | tf_op jit(solution)/shard_map/ppermute | solution.py:535
  107.8 25.7 %copy-start.41 = (f32[768]{0:T(1024)S(1)}, f32[768]{0:T(1024)}, u32[]{:S(2)}) copy-start(f32[768]{0:T(1024)} %param.17) | copy-start | bytes 9220
  129.2 6.8 %collective-permute-start.10 = (bf16[3,160,128]{2,1,0:T(8,128)(2,1)S(1)}, bf16[3,160,128]{2,1,0:T(8,128)(2,1)S(1)}, u32[]{:S(2)}, u32[]{:S(2)}) collective-permute-start(bf16[3,160,128]{2,1,0:T(8,128)(2,1)S(1)} %get-tuple-element.130), channel_id=1, source_target_pairs={{0,2},{2,4},{4,6},{6,0},{1,3},{3,5},{5,7},{7,1},{8,10},{10,12},{12... | collective-permute-start | bytes 368648 | tf_op jit(solution)/shard_map/ppermute | solution.py:535
  129.2 9.7 %collective-permute-start.11 = (bf16[3,160,128]{2,1,0:T(8,128)(2,1)S(1)}, bf16[3,160,128]{2,1,0:T(8,128)(2,1)S(1)}, u32[]{:S(2)}, u32[]{:S(2)}) collective-permute-start(bf16[3,160,128]{2,1,0:T(8,128)(2,1)S(1)} %get-tuple-element.129), channel_id=1, source_target_pairs={{0,4},{2,6},{4,0},{6,2},{1,5},{3,7},{5,1},{7,3},{8,12},{10,14},{12... | collective-permute-start | bytes 368648 | tf_op jit(solution)/shard_map/ppermute | solution.py:535
  129.2 9.7 %collective-permute-start.12 = (bf16[3,160,128]{2,1,0:T(8,128)(2,1)S(1)}, bf16[3,160,128]{2,1,0:T(8,128)(2,1)S(1)}, u32[]{:S(2)}, u32[]{:S(2)}) collective-permute-start(bf16[3,160,128]{2,1,0:T(8,128)(2,1)S(1)} %get-tuple-element.128), channel_id=1, source_target_pairs={{0,6},{2,0},{4,2},{6,4},{1,7},{3,1},{5,3},{7,5},{8,14},{10,8},{12,... | collective-permute-start | bytes 368648 | tf_op jit(solution)/shard_map/ppermute | solution.py:535
  136.1 2.9 copy-start.36
  162.2 4.0 %collective-permute-start.14 = (bf16[192,3072]{1,0:T(8,128)(2,1)}, bf16[192,3072]{1,0:T(8,128)(2,1)S(1)}, u32[]{:S(2)}, u32[]{:S(2)}) collective-permute-start(bf16[192,3072]{1,0:T(8,128)(2,1)} %get-tuple-element.81), channel_id=1, source_target_pairs={{0,8},{8,0},{1,9},{9,1},{2,10},{10,2},{3,11},{11,3},{4,12},{12,4},... | collective-permute-start | bytes 3538952 | tf_op jit(solution)/shard_map/ppermute | solution.py:535
  162.3 7.5 %collective-permute-start.13 = (bf16[192,3840]{1,0:T(8,128)(2,1)}, bf16[192,3840]{1,0:T(8,128)(2,1)}, u32[]{:S(2)}, u32[]{:S(2)}) collective-permute-start(bf16[192,3840]{1,0:T(8,128)(2,1)} %get-tuple-element.79), channel_id=1, source_target_pairs={{0,8},{8,0},{1,9},{9,1},{2,10},{10,2},{3,11},{11,3},{4,12},{12,4},... | collective-permute-start | bytes 4423688 | tf_op jit(solution)/shard_map/ppermute | solution.py:535
  162.8 10.0 %collective-permute-start.15 = (bf16[192,3072]{1,0:T(8,128)(2,1)}, bf16[192,3072]{1,0:T(8,128)(2,1)S(1)}, u32[]{:S(2)}, u32[]{:S(2)}) collective-permute-start(bf16[192,3072]{1,0:T(8,128)(2,1)} %get-tuple-element.83), channel_id=1, source_target_pairs={{0,8},{8,0},{1,9},{9,1},{2,10},{10,2},{3,11},{11,3},{4,12},{12,4},... | collective-permute-start | bytes 3538952 | tf_op jit(solution)/shard_map/ppermute | solution.py:535
  162.9 11.7 %collective-permute-start.16 = (bf16[3,160,128]{2,1,0:T(8,128)(2,1)}, bf16[3,160,128]{2,1,0:T(8,128)(2,1)S(1)}, u32[]{:S(2)}, u32[]{:S(2)}) collective-permute-start(bf16[3,160,128]{2,1,0:T(8,128)(2,1)} %get-tuple-element.85), channel_id=1, source_target_pairs={{0,6},{2,0},{4,2},{6,4},{1,7},{3,1},{5,3},{7,5},{8,14},{10,8},{12,... | collective-permute-start | bytes 368648 | tf_op jit(solution)/shard_map/ppermute | solution.py:535
  165.2 13.5 %collective-permute-start.17 = (bf16[3,160,128]{2,1,0:T(8,128)(2,1)}, bf16[3,160,128]{2,1,0:T(8,128)(2,1)S(1)}, u32[]{:S(2)}, u32[]{:S(2)}) collective-permute-start(bf16[3,160,128]{2,1,0:T(8,128)(2,1)} %get-tuple-element.86), channel_id=1, source_target_pairs={{0,4},{2,6},{4,0},{6,2},{1,5},{3,7},{5,1},{7,3},{8,12},{10,14},{12... | collective-permute-start | bytes 368648 | tf_op jit(solution)/shard_map/ppermute | solution.py:535
  166.3 12.4 %collective-permute-start.18 = (bf16[3,160,128]{2,1,0:T(8,128)(2,1)}, bf16[3,160,128]{2,1,0:T(8,128)(2,1)S(1)}, u32[]{:S(2)}, u32[]{:S(2)}) collective-permute-start(bf16[3,160,128]{2,1,0:T(8,128)(2,1)} %get-tuple-element.87), channel_id=1, source_target_pairs={{0,2},{2,4},{4,6},{6,0},{1,3},{3,5},{5,7},{7,1},{8,10},{10,12},{12... | collective-permute-start | bytes 368648 | tf_op jit(solution)/shard_map/ppermute | solution.py:535
  169.8 45.1 %collective-permute-start.20 = (bf16[192,3840]{1,0:T(8,128)(2,1)}, bf16[192,3840]{1,0:T(8,128)(2,1)}, u32[]{:S(2)}, u32[]{:S(2)}) collective-permute-start(bf16[192,3840]{1,0:T(8,128)(2,1)} %get-tuple-element.99), channel_id=1, source_target_pairs={{0,8},{8,0},{1,9},{9,1},{2,10},{10,2},{3,11},{11,3},{4,12},{12,4},... | collective-permute-start | bytes 4423688 | tf_op jit(solution)/shard_map/ppermute | solution.py:535
  169.9 3.0 copy-start.12
  172.9 42.0 %collective-permute-start.21 = (bf16[192,3840]{1,0:T(8,128)(2,1)}, bf16[192,3840]{1,0:T(8,128)(2,1)}, u32[]{:S(2)}, u32[]{:S(2)}) collective-permute-start(bf16[192,3840]{1,0:T(8,128)(2,1)} %add_convert_fusion), channel_id=1, source_target_pairs={{0,16},{16,0},{1,17},{17,1},{2,18},{18,2},{3,19},{19,3},{4,20},{20... | collective-permute-start | bytes 4423688 | tf_op jit(solution)/shard_map/ppermute | solution.py:535
  174.6 4.1 %copy-start.13 = (bf16[3,160,128]{2,1,0:T(8,128)(2,1)}, bf16[3,160,128]{2,1,0:T(8,128)(2,1)S(1)}, u32[]{:S(2)}) copy-start(bf16[3,160,128]{2,1,0:T(8,128)(2,1)S(1)} %collective-permute-done.16.refs_1_) | copy-start | bytes 368644
  189.6 14.5 %collective-permute-start.19 = (bf16[4,320,128]{2,1,0:T(8,128)(2,1)}, bf16[4,320,128]{2,1,0:T(8,128)(2,1)S(1)}, u32[]{:S(2)}, u32[]{:S(2)}) collective-permute-start(bf16[4,320,128]{2,1,0:T(8,128)(2,1)} %get-tuple-element.93), channel_id=1, source_target_pairs={{0,1},{1,0},{2,3},{3,2},{4,5},{5,4},{6,7},{7,6},{8,9},{9,8},{10,11... | collective-permute-start | bytes 983048 | tf_op jit(solution)/shard_map/ppermute | solution.py:535
  191.6 68.6 %collective-permute-start.36 = (bf16[2,4,24,3072]{3,2,1,0:T(8,128)(2,1)S(1)}, bf16[2,4,24,3072]{3,2,1,0:T(8,128)(2,1)}, u32[]{:S(2)}, u32[]{:S(2)}) collective-permute-start(bf16[2,4,24,3072]{3,2,1,0:T(8,128)(2,1)S(1)} %fusion.7), channel_id=1, source_target_pairs={{0,1},{1,0},{2,3},{3,2},{4,5},{5,4},{6,7},{7,6},{8,9},{9,8},{10,11... | collective-permute-start | bytes 3538952 | tf_op jit(solution)/shard_map/ppermute | solution.py:535
  202.1 44.6 %collective-permute-start.22 = (bf16[4,320,128]{2,1,0:T(8,128)(2,1)}, bf16[4,320,128]{2,1,0:T(8,128)(2,1)}, u32[]{:S(2)}, u32[]{:S(2)}) collective-permute-start(bf16[4,320,128]{2,1,0:T(8,128)(2,1)} %get-tuple-element.105), channel_id=1, source_target_pairs={{0,1},{1,0},{2,3},{3,2},{4,5},{5,4},{6,7},{7,6},{8,9},{9,8},{10,11... | collective-permute-start | bytes 983048 | tf_op jit(solution)/shard_map/ppermute | solution.py:535
  220.2 13.2 %copy-start.32 = (bf16[480,128]{1,0:T(8,128)(2,1)S(1)}, bf16[480,128]{1,0:T(8,128)(2,1)}, u32[]{:S(2)}) copy-start(bf16[480,128]{1,0:T(8,128)(2,1)} %get-tuple-element.95.refs_7_) | copy-start | bytes 368644
  230.8 20.3 %collective-permute-start.26 = (bf16[4,320,128]{2,1,0:T(8,128)(2,1)}, bf16[4,320,128]{2,1,0:T(8,128)(2,1)}, u32[]{:S(2)}, u32[]{:S(2)}) collective-permute-start(bf16[4,320,128]{2,1,0:T(8,128)(2,1)} %get-tuple-element.110), channel_id=1, source_target_pairs={{0,1},{1,0},{2,3},{3,2},{4,5},{5,4},{6,7},{7,6},{8,9},{9,8},{10,11... | collective-permute-start | bytes 983048 | tf_op jit(solution)/shard_map/ppermute | solution.py:535
  233.3 8.2 %collective-permute-start.23 = (bf16[480,128]{1,0:T(8,128)(2,1)S(1)}, bf16[480,128]{1,0:T(8,128)(2,1)}, u32[]{:S(2)}, u32[]{:S(2)}) collective-permute-start(bf16[480,128]{1,0:T(8,128)(2,1)S(1)} %copy-done.32), channel_id=1, source_target_pairs={{0,2},{2,4},{4,6},{6,0},{1,3},{3,5},{5,7},{7,1},{8,10},{10,12},{12... | collective-permute-start | bytes 368648 | tf_op jit(solution)/shard_map/ppermute | solution.py:535
  234.2 11.1 %collective-permute-start.24 = (bf16[480,128]{1,0:T(8,128)(2,1)}, bf16[480,128]{1,0:T(8,128)(2,1)}, u32[]{:S(2)}, u32[]{:S(2)}) collective-permute-start(bf16[480,128]{1,0:T(8,128)(2,1)} %get-tuple-element.96.refs_10_), channel_id=1, source_target_pairs={{0,4},{2,6},{4,0},{6,2},{1,5},{3,7},{5,1},{7,3},{8,12},{10,14},{12... | collective-permute-start | bytes 368648 | tf_op jit(solution)/shard_map/ppermute | solution.py:535
  241.5 5.2 %collective-permute-start.25 = (bf16[480,128]{1,0:T(8,128)(2,1)}, bf16[480,128]{1,0:T(8,128)(2,1)}, u32[]{:S(2)}, u32[]{:S(2)}) collective-permute-start(bf16[480,128]{1,0:T(8,128)(2,1)} %get-tuple-element.97.refs_13_), channel_id=1, source_target_pairs={{0,6},{2,0},{4,2},{6,4},{1,7},{3,1},{5,3},{7,5},{8,14},{10,8},{12,... | collective-permute-start | bytes 368648 | tf_op jit(solution)/shard_map/ppermute | solution.py:535
  245.3 17.9 %collective-permute-start.38 = (bf16[4,24,3840]{2,1,0:T(8,128)(2,1)}, bf16[4,24,3840]{2,1,0:T(8,128)(2,1)}, u32[]{:S(2)}, u32[]{:S(2)}) collective-permute-start(bf16[4,24,3840]{2,1,0:T(8,128)(2,1)} %fusion.15), channel_id=1, source_target_pairs={{0,1},{1,0},{2,3},{3,2},{4,5},{5,4},{6,7},{7,6},{8,9},{9,8},{10,11... | collective-permute-start | bytes 2211848 | tf_op jit(solution)/shard_map/ppermute | solution.py:535
  248.7 17.6 %collective-permute-start.27 = (bf16[480,128]{1,0:T(8,128)(2,1)}, bf16[480,128]{1,0:T(8,128)(2,1)S(1)}, u32[]{:S(2)}, u32[]{:S(2)}) collective-permute-start(bf16[480,128]{1,0:T(8,128)(2,1)} %get-tuple-element.112.refs_8_), channel_id=1, source_target_pairs={{0,2},{2,4},{4,6},{6,0},{1,3},{3,5},{5,7},{7,1},{8,10},{10,12},{12... | collective-permute-start | bytes 368648 | tf_op jit(solution)/shard_map/ppermute | solution.py:535
  249.9 19.2 %collective-permute-start.29 = (bf16[480,128]{1,0:T(8,128)(2,1)}, bf16[480,128]{1,0:T(8,128)(2,1)S(1)}, u32[]{:S(2)}, u32[]{:S(2)}) collective-permute-start(bf16[480,128]{1,0:T(8,128)(2,1)} %get-tuple-element.114.refs_11_), channel_id=1, source_target_pairs={{0,4},{2,6},{4,0},{6,2},{1,5},{3,7},{5,1},{7,3},{8,12},{10,14},{12... | collective-permute-start | bytes 368648 | tf_op jit(solution)/shard_map/ppermute | solution.py:535
  251.1 18.3 %collective-permute-start.31 = (bf16[480,128]{1,0:T(8,128)(2,1)}, bf16[480,128]{1,0:T(8,128)(2,1)S(1)}, u32[]{:S(2)}, u32[]{:S(2)}) collective-permute-start(bf16[480,128]{1,0:T(8,128)(2,1)} %get-tuple-element.116.refs_14_), channel_id=1, source_target_pairs={{0,6},{2,0},{4,2},{6,4},{1,7},{3,1},{5,3},{7,5},{8,14},{10,8},{12,... | collective-permute-start | bytes 368648 | tf_op jit(solution)/shard_map/ppermute | solution.py:535
  260.2 3.0 copy-start.35
  260.2 3.6 %copy-start.34 = (bf16[480,128]{1,0:T(8,128)(2,1)S(1)}, bf16[480,128]{1,0:T(8,128)(2,1)}, u32[]{:S(2)}) copy-start(bf16[480,128]{1,0:T(8,128)(2,1)} %get-tuple-element.115.refs_12_) | copy-start | bytes 368644
  260.2 3.6 %collective-permute-start.33 = (bf16[2,192,576]{2,1,0:T(8,128)(2,1)}, bf16[2,192,576]{2,1,0:T(8,128)(2,1)S(1)}, u32[]{:S(2)}, u32[]{:S(2)}) collective-permute-start(bf16[2,192,576]{2,1,0:T(8,128)(2,1)} %get-tuple-element.119), channel_id=1, source_target_pairs={{0,8},{8,0},{1,9},{9,1},{2,10},{10,2},{3,11},{11,3},{4,12},{12,4},... | collective-permute-start | bytes 1327112 | tf_op jit(solution)/shard_map/ppermute | solution.py:535
  262.2 3.5 %copy-start.4 = (f32[2,4,24,3072]{3,2,1,0:T(8,128)}, f32[2,4,24,3072]{3,2,1,0:T(8,128)S(1)}, u32[]{:S(2)}) copy-start(f32[2,4,24,3072]{3,2,1,0:T(8,128)S(1)} %fusion.2) | copy-start | bytes 7077892
  262.2 3.3 copy-start.16
  262.2 4.2 %copy-start.33 = (bf16[480,128]{1,0:T(8,128)(2,1)S(1)}, bf16[480,128]{1,0:T(8,128)(2,1)}, u32[]{:S(2)}) copy-start(bf16[480,128]{1,0:T(8,128)(2,1)} %get-tuple-element.117.refs_15_) | copy-start | bytes 368644
  263.2 8.0 %copy-start.3 = (f32[192,3840]{1,0:T(8,128)S(1)}, f32[192,3840]{1,0:T(8,128)}, u32[]{:S(2)}) copy-start(f32[192,3840]{1,0:T(8,128)} %copy-done.2) | copy-start | bytes 8847364
  263.2 10.1 %collective-permute-start.28 = (bf16[480,128]{1,0:T(8,128)(2,1)S(1)}, bf16[480,128]{1,0:T(8,128)(2,1)S(1)}, u32[]{:S(2)}, u32[]{:S(2)}) collective-permute-start(bf16[480,128]{1,0:T(8,128)(2,1)S(1)} %copy-done.35), channel_id=1, source_target_pairs={{0,2},{2,4},{4,6},{6,0},{1,3},{3,5},{5,7},{7,1},{8,10},{10,12},{12... | collective-permute-start | bytes 368648 | tf_op jit(solution)/shard_map/ppermute | solution.py:535
  263.8 12.2 %collective-permute-start.30 = (bf16[480,128]{1,0:T(8,128)(2,1)S(1)}, bf16[480,128]{1,0:T(8,128)(2,1)S(1)}, u32[]{:S(2)}, u32[]{:S(2)}) collective-permute-start(bf16[480,128]{1,0:T(8,128)(2,1)S(1)} %copy-done.34), channel_id=1, source_target_pairs={{0,4},{2,6},{4,0},{6,2},{1,5},{3,7},{5,1},{7,3},{8,12},{10,14},{12... | collective-permute-start | bytes 368648 | tf_op jit(solution)/shard_map/ppermute | solution.py:535
  266.4 6.9 %copy-start.27 = (bf16[480,128]{1,0:T(8,128)(2,1)}, bf16[480,128]{1,0:T(8,128)(2,1)S(1)}, u32[]{:S(2)}) copy-start(bf16[480,128]{1,0:T(8,128)(2,1)S(1)} %collective-permute-done.27.refs_4_) | copy-start | bytes 368644
  266.4 10.3 %collective-permute-start.32 = (bf16[480,128]{1,0:T(8,128)(2,1)S(1)}, bf16[480,128]{1,0:T(8,128)(2,1)}, u32[]{:S(2)}, u32[]{:S(2)}) collective-permute-start(bf16[480,128]{1,0:T(8,128)(2,1)S(1)} %copy-done.33), channel_id=1, source_target_pairs={{0,6},{2,0},{4,2},{6,4},{1,7},{3,1},{5,3},{7,5},{8,14},{10,8},{12,... | collective-permute-start | bytes 368648 | tf_op jit(solution)/shard_map/ppermute | solution.py:535
  269.1 4.2 %copy-start.28 = (bf16[480,128]{1,0:T(8,128)(2,1)}, bf16[480,128]{1,0:T(8,128)(2,1)S(1)}, u32[]{:S(2)}) copy-start(bf16[480,128]{1,0:T(8,128)(2,1)S(1)} %collective-permute-done.29.refs_7_) | copy-start | bytes 368644
  269.1 22.2 %collective-permute-start.37 = (bf16[4,24,3072]{2,1,0:T(8,128)(2,1)}, bf16[4,24,3072]{2,1,0:T(8,128)(2,1)}, u32[]{:S(2)}, u32[]{:S(2)}) collective-permute-start(bf16[4,24,3072]{2,1,0:T(8,128)(2,1)} %fusion.16), channel_id=1, source_target_pairs={{0,16},{16,0},{1,17},{17,1},{2,18},{18,2},{3,19},{19,3},{4,20},{20... | collective-permute-start | bytes 1769480 | tf_op jit(solution)/shard_map/ppermute | solution.py:535
  269.4 6.6 %copy-start.29 = (bf16[480,128]{1,0:T(8,128)(2,1)}, bf16[480,128]{1,0:T(8,128)(2,1)S(1)}, u32[]{:S(2)}) copy-start(bf16[480,128]{1,0:T(8,128)(2,1)S(1)} %collective-permute-done.31.refs_10_) | copy-start | bytes 368644
  269.4 20.1 %collective-permute-start.34 = (bf16[4,2,24,576]{3,2,0,1:T(8,128)(2,1)}, bf16[4,2,24,576]{3,2,0,1:T(8,128)(2,1)}, u32[]{:S(2)}, u32[]{:S(2)}) collective-permute-start(bf16[4,2,24,576]{3,2,0,1:T(8,128)(2,1)} %fusion.18), channel_id=1, source_target_pairs={{0,16},{16,0},{1,17},{17,1},{2,18},{18,2},{3,19},{19,3},{4,20},{20... | collective-permute-start | bytes 663560 | tf_op jit(solution)/shard_map/ppermute | solution.py:535
  273.2 18.0 %copy-start.5 = (f32[2,4,24,3072]{3,2,1,0:T(8,128)S(1)}, f32[2,4,24,3072]{3,2,1,0:T(8,128)}, u32[]{:S(2)}) copy-start(f32[2,4,24,3072]{3,2,1,0:T(8,128)} %copy-done.4) | copy-start | bytes 7077892
  273.3 19.2 %copy-start.30 = (bf16[480,128]{1,0:T(8,128)(2,1)}, bf16[480,128]{1,0:T(8,128)(2,1)S(1)}, u32[]{:S(2)}) copy-start(bf16[480,128]{1,0:T(8,128)(2,1)S(1)} %collective-permute-done.28.refs_5_) | copy-start | bytes 368644
  276.7 24.0 %all-to-all-start.2 = ((bf16[4,24,3840]{2,1,0:T(8,128)(2,1)}), bf16[4,24,3840]{2,1,0:T(8,128)(2,1)}, u32[]{:S(2)}, u32[]{:S(2)}) async-start(bf16[4,24,3840]{2,1,0:T(8,128)(2,1)} %fusion.6), calls=%async_computation.2 | async-start | bytes 1474560 | tf_op jit(solution)/shard_map/all_to_all | solution.py:698
  290.5 4.9 %collective-permute-start.35 = (bf16[4,24,576]{2,1,0:T(8,128)(2,1)S(1)}, bf16[4,24,576]{2,1,0:T(8,128)(2,1)S(1)}, u32[]{:S(2)}, u32[]{:S(2)}) collective-permute-start(bf16[4,24,576]{2,1,0:T(8,128)(2,1)S(1)} %fusion.20), channel_id=1, source_target_pairs={{0,1},{1,0},{2,3},{3,2},{4,5},{5,4},{6,7},{7,6},{8,9},{9,8},{10,11... | collective-permute-start | bytes 331784 | tf_op jit(solution)/shard_map/ppermute | solution.py:535
  300.6 21.6 %all-to-all-start.1 = ((bf16[4,24,3648]{2,1,0:T(8,128)(2,1)}), bf16[4,24,3648]{2,1,0:T(8,128)(2,1)S(1)}, u32[]{:S(2)}, u32[]{:S(2)}) async-start(bf16[4,24,3648]{2,1,0:T(8,128)(2,1)} %pad_maximum_fusion.1), calls=%async_computation.1 | async-start | bytes 1425408 | tf_op jit(solution)/shard_map/all_to_all | solution.py:708
  313.1 12.1 %copy-start.7 = (bf16[24,32,4,24]{3,2,1,0:T(4,128)(2,1)S(1)}, bf16[24,32,4,24]{3,2,1,0:T(4,128)(2,1)}, u32[]{:S(2)}) copy-start(bf16[24,32,4,24]{3,2,1,0:T(4,128)(2,1)} %copy-done.6) | copy-start | bytes 442372
  (21 other events, 32.7 us)
Sparse Core Ops, SparseCore 0:
  11.9 115.9 all-gather.2
  130.8 72.7 all-gather.4
where the time goes:
time: 346 us; the launch traced here: 341 us
  waiting for transfers between devices  95.5 us (28%)
  Pallas kernels  91.5 us (26%)
  starting transfers between devices  58 us (17%)
  blocking collectives  28.2 us (8%)
  other arithmetic  26.5 us (8%)
  local copies, waits for them, and re-layouts  26.1 us (8%)
  between operations  15.6 us (5%)
    ppermute x39, waiting for transfers between devices, shift(): return lax.ppermute(value, axis, [(i, (i + step) % n) for i in range(n)])  83.5 us
    ppermute x39, starting transfers between devices, shift(): return lax.ppermute(value, axis, [(i, (i + step) % n) for i in range(n)])  49.3 us
    pallas_call x3, Pallas kernels, attention_backward(): pl.pallas_call(functools.partial(attention_backward_kernel, rows, n_own),...  31.3 us
    all_to_all x1, blocking collectives, on_device(): parts = lax.all_to_all(parts, 'g', 0, 0)  28.2 us
    pallas_call x1, Pallas kernels, middle(): pl.pallas_call(functools.partial(middle_kernel, (n_g, wide, width, rows,...  22.6 us
    pallas_call x1, Pallas kernels, attention_forward(): pl.pallas_call(functools.partial(attention_forward_kernel, n_own), grid=(...  19.6 us
    all_to_all x1, waiting for transfers between devices, on_device(): second = lax.all_to_all(after(second, *last), 'g', 0, 0)  7.96 us
    add x6, other arithmetic, add_high(): total = total + term.astype(F32)  7.75 us
  transfers between devices with their start and end apart: 43, of which 17 were waited for; matrix products, arithmetic and copies ran while one was open for 9% of the time, Pallas kernels for 27%

commit v1 on v0

--- a/solution.py
+++ b/solution.py
@@ -302,7 +302,7 @@
             copy.wait()
 
     count = 1 + 2 * wide
-    for index in range(count):
+    for index in [0] + [at + q for q in range(wide) for at in (1, 1 + wide)]:
         start(fetch(index))
 
     def places(k):
@@ -330,7 +330,7 @@
     added = None
     grad_normed = None
     for q in range(wide):
-        up_at, down_at = 1 + 2 * q, 2 + 2 * q
+        up_at, down_at = 1 + q, 1 + wide + q
         wait(fetch(up_at))
         upper = nn(normed, weight_scr[up_at])
         wait(fetch(down_at))
@@ -619,15 +619,15 @@
     pieces = own_pieces + [others[at] for at in sorted(others)]
 
     n_all = n_a * n_c * n_g * n_r
-    up_low = up_master.astype(BF16)
     up_turned = (
-        up_low.reshape(share, n_all, wide, share).transpose(0, 2, 1, 3).reshape(share, wide, width)
+        up_master.astype(BF16)
+        .reshape(share, n_all, wide, share)
+        .transpose(0, 2, 1, 3)
+        .reshape(share, hidden)
     )
     down_turned = down_master.astype(BF16).reshape(wide, share, width)
-    blocks = [out_master.astype(BF16)]
-    for q in range(wide):
-        blocks += [up_turned[:, q], down_turned[q]]
-    weights = lax.all_gather(jnp.concatenate(blocks, axis=1), ALL, axis=0, tiled=True)
+    packed = jnp.concatenate([out_master.astype(BF16), up_turned, *down_turned], axis=1)
+    weights = lax.all_gather(packed, ALL, axis=0, tiled=True)
 
     parts = gather(gather(gather(after(parts, *ready), "r"), "c"), "a")
     parts = parts.reshape(n_a, n_c, n_r, n_g, share, heads, 3 * HEAD)
@@ -642,23 +642,17 @@
     mixed, grad_resid, sends = made[0], made[1], made[2 : 2 + n_g]
     grad_blocks = [made[2 + n_g : 2 + n_g + n_a * n_c], made[2 + n_g + n_a * n_c :]]
 
-    terms = [[(block, shift(there, "c", 1)) for block, there in zip(some[:n_a], some[n_a:])] for some in grad_blocks]
-    far = [add_low(*pair) for pair in terms[0][1:]]
-    near = jnp.stack([add_high(*pair).reshape(n_g, n_r, share, -1) for pair in terms[1]])
-    mine, other = halves(near, "r", 2)
+    come = [[shift(block, "c", 1) for block in some[n_a:]] for some in grad_blocks]
 
     columns = heads * 3 * HEAD
     padded = -(-columns // LANES) * LANES
     turned = qkv_low.reshape(share, 3, n_g, heads, HEAD).transpose(0, 2, 3, 1, 4)
-    turned = jnp.pad(turned.reshape(share, n_g, columns), ((0, 0), (0, 0), (0, padded - columns)))
-    turned = after(turned.reshape(share, n_g * padded), *ready)
-    qkv_weight = lax.all_gather(turned, ALL, axis=0, tiled=True)
+    turned = turned.reshape(share, n_g, columns)
+    qkv_weight = jnp.pad(turned, ((0, 0), (0, 0), (0, padded - columns)))
+    qkv_weight = after(qkv_weight.reshape(share, n_g * padded), *ready)
+    qkv_weight = lax.all_gather(qkv_weight, ALL, axis=0, tiled=True)
 
     grads = [sends[0]] + [shift(sends[k], "g", -k) for k in range(1, n_g)]
-    gate = [*far, *other]
-    far = [shift(block, "a", k) for k, block in enumerate(far, 1)]
-    other = [shift(block, "r", j) for j, block in enumerate(other, 1)]
-
     made = []
     grad_pieces = []
     whole = []
@@ -673,69 +667,75 @@
         whole.append([done[0]] + [shift(done[k], "g", k) for k in range(1, n_g)])
 
     for head in range(heads):
-        if head == 1:
-            gate = [made[0][0]]
+        gate = [made[-1][0]] if head == 1 else []
+        if head == 0:
+            come = [[after(block, *grads) for block in some] for some in come]
+            far = [
+                [add_low(*pair) for pair in zip(some[1:n_a], there[1:])]
+                for some, there in zip(grad_blocks, come)
+            ]
+            gate = far[0] + far[1]
+            far[0] = [shift(block, "a", k) for k, block in enumerate(far[0], 1)]
         if head >= 2:
             finish(head - 2)
             gate = [*grad_pieces[head - 2], qkv_weight]
-        if head == 2:
-            first = add_high(*terms[0][0], *(after(block, made[1][0], *made[0][1]) for block in far))
-            first, send = halves(first.reshape(n_g, n_r, share, -1), "r", 1)
-            gate += send
-            send = [shift(block, "r", j) for j, block in enumerate(send, 1)]
-        gated = [after(grads[0], *gate)] + grads[1:]
+        gated = ([after(grads[0], *gate)] if gate else grads[:1]) + grads[1:]
         own, across, grad_query = attention_backward(out, query, key, value, gated, head)
         across = [
             shift(across[(j - 1) * n_g : j * n_g] if n_r > 2 else across, "r", j)
             for j in range(1, n_r)
         ]
         made.append((own, across, grad_query))
+    made[-2] = (after(made[-2][0], *whole[-1]),) + made[-2][1:]
     finish(heads - 2)
-    first = add_high(first, *(after(block, *made[-1][1]) for block in send)).astype(BF16)
-    near = add_high(mine, *(after(block, *made[-1][1]) for block in other))
-    second = add_low(near[0], *(shift(near[k].astype(BF16), "a", k) for k in range(1, n_a)))
+    far[0] = [after(block, *grad_pieces[-1]) for block in far[0]]
+    first = add_high(grad_blocks[0][0], come[0][0], *far[0])
+    first, send = halves(first.reshape(n_g, n_r, share, -1), "r", 1)
+    far[1] = [after(block, *far[0]) for block in far[1]]
+    made[-1] = (after(made[-1][0], *send),) + made[-1][1:]
     finish(heads - 1)
-    first = lax.all_to_all(after(first, *whole[-2], *whole[-1]), "g", 0, 0)
+    send = [shift(after(block, *made[-1][1]), "r", j) for j, block in enumerate(send, 1)]
+    far[1] = [shift(block, "a", k) for k, block in enumerate(far[1], 1)]
+    second = add_high(grad_blocks[1][0], come[1][0], *far[1]).reshape(n_g, n_r, share, -1)
+    second = scatter_sum(second, "r", 1).astype(BF16)
     grad_pieces = [[some[k] for some in grad_pieces] for k in range(n_g)]
     whole = [[some[k] for some in whole] for k in range(n_g)]
 
+    grad_pieces[0][0] = after(grad_pieces[0][0], *(some[-2] for some in whole))
     mine, theirs = group_grad(scalars, own_pieces, grad_pieces, n_a, n_c)
+    theirs = after(theirs, *(some[-1] for some in whole), *send)
+    first = lax.all_to_all(add_low(first, *send), "g", 0, 0)
     qkv_grad = add_high(mine, shift(theirs, "c", 1))
     qkv_grad = qkv_grad.reshape(n_a, n_g, n_r, share, columns)
-    qkv_grad = scatter_sum(scatter_sum(qkv_grad, "a", 0), "r", 1)
-    last = [some[-1] for some in whole[1:]]
+    qkv_grad = scatter_sum(after(scatter_sum(qkv_grad, "a", 0), first), "r", 1)
     second = jnp.concatenate([qkv_grad.astype(BF16), second], axis=2)
-    second = lax.all_to_all(after(second, *last), "g", 0, 0)
-
+    second = lax.all_to_all(after(second, first), "g", 0, 0)
     input_grad = input_gradient(scalars, tokens, grad_resid, gain_one[None], qkv_weight, whole)
 
+    first = jnp.sum(first.astype(F32), axis=0)
+    out_share = first[:, :width]
+    up_share = first[:, width:]
+    second_share = jnp.sum(up_turned.astype(F32) * up_share, axis=1)
+    up_share = (
+        up_share.reshape(share, wide, n_all, share).transpose(0, 2, 1, 3).reshape(share, hidden)
+    )
+    qkv_share = second[:, :, :columns].astype(F32)
+    first_share = jnp.sum(turned.swapaxes(0, 1).astype(F32) * qkv_share, axis=(0, 2))
     qkv_share = (
-        second[:, :, :columns]
-        .astype(F32)
-        .reshape(n_g, share, heads, 3, HEAD)
+        qkv_share.reshape(n_g, share, heads, 3, HEAD)
         .transpose(1, 3, 0, 2, 4)
         .reshape(share, 3 * width)
     )
-    shares = []
-    for total in (first, second[:, :, columns:]):
-        total = jnp.sum(total.astype(F32), axis=0)
-        shares += [
-            total[:, at * width : (at + 1) * width] for at in range(total.shape[1] // width)
-        ]
-    out_share = shares[0]
-    up_turned_share = jnp.stack(shares[1::2], axis=1)
-    up_share = (
-        up_turned_share.reshape(share, wide, n_all, share)
-        .transpose(0, 2, 1, 3)
-        .reshape(share, hidden)
+    down_share = jnp.sum(second[:, :, columns:].astype(F32), axis=0)
+    down_share = (
+        down_share.reshape(share, wide, width).transpose(1, 0, 2).reshape(wide * share, width)
     )
-    down_share = jnp.concatenate(shares[2::2], axis=0)
 
     place = lax.axis_index(ALL) * share
     own_gain_one = lax.dynamic_slice_in_dim(gain_one, place, share)
     own_gain_two = lax.dynamic_slice_in_dim(gain_two, place, share)
-    first_share = jnp.sum(qkv_low.astype(F32) * qkv_share, axis=1) / own_gain_one
-    second_share = jnp.sum(up_turned.astype(F32) * up_turned_share, axis=(1, 2)) / own_gain_two
+    first_share = first_share / own_gain_one
+    second_share = second_share / own_gain_two
     return (
         mixed,
         input_grad,

time: 346 us -> 332 us (0.960)
  blocking collectives: 28.2 us -> 0 us
  waiting for transfers between devices: 95.5 us -> 106 us
  starting transfers between devices: 58 us -> 62.3 us
    all_to_all x1 -> x0, blocking collectives: 28.2 us -> none  [on_device(): parts = lax.all_to_all(parts, 'g', 0, 0)]
    all_to_all x2 -> x3, waiting for transfers between devices: 12 us -> 27.1 us  [the longest x1 21.3 us: on_device(): parts = lax.all_to_all(parts, 'g', 0, 0)]
    all_to_all x2 -> x3, starting transfers between devices: 8.63 us -> 13.8 us  [the longest x1 5.09 us: on_device(): parts = lax.all_to_all(parts, 'g', 0, 0)]
    ppermute x39, waiting for transfers between devices: 83.5 us -> 78.8 us  [shift(): return lax.ppermute(value, axis, [(i, (i + step) % n) for i in range(n)])]
    unnamed x94 -> x70, local copies, waits for them, and re-layouts: 7.51 us -> 5.31 us
    reshape x6 -> x8, local copies, waits for them, and re-layouts: 5.79 us -> 7.84 us  [the longest x2 3.68 us: on_device(): up_share.reshape(share, wide, n_all, share).transpose(0, 2, 1, 3)]
    add x6 -> x4, other arithmetic: 7.75 us -> 6.78 us  [add_high(): total = total + term.astype(F32)]
  transfers between devices with their start and end apart: 43 -> 44, of which waited for: 17 -> 16; matrix products, arithmetic and copies ran while one was open for 9% -> 11% of each run, Pallas kernels for 27% -> 28%
where the time goes in v1:
time: 332 us; the launch traced here: 327 us
  waiting for transfers between devices  106 us (32%)
  Pallas kernels  91.5 us (28%)
  starting transfers between devices  62.3 us (19%)
  local copies, waits for them, and re-layouts  25.8 us (8%)
  other arithmetic  25.6 us (8%)
  between operations  15.6 us (5%)
    ppermute x39, waiting for transfers between devices, shift(): return lax.ppermute(value, axis, [(i, (i + step) % n) for i in range(n)])  78.8 us
    ppermute x39, starting transfers between devices, shift(): return lax.ppermute(value, axis, [(i, (i + step) % n) for i in range(n)])  48.5 us
    pallas_call x3, Pallas kernels, attention_backward(): pl.pallas_call(functools.partial(attention_backward_kernel, rows, n_own),...  31 us
    pallas_call x1, Pallas kernels, middle(): pl.pallas_call(functools.partial(middle_kernel, (n_g, wide, width, rows,...  22.7 us
    all_to_all x1, waiting for transfers between devices, on_device(): parts = lax.all_to_all(parts, 'g', 0, 0)  21.3 us
    pallas_call x1, Pallas kernels, attention_forward(): pl.pallas_call(functools.partial(attention_forward_kernel, n_own), grid=(...  19.6 us
    add x4, other arithmetic, add_high(): total = total + term.astype(F32)  6.78 us
  transfers between devices with their start and end apart: 44, of which 16 were waited for; matrix products, arithmetic and copies ran while one was open for 11% of the time, Pallas kernels for 28%

profile of v1, /device:TPU:0, one launch (start us, length us, event | category | flops | bytes accessed | tf_op | source)
XLA Modules:
  0.0 326.8 jit_solution(671917427605722456)
XLA Ops:
  9.2 1.2 reshape.99
  10.6 1.3 reshape.100
  13.5 5.1 %collective-permute-start = (bf16[320,768]{1,0:T(8,128)(2,1)S(1)}, bf16[320,768]{1,0:T(8,128)(2,1)S(1)}, u32[]{:S(2)}, u32[]{:S(2)}) collective-permute-start(bf16[320,768]{1,0:T(8,128)(2,1)S(1)} %fusion.6.refs_0_), channel_id=1, source_target_pairs={{0,6},{2,0},{4,2},{6,4},{1,7},{3,1},{5,3},{7,5},{8,14},{10,8},{12,... | collective-permute-start | bytes 1474568 | tf_op jit(solution)/shard_map/ppermute | solution.py:535
  18.6 1.5 collective-permute-start.2
  21.3 5.1 %all-to-all-start = ((bf16[4,24,576]{2,1,0:T(8,128)(2,1)}), bf16[4,24,576]{2,1,0:T(8,128)(2,1)S(1)}, u32[]{:S(2)}, u32[]{:S(2)}) async-start(bf16[4,24,576]{2,1,0:T(8,128)(2,1)} %reshape.97), calls=%async_computation | async-start | bytes 245760 | tf_op jit(solution)/shard_map/all_to_all | solution.py:612
  27.6 21.3 %all-to-all-done = bf16[4,24,576]{2,1,0:T(8,128)(2,1)S(1)} async-done(((bf16[4,24,576]{2,1,0:T(8,128)(2,1)}), bf16[4,24,576]{2,1,0:T(8,128)(2,1)S(1)}, u32[]{:S(2)}, u32[]{:S(2)}) %all-to-all-start) | async-done | bytes 110624 | tf_op jit(solution)/shard_map/all_to_all | solution.py:612
  49.0 1.6 collective-permute-start.7
  50.6 4.9 %collective-permute-done.7 = bf16[4,24,576]{2,1,0:T(8,128)(2,1)S(1)} collective-permute-done((bf16[4,24,576]{2,1,0:T(8,128)(2,1)S(1)}, bf16[4,24,576]{2,1,0:T(8,128)(2,1)S(1)}, u32[]{:S(2)}, u32[]{:S(2)}) %collective-permute-start.7) | collective-permute-done | bytes 110624 | tf_op jit(solution)/shard_map/ppermute | solution.py:535
  55.7 4.1 %collective-permute-start.3 = (bf16[320,768]{1,0:T(8,128)(2,1)S(1)}, bf16[320,768]{1,0:T(8,128)(2,1)}, u32[]{:S(2)}, u32[]{:S(2)}) collective-permute-start(bf16[320,768]{1,0:T(8,128)(2,1)S(1)} %collective-permute-done.refs_1_), channel_id=1, source_target_pairs={{0,6},{2,0},{4,2},{6,4},{1,7},{3,1},{5,3},{7,5},{8,14},{10,8},{12,... | collective-permute-start | bytes 1474568 | tf_op jit(solution)/shard_map/ppermute | solution.py:535
  59.9 1.5 collective-permute-start.9
  61.4 2.5 collective-permute-start.4
  64.0 14.8 %collective-permute-done.3.refs_2_ = bf16[320,768]{1,0:T(8,128)(2,1)} collective-permute-done((bf16[320,768]{1,0:T(8,128)(2,1)S(1)}, bf16[320,768]{1,0:T(8,128)(2,1)}, u32[]{:S(2)}, u32[]{:S(2)}) %collective-permute-start.3) | collective-permute-done | bytes 491552 | tf_op jit(solution)/shard_map/ppermute | solution.py:535
  78.8 1.5 collective-permute-start.5
  81.8 1.2 maximum_bitcast_fusion
  83.0 1.2 copy.35
  84.3 2.6 collective-permute-done.6.refs_7_
  86.9 20.1 %collective-permute-done.5.refs_6_ = bf16[320,768]{1,0:T(8,128)(2,1)} collective-permute-done((bf16[320,768]{1,0:T(8,128)(2,1)}, bf16[320,768]{1,0:T(8,128)(2,1)}, u32[]{:S(2)}, u32[]{:S(2)}) %collective-permute-start.5) | collective-permute-done | bytes 491552 | tf_op jit(solution)/shard_map/ppermute | solution.py:535
  107.0 19.6 %attention_forward.1 = (bf16[4,3,160,128]{3,2,1,0:T(8,128)(2,1)}, bf16[3,1280,128]{2,1,0:T(8,128)(2,1)}, bf16[3,2560,128]{2,1,0:T(8,128)(2,1)}, bf16[3,2560,128]{2,1,0:T(8,128)(2,1)}) custom-call(s32[1]{0:T(128)S(6)} %copy.58.live_ref, bf16[320,768]{1,0:T(8,128)(2,1)} %copy-done.1, bf16[320,768]{1,0:T(8,128)(2,1)} %copy-done.2, ...), custom_call_target="tpu_custom_call" | custom-call | tf_op jit(solution)/shard_map/attention_forward/pallas_call | solution.py:110
  126.6 1.8 slice_bitcast_fusion
  128.4 4.3 %collective-permute-start.12 = (bf16[3,160,128]{2,1,0:T(8,128)(2,1)S(1)}, bf16[3,160,128]{2,1,0:T(8,128)(2,1)S(1)}, u32[]{:S(2)}, u32[]{:S(2)}) collective-permute-start(bf16[3,160,128]{2,1,0:T(8,128)(2,1)S(1)} %get-tuple-element.140), channel_id=1, source_target_pairs={{0,6},{2,0},{4,2},{6,4},{1,7},{3,1},{5,3},{7,5},{8,14},{10,8},{12,... | collective-permute-start | bytes 368648 | tf_op jit(solution)/shard_map/ppermute | solution.py:535
  133.9 1.2 collective-permute-done.10.refs_4_
  135.2 2.7 collective-permute-done.11.refs_5_
  138.5 22.7 %middle.1 = (bf16[320,768]{1,0:T(8,128)(2,1)}, f32[320,768]{1,0:T(8,128)}, bf16[3,160,128]{2,1,0:T(8,128)(2,1)}, bf16[3,160,128]{2,1,0:T(8,128)(2,1)}, bf16[3,16...) custom-call(s32[4]{0:T(128)} %pad_add_fusion.scalar_ref, ...), custom_call_target="tpu_custom_call" | custom-call | tf_op jit(solution)/shard_map/middle/pallas_call | solution.py:388
  161.3 2.5 collective-permute-start.14
  164.6 4.4 %collective-permute-done.14.refs_1_ = bf16[3,160,128]{2,1,0:T(8,128)(2,1)S(1)} collective-permute-done((bf16[3,160,128]{2,1,0:T(8,128)(2,1)}, bf16[3,160,128]{2,1,0:T(8,128)(2,1)S(1)}, u32[]{:S(2)}, u32[]{:S(2)}) %collective-permute-start.14) | collective-permute-done | bytes 122912 | tf_op jit(solution)/shard_map/ppermute | solution.py:535
  169.0 9.0 %collective-permute-done.15.refs_2_ = bf16[3,160,128]{2,1,0:T(8,128)(2,1)S(1)} collective-permute-done((bf16[3,160,128]{2,1,0:T(8,128)(2,1)}, bf16[3,160,128]{2,1,0:T(8,128)(2,1)S(1)}, u32[]{:S(2)}, u32[]{:S(2)}) %collective-permute-start.15) | collective-permute-done | bytes 122912 | tf_op jit(solution)/shard_map/ppermute | solution.py:535
  178.1 2.2 add_convert_fusion
  180.5 1.4 add_convert_fusion.1
  181.9 10.2 %attention_backward.3 = (f32[4,320,128]{2,1,0:T(8,128)}, bf16[4,320,128]{2,1,0:T(8,128)(2,1)}, bf16[4,160,128]{2,1,0:T(8,128)(2,1)}) custom-call(bf16[4,3,160,128]{3,2,1,0:T(8,128)(2,1)} %get-tuple-element.77.out_ref, bf16[3,1280,128]{2,1,0:T(8,128)(2,1)} %get-tuple-element.81.query_ref, bf16[3,2560,128]{2,1,0:T(8,128)(2,1)} %get-tuple-element.82.key_ref, ...), custom_call_target="tpu_custom_call" | custom-call | tf_op jit(solution)/shard_map/attention_backward/pallas_call | solution.py:204
  192.1 1.8 collective-permute-start.18
  193.9 10.6 %attention_backward.4 = (f32[4,320,128]{2,1,0:T(8,128)}, bf16[4,320,128]{2,1,0:T(8,128)(2,1)}, bf16[4,160,128]{2,1,0:T(8,128)(2,1)}) custom-call(bf16[4,3,160,128]{3,2,1,0:T(8,128)(2,1)} %get-tuple-element.77.out_ref, bf16[3,1280,128]{2,1,0:T(8,128)(2,1)} %get-tuple-element.81.query_ref, bf16[3,2560,128]{2,1,0:T(8,128)(2,1)} %get-tuple-element.82.key_ref, ...), custom_call_target="tpu_custom_call" | custom-call | tf_op jit(solution)/shard_map/attention_backward/pallas_call | solution.py:204
  205.6 2.1 combine.3
  208.3 3.2 collective-permute-start.21
  211.5 10.2 %attention_backward.5 = (f32[4,320,128]{2,1,0:T(8,128)}, bf16[4,320,128]{2,1,0:T(8,128)(2,1)}, bf16[4,160,128]{2,1,0:T(8,128)(2,1)}) custom-call(bf16[4,3,160,128]{3,2,1,0:T(8,128)(2,1)} %get-tuple-element.77.out_ref, bf16[3,1280,128]{2,1,0:T(8,128)(2,1)} %get-tuple-element.81.query_ref, bf16[3,2560,128]{2,1,0:T(8,128)(2,1)} %get-tuple-element.82.key_ref, ...), custom_call_target="tpu_custom_call" | custom-call | tf_op jit(solution)/shard_map/attention_backward/pallas_call | solution.py:204
  223.0 1.7 collective-permute-start.25
  224.7 2.1 combine.4
  227.9 2.7 convert_add_fusion
  231.6 1.1 collective-permute-done.25.refs_0_
  232.7 1.7 collective-permute-start.32
  234.4 2.0 collective-permute-start.37
  237.0 1.4 collective-permute-start.28
  238.5 2.9 collective-permute-start.30
  241.4 3.4 %collective-permute-done.26.refs_4_ = bf16[480,128]{1,0:T(8,128)(2,1)S(1)} collective-permute-done((bf16[480,128]{1,0:T(8,128)(2,1)}, bf16[480,128]{1,0:T(8,128)(2,1)S(1)}, u32[]{:S(2)}, u32[]{:S(2)}) %collective-permute-start.26) | collective-permute-done | bytes 122912 | tf_op jit(solution)/shard_map/ppermute | solution.py:535
  244.8 2.9 collective-permute-done.28.refs_7_
  247.7 2.1 combine.5
  249.8 2.5 collective-permute-start.27
  252.3 1.6 collective-permute-start.29
  254.6 5.6 %group_grad.1 = (f32[2,192,576]{2,1,0:T(8,128)}, bf16[2,192,576]{2,1,0:T(8,128)(2,1)}) custom-call(s32[4]{0:T(128)} %pad_add_fusion.scalar_ref, bf16[320,768]{1,0:T(8,128)(2,1)} %copy-done.1, bf16[320,768]{1,0:T(8,128)(2,1)} %copy-done.2, bf16[320,768]{1,0:T(8,128)(2,1)} %collective-permute-done.3.refs_2_, bf16[320,768]{1,0:T(8,128)(2,1)} %copy-done.3, ...), custom_call_target="tpu_custom_call" | custom-call | tf_op jit(solution)/shard_map/group_grad/pallas_call | solution.py:471
  260.3 2.2 fusion
  262.4 4.5 %all-to-all-start.1 = ((bf16[4,24,3840]{2,1,0:T(8,128)(2,1)}), bf16[4,24,3840]{2,1,0:T(8,128)(2,1)}, u32[]{:S(2)}, u32[]{:S(2)}) async-start(bf16[4,24,3840]{2,1,0:T(8,128)(2,1)} %fusion), calls=%async_computation.1 | async-start | bytes 1474560 | tf_op jit(solution)/shard_map/all_to_all | solution.py:707
  267.1 2.2 convert_add_fusion.1
  271.8 8.4 %collective-permute-done.34 = bf16[4,2,24,576]{3,2,0,1:T(8,128)(2,1)} collective-permute-done((bf16[4,2,24,576]{3,2,0,1:T(8,128)(2,1)}, bf16[4,2,24,576]{3,2,0,1:T(8,128)(2,1)}, u32[]{:S(2)}, u32[]{:S(2)}) %collective-permute-start.34) | collective-permute-done | bytes 221216 | tf_op jit(solution)/shard_map/ppermute | solution.py:535
  280.2 1.8 bitcast_add_fusion.2
  281.9 3.4 %all-to-all-done.1 = bf16[4,24,3840]{2,1,0:T(8,128)(2,1)} async-done(((bf16[4,24,3840]{2,1,0:T(8,128)(2,1)}), bf16[4,24,3840]{2,1,0:T(8,128)(2,1)}, u32[]{:S(2)}, u32[]{:S(2)}) %all-to-all-start.1) | async-done | bytes 737312 | tf_op jit(solution)/shard_map/all_to_all | solution.py:707
  286.8 1.2 fusion.1
  288.0 3.2 collective-permute-done.35
  292.3 4.2 %all-to-all-start.2 = ((bf16[4,24,3648]{2,1,0:T(8,128)(2,1)}), bf16[4,24,3648]{2,1,0:T(8,128)(2,1)}, u32[]{:S(2)}, u32[]{:S(2)}) async-start(bf16[4,24,3648]{2,1,0:T(8,128)(2,1)} %pad_maximum_fusion), calls=%async_computation.2 | async-start | bytes 1425408 | tf_op jit(solution)/shard_map/all_to_all | solution.py:712
  297.1 6.4 %input_gradient.1 = f32[320,768]{1,0:T(8,128)} custom-call(s32[4]{0:T(128)} %pad_add_fusion.scalar_ref, bf16[320,768]{1,0:T(8,128)(2,1)} %token_ref.1, f32[320,768]{1,0:T(8,128)} %get-tuple-element.79.resid_ref, f32[1,768]{1,0:T(1,128)} %broadcast_in_dim.10.gain_ref, bf16[768,2560]{1,0:T(8,128)(2,1)} %all-gather.5.cloned.1.call-done.weight_ref, ...), custom_call_target="tpu_custom_call" | custom-call | tf_op jit(solution)/shard_map/input_gradient/pallas_call | solution.py:515
  303.5 1.3 convert_reduce_fusion
  305.5 1.1 reshape.108
  306.6 1.2 copy.43
  307.9 2.6 reshape.109
  311.0 2.4 all-to-all-done.2
  315.8 1.3 convert_reduce_fusion.2
  (168 shorter events, 28.8 us)
Async XLA Ops:
  7.2 130.7 %all-gather.3.cloned.1.call-start = ((), (), s32[]{:S(2)}) async-start(), calls=%async_computation.3 | async-start | bytes 10948608 | tf_op jit(solution)/shard_map/all_gather | solution.py:630
  10.4 2.3 copy-start
  10.6 2.6 copy-start.30
  11.9 8.2 %copy-start.20 = (f32[24,2304]{1,0:T(8,128)S(1)}, f32[24,2304]{1,0:T(8,128)}, u32[]{:S(2)}) copy-start(f32[24,2304]{1,0:T(8,128)} %param.12) | copy-start | bytes 663556
  13.5 13.3 %copy-start.1 = (bf16[320,768]{1,0:T(8,128)(2,1)}, bf16[320,768]{1,0:T(8,128)(2,1)S(1)}, u32[]{:S(2)}) copy-start(bf16[320,768]{1,0:T(8,128)(2,1)S(1)} %fusion.6.refs_0_) | copy-start | bytes 1474564
  13.5 35.4 %collective-permute-start = (bf16[320,768]{1,0:T(8,128)(2,1)S(1)}, bf16[320,768]{1,0:T(8,128)(2,1)S(1)}, u32[]{:S(2)}, u32[]{:S(2)}) collective-permute-start(bf16[320,768]{1,0:T(8,128)(2,1)S(1)} %fusion.6.refs_0_), channel_id=1, source_target_pairs={{0,6},{2,0},{4,2},{6,4},{1,7},{3,1},{5,3},{7,5},{8,14},{10,8},{12,... | collective-permute-start | bytes 1474568 | tf_op jit(solution)/shard_map/ppermute | solution.py:535
  18.6 30.4 %collective-permute-start.1 = (bf16[320,768]{1,0:T(8,128)(2,1)S(1)}, bf16[320,768]{1,0:T(8,128)(2,1)S(1)}, u32[]{:S(2)}, u32[]{:S(2)}) collective-permute-start(bf16[320,768]{1,0:T(8,128)(2,1)S(1)} %fusion.6.refs_0_), channel_id=1, source_target_pairs={{0,2},{2,4},{4,6},{6,0},{1,3},{3,5},{5,7},{7,1},{8,10},{10,12},{12... | collective-permute-start | bytes 1474568 | tf_op jit(solution)/shard_map/ppermute | solution.py:535
  18.6 30.4 %collective-permute-start.2 = (bf16[320,768]{1,0:T(8,128)(2,1)S(1)}, bf16[320,768]{1,0:T(8,128)(2,1)S(1)}, u32[]{:S(2)}, u32[]{:S(2)}) collective-permute-start(bf16[320,768]{1,0:T(8,128)(2,1)S(1)} %fusion.6.refs_0_), channel_id=1, source_target_pairs={{0,1},{1,0},{2,3},{3,2},{4,5},{5,4},{6,7},{7,6},{8,9},{9,8},{10,11... | collective-permute-start | bytes 1474568 | tf_op jit(solution)/shard_map/ppermute | solution.py:535
  21.3 27.6 %all-to-all-start = ((bf16[4,24,576]{2,1,0:T(8,128)(2,1)}), bf16[4,24,576]{2,1,0:T(8,128)(2,1)S(1)}, u32[]{:S(2)}, u32[]{:S(2)}) async-start(bf16[4,24,576]{2,1,0:T(8,128)(2,1)} %reshape.97), calls=%async_computation | async-start | bytes 245760 | tf_op jit(solution)/shard_map/all_to_all | solution.py:612
  26.4 185.0 %all-gather.5.cloned.1.call-start = ((), (), s32[]{:S(2)}) async-start(), calls=%async_computation.4 | async-start | bytes 4055040 | tf_op jit(solution)/shard_map/all_gather | solution.py:653
  26.8 33.1 %copy-start.10 = (bf16[24,4,576]{2,0,1:T(8,128)(2,1)}, bf16[24,4,576]{2,0,1:T(8,128)(2,1)S(1)}, u32[]{:S(2)}) copy-start(bf16[24,4,576]{2,0,1:T(8,128)(2,1)S(1)} %reshape.101) | copy-start | bytes 331780
  48.9 12.5 %copy-start.2 = (bf16[320,768]{1,0:T(8,128)(2,1)}, bf16[320,768]{1,0:T(8,128)(2,1)S(1)}, u32[]{:S(2)}) copy-start(bf16[320,768]{1,0:T(8,128)(2,1)S(1)} %collective-permute-done.refs_1_) | copy-start | bytes 1474564
  48.9 15.0 %copy-start.3 = (bf16[320,768]{1,0:T(8,128)(2,1)}, bf16[320,768]{1,0:T(8,128)(2,1)S(1)}, u32[]{:S(2)}) copy-start(bf16[320,768]{1,0:T(8,128)(2,1)S(1)} %collective-permute-done.1.refs_3_) | copy-start | bytes 1474564
  49.0 10.8 %copy-start.16 = (bf16[320,768]{1,0:T(8,128)(2,1)}, bf16[320,768]{1,0:T(8,128)(2,1)S(1)}, u32[]{:S(2)}) copy-start(bf16[320,768]{1,0:T(8,128)(2,1)S(1)} %collective-permute-done.2.refs_4_) | copy-start | bytes 1474564
  49.0 6.5 %collective-permute-start.7 = (bf16[4,24,576]{2,1,0:T(8,128)(2,1)S(1)}, bf16[4,24,576]{2,1,0:T(8,128)(2,1)S(1)}, u32[]{:S(2)}, u32[]{:S(2)}) collective-permute-start(bf16[4,24,576]{2,1,0:T(8,128)(2,1)S(1)} %all-to-all-done), channel_id=1, source_target_pairs={{0,1},{1,0},{2,3},{3,2},{4,5},{5,4},{6,7},{7,6},{8,9},{9,8},{10,11... | collective-permute-start | bytes 331784 | tf_op jit(solution)/shard_map/ppermute | solution.py:535
  55.6 4.2 %collective-permute-start.8 = (bf16[2,4,24,576]{3,2,1,0:T(8,128)(2,1)S(1)}, bf16[2,4,24,576]{3,2,1,0:T(8,128)(2,1)S(1)}, u32[]{:S(2)}, u32[]{:S(2)}) collective-permute-start(bf16[2,4,24,576]{3,2,1,0:T(8,128)(2,1)S(1)} %pad_maximum_fusion.2), channel_id=1, source_target_pairs={{0,8},{8,0},{1,9},{9,1},{2,10},{10,2},{3,11},{11,3},{4,12},{12,4},... | collective-permute-start | bytes 663560 | tf_op jit(solution)/shard_map/ppermute | solution.py:535
  55.7 23.2 %collective-permute-start.3 = (bf16[320,768]{1,0:T(8,128)(2,1)S(1)}, bf16[320,768]{1,0:T(8,128)(2,1)}, u32[]{:S(2)}, u32[]{:S(2)}) collective-permute-start(bf16[320,768]{1,0:T(8,128)(2,1)S(1)} %collective-permute-done.refs_1_), channel_id=1, source_target_pairs={{0,6},{2,0},{4,2},{6,4},{1,7},{3,1},{5,3},{7,5},{8,14},{10,8},{12,... | collective-permute-start | bytes 1474568 | tf_op jit(solution)/shard_map/ppermute | solution.py:535
  59.9 21.0 %collective-permute-start.9 = (bf16[2,2,4,24,576]{4,3,2,1,0:T(8,128)(2,1)S(1)}, bf16[2,2,4,24,576]{4,3,2,1,0:T(8,128)(2,1)S(1)}, u32[]{:S(2)}, u32[]{:S(2)}) collective-permute-start(bf16[2,2,4,24,576]{4,3,2,1,0:T(8,128)(2,1)S(1)} %pad_maximum_fusion.1), channel_id=1, source_target_pairs={{0,16},{16,0},{1,17},{17,1},{2,18},{18,2},{3,19},{19,3},{4,20},{20... | collective-permute-start | bytes 1327112 | tf_op jit(solution)/shard_map/ppermute | solution.py:535
  61.4 22.8 %collective-permute-start.4 = (bf16[320,768]{1,0:T(8,128)(2,1)S(1)}, bf16[320,768]{1,0:T(8,128)(2,1)}, u32[]{:S(2)}, u32[]{:S(2)}) collective-permute-start(bf16[320,768]{1,0:T(8,128)(2,1)S(1)} %collective-permute-done.refs_1_), channel_id=1, source_target_pairs={{0,1},{1,0},{2,3},{3,2},{4,5},{5,4},{6,7},{7,6},{8,9},{9,8},{10,11... | collective-permute-start | bytes 1474568 | tf_op jit(solution)/shard_map/ppermute | solution.py:535
  63.9 23.0 %collective-permute-start.6 = (bf16[320,768]{1,0:T(8,128)(2,1)S(1)}, bf16[320,768]{1,0:T(8,128)(2,1)}, u32[]{:S(2)}, u32[]{:S(2)}) collective-permute-start(bf16[320,768]{1,0:T(8,128)(2,1)S(1)} %collective-permute-done.1.refs_3_), channel_id=1, source_target_pairs={{0,1},{1,0},{2,3},{3,2},{4,5},{5,4},{6,7},{7,6},{8,9},{9,8},{10,11... | collective-permute-start | bytes 1474568 | tf_op jit(solution)/shard_map/ppermute | solution.py:535
  78.8 28.1 %collective-permute-start.5 = (bf16[320,768]{1,0:T(8,128)(2,1)}, bf16[320,768]{1,0:T(8,128)(2,1)}, u32[]{:S(2)}, u32[]{:S(2)}) collective-permute-start(bf16[320,768]{1,0:T(8,128)(2,1)} %collective-permute-done.3.refs_2_), channel_id=1, source_target_pairs={{0,1},{1,0},{2,3},{3,2},{4,5},{5,4},{6,7},{7,6},{8,9},{9,8},{10,11... | collective-permute-start | bytes 1474568 | tf_op jit(solution)/shard_map/ppermute | solution.py:535
  107.0 25.7 %copy-start.31 = (f32[768]{0:T(1024)S(1)}, f32[768]{0:T(1024)}, u32[]{:S(2)}) copy-start(f32[768]{0:T(1024)} %param.17) | copy-start | bytes 9220
  128.3 6.8 %collective-permute-start.10 = (bf16[3,160,128]{2,1,0:T(8,128)(2,1)S(1)}, bf16[3,160,128]{2,1,0:T(8,128)(2,1)S(1)}, u32[]{:S(2)}, u32[]{:S(2)}) collective-permute-start(bf16[3,160,128]{2,1,0:T(8,128)(2,1)S(1)} %get-tuple-element.142), channel_id=1, source_target_pairs={{0,2},{2,4},{4,6},{6,0},{1,3},{3,5},{5,7},{7,1},{8,10},{10,12},{12... | collective-permute-start | bytes 368648 | tf_op jit(solution)/shard_map/ppermute | solution.py:535
  128.3 9.5 %collective-permute-start.11 = (bf16[3,160,128]{2,1,0:T(8,128)(2,1)S(1)}, bf16[3,160,128]{2,1,0:T(8,128)(2,1)S(1)}, u32[]{:S(2)}, u32[]{:S(2)}) collective-permute-start(bf16[3,160,128]{2,1,0:T(8,128)(2,1)S(1)} %get-tuple-element.141), channel_id=1, source_target_pairs={{0,4},{2,6},{4,0},{6,2},{1,5},{3,7},{5,1},{7,3},{8,12},{10,14},{12... | collective-permute-start | bytes 368648 | tf_op jit(solution)/shard_map/ppermute | solution.py:535
  128.4 9.5 %collective-permute-start.12 = (bf16[3,160,128]{2,1,0:T(8,128)(2,1)S(1)}, bf16[3,160,128]{2,1,0:T(8,128)(2,1)S(1)}, u32[]{:S(2)}, u32[]{:S(2)}) collective-permute-start(bf16[3,160,128]{2,1,0:T(8,128)(2,1)S(1)} %get-tuple-element.140), channel_id=1, source_target_pairs={{0,6},{2,0},{4,2},{6,4},{1,7},{3,1},{5,3},{7,5},{8,14},{10,8},{12,... | collective-permute-start | bytes 368648 | tf_op jit(solution)/shard_map/ppermute | solution.py:535
  135.2 2.7 copy-start.26
  161.2 16.8 %collective-permute-start.13 = (bf16[192,3840]{1,0:T(8,128)(2,1)}, bf16[192,3840]{1,0:T(8,128)(2,1)S(1)}, u32[]{:S(2)}, u32[]{:S(2)}) collective-permute-start(bf16[192,3840]{1,0:T(8,128)(2,1)} %get-tuple-element.86), channel_id=1, source_target_pairs={{0,8},{8,0},{1,9},{9,1},{2,10},{10,2},{3,11},{11,3},{4,12},{12,4},... | collective-permute-start | bytes 4423688 | tf_op jit(solution)/shard_map/ppermute | solution.py:535
  161.3 7.7 %collective-permute-start.14 = (bf16[3,160,128]{2,1,0:T(8,128)(2,1)}, bf16[3,160,128]{2,1,0:T(8,128)(2,1)S(1)}, u32[]{:S(2)}, u32[]{:S(2)}) collective-permute-start(bf16[3,160,128]{2,1,0:T(8,128)(2,1)} %get-tuple-element.87), channel_id=1, source_target_pairs={{0,6},{2,0},{4,2},{6,4},{1,7},{3,1},{5,3},{7,5},{8,14},{10,8},{12,... | collective-permute-start | bytes 368648 | tf_op jit(solution)/shard_map/ppermute | solution.py:535
  163.8 14.2 %collective-permute-start.15 = (bf16[3,160,128]{2,1,0:T(8,128)(2,1)}, bf16[3,160,128]{2,1,0:T(8,128)(2,1)S(1)}, u32[]{:S(2)}, u32[]{:S(2)}) collective-permute-start(bf16[3,160,128]{2,1,0:T(8,128)(2,1)} %get-tuple-element.88), channel_id=1, source_target_pairs={{0,4},{2,6},{4,0},{6,2},{1,5},{3,7},{5,1},{7,3},{8,12},{10,14},{12... | collective-permute-start | bytes 368648 | tf_op jit(solution)/shard_map/ppermute | solution.py:535
  164.6 13.4 %collective-permute-start.16 = (bf16[3,160,128]{2,1,0:T(8,128)(2,1)}, bf16[3,160,128]{2,1,0:T(8,128)(2,1)S(1)}, u32[]{:S(2)}, u32[]{:S(2)}) collective-permute-start(bf16[3,160,128]{2,1,0:T(8,128)(2,1)} %get-tuple-element.89), channel_id=1, source_target_pairs={{0,2},{2,4},{4,6},{6,0},{1,3},{3,5},{5,7},{7,1},{8,10},{10,12},{12... | collective-permute-start | bytes 368648 | tf_op jit(solution)/shard_map/ppermute | solution.py:535
  164.6 43.7 %collective-permute-start.23 = (bf16[192,3840]{1,0:T(8,128)(2,1)}, bf16[192,3840]{1,0:T(8,128)(2,1)}, u32[]{:S(2)}, u32[]{:S(2)}) collective-permute-start(bf16[192,3840]{1,0:T(8,128)(2,1)} %get-tuple-element.113), channel_id=1, source_target_pairs={{0,8},{8,0},{1,9},{9,1},{2,10},{10,2},{3,11},{11,3},{4,12},{12,4},... | collective-permute-start | bytes 4423688 | tf_op jit(solution)/shard_map/ppermute | solution.py:535
  169.0 11.2 %copy-start.12 = (bf16[3,160,128]{2,1,0:T(8,128)(2,1)}, bf16[3,160,128]{2,1,0:T(8,128)(2,1)S(1)}, u32[]{:S(2)}) copy-start(bf16[3,160,128]{2,1,0:T(8,128)(2,1)S(1)} %collective-permute-done.14.refs_1_) | copy-start | bytes 368644
  169.0 11.5 %collective-permute-start.17 = (bf16[192,3072]{1,0:T(8,128)(2,1)}, bf16[192,3072]{1,0:T(8,128)(2,1)S(1)}, u32[]{:S(2)}, u32[]{:S(2)}) collective-permute-start(bf16[192,3072]{1,0:T(8,128)(2,1)} %get-tuple-element.92), channel_id=1, source_target_pairs={{0,8},{8,0},{1,9},{9,1},{2,10},{10,2},{3,11},{11,3},{4,12},{12,4},... | collective-permute-start | bytes 3538952 | tf_op jit(solution)/shard_map/ppermute | solution.py:535
  178.0 2.4 copy-start.8
  180.3 46.5 %collective-permute-start.24 = (bf16[192,3840]{1,0:T(8,128)(2,1)S(1)}, bf16[192,3840]{1,0:T(8,128)(2,1)S(1)}, u32[]{:S(2)}, u32[]{:S(2)}) collective-permute-start(bf16[192,3840]{1,0:T(8,128)(2,1)S(1)} %add_convert_fusion), channel_id=1, source_target_pairs={{0,16},{16,0},{1,17},{17,1},{2,18},{18,2},{3,19},{19,3},{4,20},{20... | collective-permute-start | bytes 4423688 | tf_op jit(solution)/shard_map/ppermute | solution.py:535
  192.1 12.7 %collective-permute-start.18 = (bf16[4,320,128]{2,1,0:T(8,128)(2,1)}, bf16[4,320,128]{2,1,0:T(8,128)(2,1)S(1)}, u32[]{:S(2)}, u32[]{:S(2)}) collective-permute-start(bf16[4,320,128]{2,1,0:T(8,128)(2,1)} %get-tuple-element.100), channel_id=1, source_target_pairs={{0,1},{1,0},{2,3},{3,2},{4,5},{5,4},{6,7},{7,6},{8,9},{9,8},{10,11... | collective-permute-start | bytes 983048 | tf_op jit(solution)/shard_map/ppermute | solution.py:535
  204.5 20.2 %collective-permute-start.22 = (bf16[4,320,128]{2,1,0:T(8,128)(2,1)}, bf16[4,320,128]{2,1,0:T(8,128)(2,1)}, u32[]{:S(2)}, u32[]{:S(2)}) collective-permute-start(bf16[4,320,128]{2,1,0:T(8,128)(2,1)} %get-tuple-element.110), channel_id=1, source_target_pairs={{0,1},{1,0},{2,3},{3,2},{4,5},{5,4},{6,7},{7,6},{8,9},{9,8},{10,11... | collective-permute-start | bytes 983048 | tf_op jit(solution)/shard_map/ppermute | solution.py:535
  207.6 14.0 %collective-permute-start.19 = (bf16[480,128]{1,0:T(8,128)(2,1)}, bf16[480,128]{1,0:T(8,128)(2,1)S(1)}, u32[]{:S(2)}, u32[]{:S(2)}) collective-permute-start(bf16[480,128]{1,0:T(8,128)(2,1)} %get-tuple-element.102.refs_7_), channel_id=1, source_target_pairs={{0,2},{2,4},{4,6},{6,0},{1,3},{3,5},{5,7},{7,1},{8,10},{10,12},{12... | collective-permute-start | bytes 368648 | tf_op jit(solution)/shard_map/ppermute | solution.py:535
  207.6 14.1 %collective-permute-start.20 = (bf16[480,128]{1,0:T(8,128)(2,1)}, bf16[480,128]{1,0:T(8,128)(2,1)S(1)}, u32[]{:S(2)}, u32[]{:S(2)}) collective-permute-start(bf16[480,128]{1,0:T(8,128)(2,1)} %get-tuple-element.103.refs_10_), channel_id=1, source_target_pairs={{0,4},{2,6},{4,0},{6,2},{1,5},{3,7},{5,1},{7,3},{8,12},{10,14},{12... | collective-permute-start | bytes 368648 | tf_op jit(solution)/shard_map/ppermute | solution.py:535
  208.3 16.4 %collective-permute-start.21 = (bf16[480,128]{1,0:T(8,128)(2,1)}, bf16[480,128]{1,0:T(8,128)(2,1)S(1)}, u32[]{:S(2)}, u32[]{:S(2)}) collective-permute-start(bf16[480,128]{1,0:T(8,128)(2,1)} %get-tuple-element.104.refs_13_), channel_id=1, source_target_pairs={{0,6},{2,0},{4,2},{6,4},{1,7},{3,1},{5,3},{7,5},{8,14},{10,8},{12,... | collective-permute-start | bytes 368648 | tf_op jit(solution)/shard_map/ppermute | solution.py:535
  221.7 16.8 %collective-permute-start.36 = (bf16[192,3072]{1,0:T(8,128)(2,1)}, bf16[192,3072]{1,0:T(8,128)(2,1)}, u32[]{:S(2)}, u32[]{:S(2)}) collective-permute-start(bf16[192,3072]{1,0:T(8,128)(2,1)} %get-tuple-element.134), channel_id=1, source_target_pairs={{0,8},{8,0},{1,9},{9,1},{2,10},{10,2},{3,11},{11,3},{4,12},{12,4},... | collective-permute-start | bytes 3538952 | tf_op jit(solution)/shard_map/ppermute | solution.py:535
  223.0 9.8 %collective-permute-start.25 = (bf16[4,320,128]{2,1,0:T(8,128)(2,1)}, bf16[4,320,128]{2,1,0:T(8,128)(2,1)S(1)}, u32[]{:S(2)}, u32[]{:S(2)}) collective-permute-start(bf16[4,320,128]{2,1,0:T(8,128)(2,1)} %get-tuple-element.122), channel_id=1, source_target_pairs={{0,1},{1,0},{2,3},{3,2},{4,5},{5,4},{6,7},{7,6},{8,9},{9,8},{10,11... | collective-permute-start | bytes 983048 | tf_op jit(solution)/shard_map/ppermute | solution.py:535
  224.7 6.0 %copy-start.23 = (bf16[480,128]{1,0:T(8,128)(2,1)}, bf16[480,128]{1,0:T(8,128)(2,1)S(1)}, u32[]{:S(2)}) copy-start(bf16[480,128]{1,0:T(8,128)(2,1)S(1)} %collective-permute-done.21.refs_9_) | copy-start | bytes 368644
  232.7 14.9 %copy-start.18 = (bf16[4,320,128]{2,1,0:T(8,128)(2,1)}, bf16[4,320,128]{2,1,0:T(8,128)(2,1)S(1)}, u32[]{:S(2)}) copy-start(bf16[4,320,128]{2,1,0:T(8,128)(2,1)S(1)} %collective-permute-done.25.refs_0_) | copy-start | bytes 983044
  232.7 27.5 %collective-permute-start.32 = (bf16[4,24,3840]{2,1,0:T(8,128)(2,1)}, bf16[4,24,3840]{2,1,0:T(8,128)(2,1)}, u32[]{:S(2)}, u32[]{:S(2)}) collective-permute-start(bf16[4,24,3840]{2,1,0:T(8,128)(2,1)} %fusion.7), channel_id=1, source_target_pairs={{0,1},{1,0},{2,3},{3,2},{4,5},{5,4},{6,7},{7,6},{8,9},{9,8},{10,11... | collective-permute-start | bytes 2211848 | tf_op jit(solution)/shard_map/ppermute | solution.py:535
  234.4 32.6 %collective-permute-start.37 = (bf16[192,3072]{1,0:T(8,128)(2,1)}, bf16[192,3072]{1,0:T(8,128)(2,1)}, u32[]{:S(2)}, u32[]{:S(2)}) collective-permute-start(bf16[192,3072]{1,0:T(8,128)(2,1)} %add_convert_fusion.1), channel_id=1, source_target_pairs={{0,16},{16,0},{1,17},{17,1},{2,18},{18,2},{3,19},{19,3},{4,20},{20... | collective-permute-start | bytes 3538952 | tf_op jit(solution)/shard_map/ppermute | solution.py:535
  236.5 8.3 %collective-permute-start.26 = (bf16[480,128]{1,0:T(8,128)(2,1)}, bf16[480,128]{1,0:T(8,128)(2,1)S(1)}, u32[]{:S(2)}, u32[]{:S(2)}) collective-permute-start(bf16[480,128]{1,0:T(8,128)(2,1)} %get-tuple-element.115.refs_8_), channel_id=1, source_target_pairs={{0,2},{2,4},{4,6},{6,0},{1,3},{3,5},{5,7},{7,1},{8,10},{10,12},{12... | collective-permute-start | bytes 368648 | tf_op jit(solution)/shard_map/ppermute | solution.py:535
  237.0 10.6 %collective-permute-start.28 = (bf16[480,128]{1,0:T(8,128)(2,1)}, bf16[480,128]{1,0:T(8,128)(2,1)S(1)}, u32[]{:S(2)}, u32[]{:S(2)}) collective-permute-start(bf16[480,128]{1,0:T(8,128)(2,1)} %get-tuple-element.116.refs_11_), channel_id=1, source_target_pairs={{0,4},{2,6},{4,0},{6,2},{1,5},{3,7},{5,1},{7,3},{8,12},{10,14},{12... | collective-permute-start | bytes 368648 | tf_op jit(solution)/shard_map/ppermute | solution.py:535
  238.5 9.2 %collective-permute-start.30 = (bf16[480,128]{1,0:T(8,128)(2,1)}, bf16[480,128]{1,0:T(8,128)(2,1)}, u32[]{:S(2)}, u32[]{:S(2)}) collective-permute-start(bf16[480,128]{1,0:T(8,128)(2,1)} %get-tuple-element.117.refs_14_), channel_id=1, source_target_pairs={{0,6},{2,0},{4,2},{6,4},{1,7},{3,1},{5,3},{7,5},{8,14},{10,8},{12,... | collective-permute-start | bytes 368648 | tf_op jit(solution)/shard_map/ppermute | solution.py:535
  244.8 15.4 %copy-start.24 = (bf16[480,128]{1,0:T(8,128)(2,1)}, bf16[480,128]{1,0:T(8,128)(2,1)S(1)}, u32[]{:S(2)}) copy-start(bf16[480,128]{1,0:T(8,128)(2,1)S(1)} %collective-permute-done.26.refs_4_) | copy-start | bytes 368644
  247.7 12.6 %copy-start.25 = (bf16[480,128]{1,0:T(8,128)(2,1)}, bf16[480,128]{1,0:T(8,128)(2,1)S(1)}, u32[]{:S(2)}) copy-start(bf16[480,128]{1,0:T(8,128)(2,1)S(1)} %collective-permute-done.28.refs_7_) | copy-start | bytes 368644
  249.8 17.2 %collective-permute-start.27 = (bf16[480,128]{1,0:T(8,128)(2,1)}, bf16[480,128]{1,0:T(8,128)(2,1)}, u32[]{:S(2)}, u32[]{:S(2)}) collective-permute-start(bf16[480,128]{1,0:T(8,128)(2,1)} %get-tuple-element.124.refs_9_), channel_id=1, source_target_pairs={{0,2},{2,4},{4,6},{6,0},{1,3},{3,5},{5,7},{7,1},{8,10},{10,12},{12... | collective-permute-start | bytes 368648 | tf_op jit(solution)/shard_map/ppermute | solution.py:535
  252.3 14.7 %collective-permute-start.29 = (bf16[480,128]{1,0:T(8,128)(2,1)}, bf16[480,128]{1,0:T(8,128)(2,1)}, u32[]{:S(2)}, u32[]{:S(2)}) collective-permute-start(bf16[480,128]{1,0:T(8,128)(2,1)} %get-tuple-element.125.refs_12_), channel_id=1, source_target_pairs={{0,4},{2,6},{4,0},{6,2},{1,5},{3,7},{5,1},{7,3},{8,12},{10,14},{12... | collective-permute-start | bytes 368648 | tf_op jit(solution)/shard_map/ppermute | solution.py:535
  253.9 13.1 %collective-permute-start.31 = (bf16[480,128]{1,0:T(8,128)(2,1)}, bf16[480,128]{1,0:T(8,128)(2,1)}, u32[]{:S(2)}, u32[]{:S(2)}) collective-permute-start(bf16[480,128]{1,0:T(8,128)(2,1)} %get-tuple-element.126.refs_15_), channel_id=1, source_target_pairs={{0,6},{2,0},{4,2},{6,4},{1,7},{3,1},{5,3},{7,5},{8,14},{10,8},{12,... | collective-permute-start | bytes 368648 | tf_op jit(solution)/shard_map/ppermute | solution.py:535
  262.4 4.6 %copy-start.9 = (bf16[192,3072]{1,0:T(8,128)(2,1)S(1)}, bf16[192,3072]{1,0:T(8,128)(2,1)}, u32[]{:S(2)}) copy-start(bf16[192,3072]{1,0:T(8,128)(2,1)} %get-tuple-element.133) | copy-start | bytes 3538948
  262.4 22.8 %all-to-all-start.1 = ((bf16[4,24,3840]{2,1,0:T(8,128)(2,1)}), bf16[4,24,3840]{2,1,0:T(8,128)(2,1)}, u32[]{:S(2)}, u32[]{:S(2)}) async-start(bf16[4,24,3840]{2,1,0:T(8,128)(2,1)} %fusion), calls=%async_computation.1 | async-start | bytes 1474560 | tf_op jit(solution)/shard_map/all_to_all | solution.py:707
  267.0 3.7 %collective-permute-start.33 = (bf16[2,192,576]{2,1,0:T(8,128)(2,1)}, bf16[2,192,576]{2,1,0:T(8,128)(2,1)S(1)}, u32[]{:S(2)}, u32[]{:S(2)}) collective-permute-start(bf16[2,192,576]{2,1,0:T(8,128)(2,1)} %get-tuple-element.131), channel_id=1, source_target_pairs={{0,8},{8,0},{1,9},{9,1},{2,10},{10,2},{3,11},{11,3},{4,12},{12,4},... | collective-permute-start | bytes 1327112 | tf_op jit(solution)/shard_map/ppermute | solution.py:535
  270.2 16.6 %collective-permute-start.38 = (bf16[4,24,3072]{2,1,0:T(8,128)(2,1)}, bf16[4,24,3072]{2,1,0:T(8,128)(2,1)}, u32[]{:S(2)}, u32[]{:S(2)}) collective-permute-start(bf16[4,24,3072]{2,1,0:T(8,128)(2,1)} %fusion.8), channel_id=1, source_target_pairs={{0,1},{1,0},{2,3},{3,2},{4,5},{5,4},{6,7},{7,6},{8,9},{9,8},{10,11... | collective-permute-start | bytes 1769480 | tf_op jit(solution)/shard_map/ppermute | solution.py:535
  271.5 8.7 %collective-permute-start.34 = (bf16[4,2,24,576]{3,2,0,1:T(8,128)(2,1)}, bf16[4,2,24,576]{3,2,0,1:T(8,128)(2,1)}, u32[]{:S(2)}, u32[]{:S(2)}) collective-permute-start(bf16[4,2,24,576]{3,2,0,1:T(8,128)(2,1)} %fusion.9), channel_id=1, source_target_pairs={{0,16},{16,0},{1,17},{17,1},{2,18},{18,2},{3,19},{19,3},{4,20},{20... | collective-permute-start | bytes 663560 | tf_op jit(solution)/shard_map/ppermute | solution.py:535
  281.9 9.3 %copy-start.4 = (f32[4,2,24,576]{3,2,0,1:T(8,128)S(1)}, f32[4,2,24,576]{3,2,0,1:T(8,128)}, u32[]{:S(2)}) copy-start(f32[4,2,24,576]{3,2,0,1:T(8,128)} %bitcast_add_fusion.2) | copy-start | bytes 1327108
  286.2 4.9 %collective-permute-start.35 = (bf16[4,24,576]{2,1,0:T(8,128)(2,1)S(1)}, bf16[4,24,576]{2,1,0:T(8,128)(2,1)S(1)}, u32[]{:S(2)}, u32[]{:S(2)}) collective-permute-start(bf16[4,24,576]{2,1,0:T(8,128)(2,1)S(1)} %fusion.12), channel_id=1, source_target_pairs={{0,1},{1,0},{2,3},{3,2},{4,5},{5,4},{6,7},{7,6},{8,9},{9,8},{10,11... | collective-permute-start | bytes 331784 | tf_op jit(solution)/shard_map/ppermute | solution.py:535
  292.3 21.1 %all-to-all-start.2 = ((bf16[4,24,3648]{2,1,0:T(8,128)(2,1)}), bf16[4,24,3648]{2,1,0:T(8,128)(2,1)}, u32[]{:S(2)}, u32[]{:S(2)}) async-start(bf16[4,24,3648]{2,1,0:T(8,128)(2,1)} %pad_maximum_fusion), calls=%async_computation.2 | async-start | bytes 1425408 | tf_op jit(solution)/shard_map/all_to_all | solution.py:712
  297.1 8.3 %copy-start.7 = (bf16[24,3072]{1,0:T(8,128)(2,1)S(1)}, bf16[24,3072]{1,0:T(8,128)(2,1)}, u32[]{:S(2)}) copy-start(bf16[24,3072]{1,0:T(8,128)(2,1)} %copy-done.6) | copy-start | bytes 442372
  314.8 3.3 %copy-start.11 = (bf16[24,4,576]{2,0,1:T(8,128)(2,1)S(1)}, bf16[24,4,576]{2,0,1:T(8,128)(2,1)}, u32[]{:S(2)}) copy-start(bf16[24,4,576]{2,0,1:T(8,128)(2,1)} %copy-done.10) | copy-start | bytes 331780
  (12 other events, 14.1 us)
Sparse Core Ops, SparseCore 0:
  12.9 115.8 all-gather.2
  131.7 71.3 all-gather.4

commit v2 on v1

--- a/solution.py
+++ b/solution.py
@@ -139,7 +139,7 @@
     half = rows // 2
     lane = lax.broadcasted_iota(jnp.int32, (rows, HEAD), 1)
     for index in range(n_own):
-        packed = grads[index][0]
+        packed = grads[index][...]
         grad = jnp.concatenate([packed[:, :HEAD], packed[:, HEAD:]], axis=0)
         packed_out = out_ref[index, 0]
         attended = jnp.concatenate([packed_out[:, :HEAD], packed_out[:, HEAD:]], axis=0)
@@ -205,7 +205,10 @@
         functools.partial(attention_backward_kernel, rows, n_own),
         grid=(1,),
         in_specs=[stacked(n_own, half), per_head(n_queries), per_head(n_keys), per_head(n_keys)]
-        + [per_head(half) for _ in grads],
+        + [
+            pl.BlockSpec((None, half, LANES), lambda i: (head - 1, 0, 0)) if head else vmem
+            for _ in grads
+        ],
         out_specs=[vmem, vmem, vmem],
         out_shape=[
             jax.ShapeDtypeStruct((n_own, rows, LANES), F32),
@@ -240,6 +243,8 @@
 def middle_kernel(sizes, scalar_ref, *refs):
     n_g, wide, width, rows, n_a, chunks = sizes
     refs = list(refs)
+    part = width // n_g
+    heads = part // HEAD
 
     def take(count):
         taken = refs[:count]
@@ -250,12 +255,10 @@
     pieces = take(n_g)
     (weight_hbm,) = take(1)
     mixed_ref, resid_ref = take(2)
-    grads = take(n_g)
+    grads = take(2 * n_g)
     grad_hbm = [take(2 * n_a) for _ in chunks]
     weight_scr, made_scr, attended_scr, in_sem, out_sem = refs
     half = rows // 2
-    part = width // n_g
-    heads = part // HEAD
     block = width // (2 * n_a)
     here_a, here_c = scalar_ref[3], scalar_ref[2]
 
@@ -362,9 +365,11 @@
         grad_block = nt(branch, weight_scr[0, places(k), :])
         for h in range(heads):
             here = slice(h * HEAD, (h + 1) * HEAD)
-            grads[k][h] = jnp.concatenate(
-                [grad_block[:half, here], grad_block[half:, here]], axis=1
-            ).astype(BF16)
+            packed = jnp.concatenate([grad_block[:half, here], grad_block[half:, here]], axis=1)
+            if h == 0:
+                grads[k][...] = packed.astype(BF16)
+            else:
+                grads[n_g + k][h - 1] = packed.astype(BF16)
     for k in range(n_g):
         made_scr[0, places(k), :] = tn(attended_scr[k], branch).astype(BF16)
     start(flush(0))
@@ -375,6 +380,7 @@
 def middle(scalars, tokens, cotangent, gain, pieces, weights, n_a):
     rows, width = tokens.shape
     n_g = len(pieces)
+    heads, half, _ = pieces[0].shape
     count = weights.shape[1] // width
     wide = (count - 1) // 2
     chunks = (1 + 2 * (wide // 2), 2 * (wide - wide // 2))
@@ -388,12 +394,13 @@
     return pl.pallas_call(
         functools.partial(middle_kernel, (n_g, wide, width, rows, n_a, chunks)),
         in_specs=[pl.BlockSpec(memory_space=pltpu.SMEM)] + [vmem] * (3 + n_g) + [anywhere],
-        out_specs=[vmem] * (2 + n_g) + [anywhere] * len(flat),
+        out_specs=[vmem] * (2 + 2 * n_g) + [anywhere] * len(flat),
         out_shape=[
             jax.ShapeDtypeStruct((rows, width), BF16),
             jax.ShapeDtypeStruct((rows, width), F32),
         ]
-        + [jax.ShapeDtypeStruct(piece.shape, BF16) for piece in pieces]
+        + [jax.ShapeDtypeStruct((half, LANES), BF16)] * n_g
+        + [jax.ShapeDtypeStruct((heads - 1, half, LANES), BF16)] * n_g
         + flat,
         scratch_shapes=[
             pltpu.VMEM((count, width, width), BF16),
@@ -523,6 +530,47 @@
     )(scalars, tokens, grad_resid, gain, weight, *flat)
 
 
+def share_kernel(wide, got_ref, weight_ref, gain_ref, down_ref, qkv_ref, norm_ref):
+    n_g, share, columns = weight_ref.shape
+    heads = columns // (3 * HEAD)
+    width = n_g * heads * HEAD
+    for q in range(wide):
+        here = slice(q * width, (q + 1) * width)
+        total = got_ref[0, :, here].astype(F32)
+        for g in range(1, n_g):
+            total = total + got_ref[g, :, here].astype(F32)
+        down_ref[q] = total
+    norm = jnp.zeros((share, 1), F32)
+    for g in range(n_g):
+        made = got_ref[g, :, wide * width :].astype(F32)
+        norm = norm + jnp.sum(made * weight_ref[g].astype(F32), axis=1, keepdims=True)
+        for h in range(heads):
+            for part in range(3):
+                start = part * width + (g * heads + h) * HEAD
+                at = (h * 3 + part) * HEAD
+                qkv_ref[:, start : start + HEAD] = made[:, at : at + HEAD]
+    norm_ref[...] = norm / gain_ref[...]
+
+
+def last_shares(got, weight, gain):
+    n_g, share, columns = weight.shape
+    width = n_g * columns // 3
+    wide = (got.shape[2] - columns) // width
+    vmem = pl.BlockSpec(memory_space=pltpu.VMEM)
+    return pl.pallas_call(
+        functools.partial(share_kernel, wide),
+        in_specs=[vmem] * 3,
+        out_specs=[vmem] * 3,
+        out_shape=[
+            jax.ShapeDtypeStruct((wide, share, width), F32),
+            jax.ShapeDtypeStruct((share, 3 * width), F32),
+            jax.ShapeDtypeStruct((share, 1), F32),
+        ],
+        compiler_params=pltpu.CompilerParams(vmem_limit_bytes=VMEM_LIMIT),
+        name="last_shares",
+    )(got, weight, gain)
+
+
 def norm_rows(values, gain_vector):
     mean_value = jnp.mean(values, axis=-1, keepdims=True)
     centered = values - mean_value
@@ -639,8 +687,9 @@
     out, query, key, value = attention_forward(scene_tokens, pieces, group_weight, n_g)
     back = [out[0]] + [shift(out[k], "g", k) for k in range(1, n_g)]
     made = middle(scalars, tokens, cotangent, gain_two[None], back, weights, n_a)
-    mixed, grad_resid, sends = made[0], made[1], made[2 : 2 + n_g]
-    grad_blocks = [made[2 + n_g : 2 + n_g + n_a * n_c], made[2 + n_g + n_a * n_c :]]
+    mixed, grad_resid, sends = made[0], made[1], made[2 : 2 + 2 * n_g]
+    made = made[2 + 2 * n_g :]
+    grad_blocks = [made[: n_a * n_c], made[n_a * n_c :]]
 
     come = [[shift(block, "c", 1) for block in some[n_a:]] for some in grad_blocks]
 
@@ -652,7 +701,10 @@
     qkv_weight = after(qkv_weight.reshape(share, n_g * padded), *ready)
     qkv_weight = lax.all_gather(qkv_weight, ALL, axis=0, tiled=True)
 
-    grads = [sends[0]] + [shift(sends[k], "g", -k) for k in range(1, n_g)]
+    grads = [[sends[0]] + [shift(sends[k], "g", -k) for k in range(1, n_g)]]
+    some = [after(block, *grads[0]) for block in sends[n_g:]]
+    grads += [[some[0]] + [shift(some[k], "g", -k) for k in range(1, n_g)]] * (heads - 1)
+
     made = []
     grad_pieces = []
     whole = []
@@ -667,9 +719,9 @@
         whole.append([done[0]] + [shift(done[k], "g", k) for k in range(1, n_g)])
 
     for head in range(heads):
-        gate = [made[-1][0]] if head == 1 else []
-        if head == 0:
-            come = [[after(block, *grads) for block in some] for some in come]
+        gate = []
+        if head == 1:
+            come = [[after(block, made[0][0], *grads[1]) for block in some] for some in come]
             far = [
                 [add_low(*pair) for pair in zip(some[1:n_a], there[1:])]
                 for some, there in zip(grad_blocks, come)
@@ -679,7 +731,9 @@
         if head >= 2:
             finish(head - 2)
             gate = [*grad_pieces[head - 2], qkv_weight]
-        gated = ([after(grads[0], *gate)] if gate else grads[:1]) + grads[1:]
+        gated = grads[head]
+        if gate:
+            gated = [after(gated[0], *gate)] + gated[1:]
         own, across, grad_query = attention_backward(out, query, key, value, gated, head)
         across = [
             shift(across[(j - 1) * n_g : j * n_g] if n_r > 2 else across, "r", j)
@@ -708,7 +762,7 @@
     qkv_grad = add_high(mine, shift(theirs, "c", 1))
     qkv_grad = qkv_grad.reshape(n_a, n_g, n_r, share, columns)
     qkv_grad = scatter_sum(after(scatter_sum(qkv_grad, "a", 0), first), "r", 1)
-    second = jnp.concatenate([qkv_grad.astype(BF16), second], axis=2)
+    second = jnp.concatenate([second, qkv_grad.astype(BF16)], axis=2)
     second = lax.all_to_all(after(second, first), "g", 0, 0)
     input_grad = input_gradient(scalars, tokens, grad_resid, gain_one[None], qkv_weight, whole)
 
@@ -719,23 +773,15 @@
     up_share = (
         up_share.reshape(share, wide, n_all, share).transpose(0, 2, 1, 3).reshape(share, hidden)
     )
-    qkv_share = second[:, :, :columns].astype(F32)
-    first_share = jnp.sum(turned.swapaxes(0, 1).astype(F32) * qkv_share, axis=(0, 2))
-    qkv_share = (
-        qkv_share.reshape(n_g, share, heads, 3, HEAD)
-        .transpose(1, 3, 0, 2, 4)
-        .reshape(share, 3 * width)
-    )
-    down_share = jnp.sum(second[:, :, columns:].astype(F32), axis=0)
-    down_share = (
-        down_share.reshape(share, wide, width).transpose(1, 0, 2).reshape(wide * share, width)
-    )
-
     place = lax.axis_index(ALL) * share
     own_gain_one = lax.dynamic_slice_in_dim(gain_one, place, share)
     own_gain_two = lax.dynamic_slice_in_dim(gain_two, place, share)
-    first_share = first_share / own_gain_one
     second_share = second_share / own_gain_two
+    down_share, qkv_share, first_share = last_shares(
+        second, turned.swapaxes(0, 1), own_gain_one[:, None]
+    )
+    down_share = down_share.reshape(wide * share, width)
+    first_share = first_share[:, 0]
     return (
         mixed,
         input_grad,

time: 332 us -> 329 us (level)
  waiting for transfers between devices: 106 us -> 99.1 us
  starting transfers between devices: 62.3 us -> 66.7 us
    ppermute x39 -> x42, waiting for transfers between devices: 78.8 us -> 72.9 us  [shift(): return lax.ppermute(value, axis, [(i, (i + step) % n) for i in range(n)])]
    ppermute x39 -> x42, starting transfers between devices: 48.5 us -> 52.8 us  [shift(): return lax.ppermute(value, axis, [(i, (i + step) % n) for i in range(n)])]
  transfers between devices with their start and end apart: 44 -> 47, of which waited for: 16 -> 16; matrix products, arithmetic and copies ran while one was open for 11% -> 11% of each run, Pallas kernels for 28% -> 28%
where the time goes in v2:
time: 329 us; the launch traced here: 324 us
  waiting for transfers between devices  99.1 us (30%)
  Pallas kernels  93.7 us (28%)
  starting transfers between devices  66.7 us (20%)
  local copies, waits for them, and re-layouts  25.4 us (8%)
  other arithmetic  23.9 us (7%)
  between operations  15.5 us (5%)
    ppermute x42, waiting for transfers between devices, shift(): return lax.ppermute(value, axis, [(i, (i + step) % n) for i in range(n)])  72.9 us
    ppermute x42, starting transfers between devices, shift(): return lax.ppermute(value, axis, [(i, (i + step) % n) for i in range(n)])  52.8 us
    pallas_call x3, Pallas kernels, attention_backward(): pl.pallas_call(functools.partial(attention_backward_kernel, rows, n_own),...  31.1 us
    pallas_call x1, Pallas kernels, middle(): pl.pallas_call(functools.partial(middle_kernel, (n_g, wide, width, rows,...  22.7 us
    all_to_all x1, waiting for transfers between devices, on_device(): parts = lax.all_to_all(parts, 'g', 0, 0)  21.3 us
    pallas_call x1, Pallas kernels, attention_forward(): pl.pallas_call(functools.partial(attention_forward_kernel, n_own), grid=(...  19.7 us
    add x4, other arithmetic, add_high(): total = total + term.astype(F32)  6.78 us
    convert_element_type x3, other arithmetic, add_low(): return add_high(*terms).astype(BF16)  6.76 us
  transfers between devices with their start and end apart: 47, of which 16 were waited for; matrix products, arithmetic and copies ran while one was open for 11% of the time, Pallas kernels for 28%

profile of v2, /device:TPU:0, one launch (start us, length us, event | category | flops | bytes accessed | tf_op | source)
XLA Modules:
  0.0 324.3 jit_solution(16359592025180520236)
XLA Ops:
  10.6 1.3 reshape.91
  13.5 5.1 %collective-permute-start = (bf16[320,768]{1,0:T(8,128)(2,1)S(1)}, bf16[320,768]{1,0:T(8,128)(2,1)S(1)}, u32[]{:S(2)}, u32[]{:S(2)}) collective-permute-start(bf16[320,768]{1,0:T(8,128)(2,1)S(1)} %fusion.6.refs_0_), channel_id=1, source_target_pairs={{0,6},{2,0},{4,2},{6,4},{1,7},{3,1},{5,3},{7,5},{8,14},{10,8},{12,... | collective-permute-start | bytes 1474568 | tf_op jit(solution)/shard_map/ppermute | solution.py:583
  18.6 1.5 collective-permute-start.2
  21.3 5.1 %all-to-all-start = ((bf16[4,24,576]{2,1,0:T(8,128)(2,1)}), bf16[4,24,576]{2,1,0:T(8,128)(2,1)S(1)}, u32[]{:S(2)}, u32[]{:S(2)}) async-start(bf16[4,24,576]{2,1,0:T(8,128)(2,1)} %reshape.88), calls=%async_computation | async-start | bytes 245760 | tf_op jit(solution)/shard_map/all_to_all | solution.py:660
  27.6 21.3 %all-to-all-done = bf16[4,24,576]{2,1,0:T(8,128)(2,1)S(1)} async-done(((bf16[4,24,576]{2,1,0:T(8,128)(2,1)}), bf16[4,24,576]{2,1,0:T(8,128)(2,1)S(1)}, u32[]{:S(2)}, u32[]{:S(2)}) %all-to-all-start) | async-done | bytes 110624 | tf_op jit(solution)/shard_map/all_to_all | solution.py:660
  49.0 1.6 collective-permute-start.7
  50.6 4.9 %collective-permute-done.7 = bf16[4,24,576]{2,1,0:T(8,128)(2,1)S(1)} collective-permute-done((bf16[4,24,576]{2,1,0:T(8,128)(2,1)S(1)}, bf16[4,24,576]{2,1,0:T(8,128)(2,1)S(1)}, u32[]{:S(2)}, u32[]{:S(2)}) %collective-permute-start.7) | collective-permute-done | bytes 110624 | tf_op jit(solution)/shard_map/ppermute | solution.py:583
  55.7 4.1 %collective-permute-start.3 = (bf16[320,768]{1,0:T(8,128)(2,1)S(1)}, bf16[320,768]{1,0:T(8,128)(2,1)}, u32[]{:S(2)}, u32[]{:S(2)}) collective-permute-start(bf16[320,768]{1,0:T(8,128)(2,1)S(1)} %collective-permute-done.refs_1_), channel_id=1, source_target_pairs={{0,6},{2,0},{4,2},{6,4},{1,7},{3,1},{5,3},{7,5},{8,14},{10,8},{12,... | collective-permute-start | bytes 1474568 | tf_op jit(solution)/shard_map/ppermute | solution.py:583
  59.9 1.5 collective-permute-start.9
  61.4 2.5 collective-permute-start.4
  64.0 14.8 %collective-permute-done.3.refs_2_ = bf16[320,768]{1,0:T(8,128)(2,1)} collective-permute-done((bf16[320,768]{1,0:T(8,128)(2,1)S(1)}, bf16[320,768]{1,0:T(8,128)(2,1)}, u32[]{:S(2)}, u32[]{:S(2)}) %collective-permute-start.3) | collective-permute-done | bytes 491552 | tf_op jit(solution)/shard_map/ppermute | solution.py:583
  78.8 1.5 collective-permute-start.5
  81.8 1.2 maximum_bitcast_fusion
  83.0 1.2 copy.22
  84.3 2.6 collective-permute-done.6.refs_7_
  86.9 20.1 %collective-permute-done.5.refs_6_ = bf16[320,768]{1,0:T(8,128)(2,1)} collective-permute-done((bf16[320,768]{1,0:T(8,128)(2,1)}, bf16[320,768]{1,0:T(8,128)(2,1)}, u32[]{:S(2)}, u32[]{:S(2)}) %collective-permute-start.5) | collective-permute-done | bytes 491552 | tf_op jit(solution)/shard_map/ppermute | solution.py:583
  107.0 19.7 %attention_forward.1 = (bf16[4,3,160,128]{3,2,1,0:T(8,128)(2,1)}, bf16[3,1280,128]{2,1,0:T(8,128)(2,1)}, bf16[3,2560,128]{2,1,0:T(8,128)(2,1)}, bf16[3,2560,128]{2,1,0:T(8,128)(2,1)}) custom-call(s32[1]{0:T(128)S(6)} %copy.44.live_ref, bf16[320,768]{1,0:T(8,128)(2,1)} %copy-done.1, bf16[320,768]{1,0:T(8,128)(2,1)} %copy-done.2, ...), custom_call_target="tpu_custom_call" | custom-call | tf_op jit(solution)/shard_map/attention_forward/pallas_call | solution.py:110
  126.6 1.8 slice_bitcast_fusion
  128.4 4.3 %collective-permute-start.12 = (bf16[3,160,128]{2,1,0:T(8,128)(2,1)S(1)}, bf16[3,160,128]{2,1,0:T(8,128)(2,1)S(1)}, u32[]{:S(2)}, u32[]{:S(2)}) collective-permute-start(bf16[3,160,128]{2,1,0:T(8,128)(2,1)S(1)} %get-tuple-element.160), channel_id=1, source_target_pairs={{0,6},{2,0},{4,2},{6,4},{1,7},{3,1},{5,3},{7,5},{8,14},{10,8},{12,... | collective-permute-start | bytes 368648 | tf_op jit(solution)/shard_map/ppermute | solution.py:583
  133.9 1.3 collective-permute-done.10.refs_4_
  135.2 2.7 collective-permute-done.11.refs_5_
  138.6 22.7 %middle.1 = (bf16[320,768]{1,0:T(8,128)(2,1)}, f32[320,768]{1,0:T(8,128)}, bf16[160,128]{1,0:T(8,128)(2,1)}, bf16[160,128]{1,0:T(8,128)(2,1)}, bf16[160,128]{1,0...) custom-call(s32[4]{0:T(128)} %pad_add_fusion.scalar_ref, ...), custom_call_target="tpu_custom_call" | custom-call | tf_op jit(solution)/shard_map/middle/pallas_call | solution.py:394
  161.3 2.5 collective-permute-start.13
  164.7 1.8 collective-permute-done.13.refs_1_
  166.5 4.5 %collective-permute-done.14.refs_2_ = bf16[160,128]{1,0:T(8,128)(2,1)S(1)} collective-permute-done((bf16[160,128]{1,0:T(8,128)(2,1)}, bf16[160,128]{1,0:T(8,128)(2,1)S(1)}, u32[]{:S(2)}, u32[]{:S(2)}) %collective-permute-start.14) | collective-permute-done | bytes 40992 | tf_op jit(solution)/shard_map/ppermute | solution.py:583
  171.1 1.5 collective-permute-start.18
  172.6 2.3 collective-permute-start.17
  175.0 10.3 %attention_backward.3 = (f32[4,320,128]{2,1,0:T(8,128)}, bf16[4,320,128]{2,1,0:T(8,128)(2,1)}, bf16[4,160,128]{2,1,0:T(8,128)(2,1)}) custom-call(bf16[4,3,160,128]{3,2,1,0:T(8,128)(2,1)} %get-tuple-element.87.out_ref, bf16[3,1280,128]{2,1,0:T(8,128)(2,1)} %get-tuple-element.91.query_ref, bf16[3,2560,128]{2,1,0:T(8,128)(2,1)} %get-tuple-element.92.key_ref, ...), custom_call_target="tpu_custom_call" | custom-call | tf_op jit(solution)/shard_map/attention_backward/pallas_call | solution.py:204
  187.0 1.8 add_convert_fusion
  189.6 1.9 collective-permute-start.21
  191.5 2.7 add_convert_fusion.1
  194.3 10.6 %attention_backward.4 = (f32[4,320,128]{2,1,0:T(8,128)}, bf16[4,320,128]{2,1,0:T(8,128)(2,1)}, bf16[4,160,128]{2,1,0:T(8,128)(2,1)}) custom-call(bf16[4,3,160,128]{3,2,1,0:T(8,128)(2,1)} %get-tuple-element.87.out_ref, bf16[3,1280,128]{2,1,0:T(8,128)(2,1)} %get-tuple-element.91.query_ref, bf16[3,2560,128]{2,1,0:T(8,128)(2,1)} %get-tuple-element.92.key_ref, ...), custom_call_target="tpu_custom_call" | custom-call | tf_op jit(solution)/shard_map/attention_backward/pallas_call | solution.py:204
  205.8 2.1 combine.3
  207.9 2.6 collective-permute-start.22
  210.5 2.4 collective-permute-start.24
  212.8 10.2 %attention_backward.5 = (f32[4,320,128]{2,1,0:T(8,128)}, bf16[4,320,128]{2,1,0:T(8,128)(2,1)}, bf16[4,160,128]{2,1,0:T(8,128)(2,1)}) custom-call(bf16[4,3,160,128]{3,2,1,0:T(8,128)(2,1)} %get-tuple-element.87.out_ref, bf16[3,1280,128]{2,1,0:T(8,128)(2,1)} %get-tuple-element.91.query_ref, bf16[3,2560,128]{2,1,0:T(8,128)(2,1)} %get-tuple-element.92.key_ref, ...), custom_call_target="tpu_custom_call" | custom-call | tf_op jit(solution)/shard_map/attention_backward/pallas_call | solution.py:204
  224.3 1.6 collective-permute-start.28
  226.0 2.1 combine.4
  229.2 2.7 convert_add_fusion
  234.1 1.6 collective-permute-start.38
  235.7 1.9 collective-permute-start.36
  237.6 2.4 collective-permute-start.31
  240.0 1.5 collective-permute-start.33
  241.5 4.4 %collective-permute-done.29.refs_4_ = bf16[480,128]{1,0:T(8,128)(2,1)S(1)} collective-permute-done((bf16[480,128]{1,0:T(8,128)(2,1)}, bf16[480,128]{1,0:T(8,128)(2,1)S(1)}, u32[]{:S(2)}, u32[]{:S(2)}) %collective-permute-start.29) | collective-permute-done | bytes 122912 | tf_op jit(solution)/shard_map/ppermute | solution.py:583
  245.9 2.9 collective-permute-done.31.refs_7_
  248.8 2.1 combine.5
  250.9 2.2 collective-permute-start.30
  253.1 1.7 collective-permute-start.32
  255.4 5.6 %group_grad.1 = (f32[2,192,576]{2,1,0:T(8,128)}, bf16[2,192,576]{2,1,0:T(8,128)(2,1)}) custom-call(s32[4]{0:T(128)} %pad_add_fusion.scalar_ref, bf16[320,768]{1,0:T(8,128)(2,1)} %copy-done.1, bf16[320,768]{1,0:T(8,128)(2,1)} %copy-done.2, bf16[320,768]{1,0:T(8,128)(2,1)} %collective-permute-done.3.refs_2_, bf16[320,768]{1,0:T(8,128)(2,1)} %copy-done.3, ...), custom_call_target="tpu_custom_call" | custom-call | tf_op jit(solution)/shard_map/group_grad/pallas_call | solution.py:478
  261.0 2.2 fusion
  263.2 4.5 %all-to-all-start.1 = ((bf16[4,24,3840]{2,1,0:T(8,128)(2,1)}), bf16[4,24,3840]{2,1,0:T(8,128)(2,1)}, u32[]{:S(2)}, u32[]{:S(2)}) async-start(bf16[4,24,3840]{2,1,0:T(8,128)(2,1)} %fusion), calls=%async_computation.1 | async-start | bytes 1474560 | tf_op jit(solution)/shard_map/all_to_all | solution.py:761
  267.9 2.2 convert_add_fusion.1
  272.6 8.4 %collective-permute-done.40 = bf16[4,2,24,576]{3,2,0,1:T(8,128)(2,1)} collective-permute-done((bf16[4,2,24,576]{3,2,0,1:T(8,128)(2,1)}, bf16[4,2,24,576]{3,2,0,1:T(8,128)(2,1)}, u32[]{:S(2)}, u32[]{:S(2)}) %collective-permute-start.40) | collective-permute-done | bytes 221216 | tf_op jit(solution)/shard_map/ppermute | solution.py:583
  281.0 1.8 bitcast_add_fusion.2
  282.7 3.1 all-to-all-done.1
  288.4 3.2 %collective-permute-done.41 = bf16[4,24,576]{2,1,0:T(8,128)(2,1)S(1)} collective-permute-done((bf16[4,24,576]{2,1,0:T(8,128)(2,1)S(1)}, bf16[4,24,576]{2,1,0:T(8,128)(2,1)S(1)}, u32[]{:S(2)}, u32[]{:S(2)}) %collective-permute-start.41) | collective-permute-done | bytes 110624 | tf_op jit(solution)/shard_map/ppermute | solution.py:583
  292.6 4.2 %all-to-all-start.2 = ((bf16[4,24,3648]{2,1,0:T(8,128)(2,1)}), bf16[4,24,3648]{2,1,0:T(8,128)(2,1)}, u32[]{:S(2)}, u32[]{:S(2)}) async-start(bf16[4,24,3648]{2,1,0:T(8,128)(2,1)} %pad_maximum_fusion), calls=%async_computation.2 | async-start | bytes 1425408 | tf_op jit(solution)/shard_map/all_to_all | solution.py:766
  298.2 6.3 %input_gradient.1 = f32[320,768]{1,0:T(8,128)} custom-call(s32[4]{0:T(128)} %pad_add_fusion.scalar_ref, bf16[320,768]{1,0:T(8,128)(2,1)} %token_ref.1, f32[320,768]{1,0:T(8,128)} %get-tuple-element.89.resid_ref, f32[1,768]{1,0:T(1,128)} %broadcast_in_dim.13.gain_ref, bf16[768,2560]{1,0:T(8,128)(2,1)} %all-gather.5.cloned.1.call-done.weight_ref, ...), custom_call_target="tpu_custom_call" | custom-call | tf_op jit(solution)/shard_map/input_gradient/pallas_call | solution.py:522
  304.5 1.3 convert_reduce_fusion
  307.6 1.2 copy.30
  308.9 2.6 reshape.98
  312.0 1.7 all-to-all-done.2.got_ref
  313.8 2.2 last_shares.1
  315.9 1.3 reduce
  (179 shorter events, 30.0 us)
Async XLA Ops:
  7.2 130.7 %all-gather.3.cloned.1.call-start = ((), (), s32[]{:S(2)}) async-start(), calls=%async_computation.3 | async-start | bytes 10948608 | tf_op jit(solution)/shard_map/all_gather | solution.py:678
  11.9 8.2 %copy-start.21 = (f32[24,2304]{1,0:T(8,128)S(1)}, f32[24,2304]{1,0:T(8,128)}, u32[]{:S(2)}) copy-start(f32[24,2304]{1,0:T(8,128)} %param.12) | copy-start | bytes 663556
  13.5 13.3 %copy-start.1 = (bf16[320,768]{1,0:T(8,128)(2,1)}, bf16[320,768]{1,0:T(8,128)(2,1)S(1)}, u32[]{:S(2)}) copy-start(bf16[320,768]{1,0:T(8,128)(2,1)S(1)} %fusion.6.refs_0_) | copy-start | bytes 1474564
  13.5 35.4 %collective-permute-start = (bf16[320,768]{1,0:T(8,128)(2,1)S(1)}, bf16[320,768]{1,0:T(8,128)(2,1)S(1)}, u32[]{:S(2)}, u32[]{:S(2)}) collective-permute-start(bf16[320,768]{1,0:T(8,128)(2,1)S(1)} %fusion.6.refs_0_), channel_id=1, source_target_pairs={{0,6},{2,0},{4,2},{6,4},{1,7},{3,1},{5,3},{7,5},{8,14},{10,8},{12,... | collective-permute-start | bytes 1474568 | tf_op jit(solution)/shard_map/ppermute | solution.py:583
  18.6 30.4 %collective-permute-start.1 = (bf16[320,768]{1,0:T(8,128)(2,1)S(1)}, bf16[320,768]{1,0:T(8,128)(2,1)S(1)}, u32[]{:S(2)}, u32[]{:S(2)}) collective-permute-start(bf16[320,768]{1,0:T(8,128)(2,1)S(1)} %fusion.6.refs_0_), channel_id=1, source_target_pairs={{0,2},{2,4},{4,6},{6,0},{1,3},{3,5},{5,7},{7,1},{8,10},{10,12},{12... | collective-permute-start | bytes 1474568 | tf_op jit(solution)/shard_map/ppermute | solution.py:583
  18.6 30.4 %collective-permute-start.2 = (bf16[320,768]{1,0:T(8,128)(2,1)S(1)}, bf16[320,768]{1,0:T(8,128)(2,1)S(1)}, u32[]{:S(2)}, u32[]{:S(2)}) collective-permute-start(bf16[320,768]{1,0:T(8,128)(2,1)S(1)} %fusion.6.refs_0_), channel_id=1, source_target_pairs={{0,1},{1,0},{2,3},{3,2},{4,5},{5,4},{6,7},{7,6},{8,9},{9,8},{10,11... | collective-permute-start | bytes 1474568 | tf_op jit(solution)/shard_map/ppermute | solution.py:583
  21.3 27.6 %all-to-all-start = ((bf16[4,24,576]{2,1,0:T(8,128)(2,1)}), bf16[4,24,576]{2,1,0:T(8,128)(2,1)S(1)}, u32[]{:S(2)}, u32[]{:S(2)}) async-start(bf16[4,24,576]{2,1,0:T(8,128)(2,1)} %reshape.88), calls=%async_computation | async-start | bytes 245760 | tf_op jit(solution)/shard_map/all_to_all | solution.py:660
  26.4 186.4 %all-gather.5.cloned.1.call-start = ((), (), s32[]{:S(2)}) async-start(), calls=%async_computation.4 | async-start | bytes 4055040 | tf_op jit(solution)/shard_map/all_gather | solution.py:702
  26.8 33.1 %copy-start.12 = (bf16[24,4,576]{2,0,1:T(8,128)(2,1)}, bf16[24,4,576]{2,0,1:T(8,128)(2,1)S(1)}, u32[]{:S(2)}) copy-start(bf16[24,4,576]{2,0,1:T(8,128)(2,1)S(1)} %reshape.92) | copy-start | bytes 331780
  48.9 12.5 %copy-start.2 = (bf16[320,768]{1,0:T(8,128)(2,1)}, bf16[320,768]{1,0:T(8,128)(2,1)S(1)}, u32[]{:S(2)}) copy-start(bf16[320,768]{1,0:T(8,128)(2,1)S(1)} %collective-permute-done.refs_1_) | copy-start | bytes 1474564
  48.9 15.0 %copy-start.3 = (bf16[320,768]{1,0:T(8,128)(2,1)}, bf16[320,768]{1,0:T(8,128)(2,1)S(1)}, u32[]{:S(2)}) copy-start(bf16[320,768]{1,0:T(8,128)(2,1)S(1)} %collective-permute-done.1.refs_3_) | copy-start | bytes 1474564
  49.0 10.8 %copy-start.14 = (bf16[320,768]{1,0:T(8,128)(2,1)}, bf16[320,768]{1,0:T(8,128)(2,1)S(1)}, u32[]{:S(2)}) copy-start(bf16[320,768]{1,0:T(8,128)(2,1)S(1)} %collective-permute-done.2.refs_4_) | copy-start | bytes 1474564
  49.0 6.5 %collective-permute-start.7 = (bf16[4,24,576]{2,1,0:T(8,128)(2,1)S(1)}, bf16[4,24,576]{2,1,0:T(8,128)(2,1)S(1)}, u32[]{:S(2)}, u32[]{:S(2)}) collective-permute-start(bf16[4,24,576]{2,1,0:T(8,128)(2,1)S(1)} %all-to-all-done), channel_id=1, source_target_pairs={{0,1},{1,0},{2,3},{3,2},{4,5},{5,4},{6,7},{7,6},{8,9},{9,8},{10,11... | collective-permute-start | bytes 331784 | tf_op jit(solution)/shard_map/ppermute | solution.py:583
  55.6 4.2 %collective-permute-start.8 = (bf16[2,4,24,576]{3,2,1,0:T(8,128)(2,1)S(1)}, bf16[2,4,24,576]{3,2,1,0:T(8,128)(2,1)S(1)}, u32[]{:S(2)}, u32[]{:S(2)}) collective-permute-start(bf16[2,4,24,576]{3,2,1,0:T(8,128)(2,1)S(1)} %pad_maximum_fusion.2), channel_id=1, source_target_pairs={{0,8},{8,0},{1,9},{9,1},{2,10},{10,2},{3,11},{11,3},{4,12},{12,4},... | collective-permute-start | bytes 663560 | tf_op jit(solution)/shard_map/ppermute | solution.py:583
  55.7 23.2 %collective-permute-start.3 = (bf16[320,768]{1,0:T(8,128)(2,1)S(1)}, bf16[320,768]{1,0:T(8,128)(2,1)}, u32[]{:S(2)}, u32[]{:S(2)}) collective-permute-start(bf16[320,768]{1,0:T(8,128)(2,1)S(1)} %collective-permute-done.refs_1_), channel_id=1, source_target_pairs={{0,6},{2,0},{4,2},{6,4},{1,7},{3,1},{5,3},{7,5},{8,14},{10,8},{12,... | collective-permute-start | bytes 1474568 | tf_op jit(solution)/shard_map/ppermute | solution.py:583
  59.9 21.0 %collective-permute-start.9 = (bf16[2,2,4,24,576]{4,3,2,1,0:T(8,128)(2,1)S(1)}, bf16[2,2,4,24,576]{4,3,2,1,0:T(8,128)(2,1)S(1)}, u32[]{:S(2)}, u32[]{:S(2)}) collective-permute-start(bf16[2,2,4,24,576]{4,3,2,1,0:T(8,128)(2,1)S(1)} %pad_maximum_fusion.1), channel_id=1, source_target_pairs={{0,16},{16,0},{1,17},{17,1},{2,18},{18,2},{3,19},{19,3},{4,20},{20... | collective-permute-start | bytes 1327112 | tf_op jit(solution)/shard_map/ppermute | solution.py:583
  61.4 22.8 %collective-permute-start.4 = (bf16[320,768]{1,0:T(8,128)(2,1)S(1)}, bf16[320,768]{1,0:T(8,128)(2,1)}, u32[]{:S(2)}, u32[]{:S(2)}) collective-permute-start(bf16[320,768]{1,0:T(8,128)(2,1)S(1)} %collective-permute-done.refs_1_), channel_id=1, source_target_pairs={{0,1},{1,0},{2,3},{3,2},{4,5},{5,4},{6,7},{7,6},{8,9},{9,8},{10,11... | collective-permute-start | bytes 1474568 | tf_op jit(solution)/shard_map/ppermute | solution.py:583
  63.9 23.0 %collective-permute-start.6 = (bf16[320,768]{1,0:T(8,128)(2,1)S(1)}, bf16[320,768]{1,0:T(8,128)(2,1)}, u32[]{:S(2)}, u32[]{:S(2)}) collective-permute-start(bf16[320,768]{1,0:T(8,128)(2,1)S(1)} %collective-permute-done.1.refs_3_), channel_id=1, source_target_pairs={{0,1},{1,0},{2,3},{3,2},{4,5},{5,4},{6,7},{7,6},{8,9},{9,8},{10,11... | collective-permute-start | bytes 1474568 | tf_op jit(solution)/shard_map/ppermute | solution.py:583
  78.8 28.1 %collective-permute-start.5 = (bf16[320,768]{1,0:T(8,128)(2,1)}, bf16[320,768]{1,0:T(8,128)(2,1)}, u32[]{:S(2)}, u32[]{:S(2)}) collective-permute-start(bf16[320,768]{1,0:T(8,128)(2,1)} %collective-permute-done.3.refs_2_), channel_id=1, source_target_pairs={{0,1},{1,0},{2,3},{3,2},{4,5},{5,4},{6,7},{7,6},{8,9},{9,8},{10,11... | collective-permute-start | bytes 1474568 | tf_op jit(solution)/shard_map/ppermute | solution.py:583
  107.0 25.8 %copy-start.35 = (f32[768]{0:T(1024)S(1)}, f32[768]{0:T(1024)}, u32[]{:S(2)}) copy-start(f32[768]{0:T(1024)} %param.17) | copy-start | bytes 9220
  128.4 6.8 %collective-permute-start.10 = (bf16[3,160,128]{2,1,0:T(8,128)(2,1)S(1)}, bf16[3,160,128]{2,1,0:T(8,128)(2,1)S(1)}, u32[]{:S(2)}, u32[]{:S(2)}) collective-permute-start(bf16[3,160,128]{2,1,0:T(8,128)(2,1)S(1)} %get-tuple-element.162), channel_id=1, source_target_pairs={{0,2},{2,4},{4,6},{6,0},{1,3},{3,5},{5,7},{7,1},{8,10},{10,12},{12... | collective-permute-start | bytes 368648 | tf_op jit(solution)/shard_map/ppermute | solution.py:583
  128.4 9.5 %collective-permute-start.11 = (bf16[3,160,128]{2,1,0:T(8,128)(2,1)S(1)}, bf16[3,160,128]{2,1,0:T(8,128)(2,1)S(1)}, u32[]{:S(2)}, u32[]{:S(2)}) collective-permute-start(bf16[3,160,128]{2,1,0:T(8,128)(2,1)S(1)} %get-tuple-element.161), channel_id=1, source_target_pairs={{0,4},{2,6},{4,0},{6,2},{1,5},{3,7},{5,1},{7,3},{8,12},{10,14},{12... | collective-permute-start | bytes 368648 | tf_op jit(solution)/shard_map/ppermute | solution.py:583
  128.4 9.5 %collective-permute-start.12 = (bf16[3,160,128]{2,1,0:T(8,128)(2,1)S(1)}, bf16[3,160,128]{2,1,0:T(8,128)(2,1)S(1)}, u32[]{:S(2)}, u32[]{:S(2)}) collective-permute-start(bf16[3,160,128]{2,1,0:T(8,128)(2,1)S(1)} %get-tuple-element.160), channel_id=1, source_target_pairs={{0,6},{2,0},{4,2},{6,4},{1,7},{3,1},{5,3},{7,5},{8,14},{10,8},{12,... | collective-permute-start | bytes 368648 | tf_op jit(solution)/shard_map/ppermute | solution.py:583
  161.2 24.6 %collective-permute-start.16 = (bf16[192,3840]{1,0:T(8,128)(2,1)}, bf16[192,3840]{1,0:T(8,128)(2,1)S(1)}, u32[]{:S(2)}, u32[]{:S(2)}) collective-permute-start(bf16[192,3840]{1,0:T(8,128)(2,1)} %get-tuple-element.102), channel_id=1, source_target_pairs={{0,8},{8,0},{1,9},{9,1},{2,10},{10,2},{3,11},{11,3},{4,12},{12,4},... | collective-permute-start | bytes 4423688 | tf_op jit(solution)/shard_map/ppermute | solution.py:583
  161.3 5.2 %collective-permute-start.13 = (bf16[160,128]{1,0:T(8,128)(2,1)}, bf16[160,128]{1,0:T(8,128)(2,1)S(1)}, u32[]{:S(2)}, u32[]{:S(2)}) collective-permute-start(bf16[160,128]{1,0:T(8,128)(2,1)} %get-tuple-element.95), channel_id=1, source_target_pairs={{0,6},{2,0},{4,2},{6,4},{1,7},{3,1},{5,3},{7,5},{8,14},{10,8},{12,... | collective-permute-start | bytes 122888 | tf_op jit(solution)/shard_map/ppermute | solution.py:583
  163.9 7.2 %collective-permute-start.14 = (bf16[160,128]{1,0:T(8,128)(2,1)}, bf16[160,128]{1,0:T(8,128)(2,1)S(1)}, u32[]{:S(2)}, u32[]{:S(2)}) collective-permute-start(bf16[160,128]{1,0:T(8,128)(2,1)} %get-tuple-element.96), channel_id=1, source_target_pairs={{0,4},{2,6},{4,0},{6,2},{1,5},{3,7},{5,1},{7,3},{8,12},{10,14},{12... | collective-permute-start | bytes 122888 | tf_op jit(solution)/shard_map/ppermute | solution.py:583
  164.7 6.4 %collective-permute-start.15 = (bf16[160,128]{1,0:T(8,128)(2,1)}, bf16[160,128]{1,0:T(8,128)(2,1)S(1)}, u32[]{:S(2)}, u32[]{:S(2)}) collective-permute-start(bf16[160,128]{1,0:T(8,128)(2,1)} %get-tuple-element.97), channel_id=1, source_target_pairs={{0,2},{2,4},{4,6},{6,0},{1,3},{3,5},{5,7},{7,1},{8,10},{10,12},{12... | collective-permute-start | bytes 122888 | tf_op jit(solution)/shard_map/ppermute | solution.py:583
  166.5 8.4 %copy-start.31 = (bf16[160,128]{1,0:T(8,128)(2,1)}, bf16[160,128]{1,0:T(8,128)(2,1)S(1)}, u32[]{:S(2)}) copy-start(bf16[160,128]{1,0:T(8,128)(2,1)S(1)} %collective-permute-done.13.refs_1_) | copy-start | bytes 122884
  171.1 14.2 %collective-permute-start.19 = (bf16[2,160,128]{2,1,0:T(8,128)(2,1)}, bf16[2,160,128]{2,1,0:T(8,128)(2,1)S(1)}, u32[]{:S(2)}, u32[]{:S(2)}) collective-permute-start(bf16[2,160,128]{2,1,0:T(8,128)(2,1)} %get-tuple-element.108), channel_id=1, source_target_pairs={{0,2},{2,4},{4,6},{6,0},{1,3},{3,5},{5,7},{7,1},{8,10},{10,12},{12... | collective-permute-start | bytes 245768 | tf_op jit(solution)/shard_map/ppermute | solution.py:583
  171.1 14.7 %collective-permute-start.18 = (bf16[2,160,128]{2,1,0:T(8,128)(2,1)}, bf16[2,160,128]{2,1,0:T(8,128)(2,1)S(1)}, u32[]{:S(2)}, u32[]{:S(2)}) collective-permute-start(bf16[2,160,128]{2,1,0:T(8,128)(2,1)} %get-tuple-element.106), channel_id=1, source_target_pairs={{0,4},{2,6},{4,0},{6,2},{1,5},{3,7},{5,1},{7,3},{8,12},{10,14},{12... | collective-permute-start | bytes 245768 | tf_op jit(solution)/shard_map/ppermute | solution.py:583
  172.6 13.2 %collective-permute-start.17 = (bf16[2,160,128]{2,1,0:T(8,128)(2,1)}, bf16[2,160,128]{2,1,0:T(8,128)(2,1)S(1)}, u32[]{:S(2)}, u32[]{:S(2)}) collective-permute-start(bf16[2,160,128]{2,1,0:T(8,128)(2,1)} %get-tuple-element.104), channel_id=1, source_target_pairs={{0,6},{2,0},{4,2},{6,4},{1,7},{3,1},{5,3},{7,5},{8,14},{10,8},{12,... | collective-permute-start | bytes 245768 | tf_op jit(solution)/shard_map/ppermute | solution.py:583
  174.9 16.6 %collective-permute-start.20 = (bf16[192,3072]{1,0:T(8,128)(2,1)}, bf16[192,3072]{1,0:T(8,128)(2,1)}, u32[]{:S(2)}, u32[]{:S(2)}) collective-permute-start(bf16[192,3072]{1,0:T(8,128)(2,1)} %get-tuple-element.111), channel_id=1, source_target_pairs={{0,8},{8,0},{1,9},{9,1},{2,10},{10,2},{3,11},{11,3},{4,12},{12,4},... | collective-permute-start | bytes 3538952 | tf_op jit(solution)/shard_map/ppermute | solution.py:583
  175.0 12.1 %copy-start.6 = (bf16[192,3840]{1,0:T(8,128)(2,1)S(1)}, bf16[192,3840]{1,0:T(8,128)(2,1)}, u32[]{:S(2)}) copy-start(bf16[192,3840]{1,0:T(8,128)(2,1)} %get-tuple-element.101) | copy-start | bytes 4423684
  185.3 9.0 %copy-start.18 = (bf16[2,160,128]{2,1,0:T(8,128)(2,1)}, bf16[2,160,128]{2,1,0:T(8,128)(2,1)S(1)}, u32[]{:S(2)}) copy-start(bf16[2,160,128]{2,1,0:T(8,128)(2,1)S(1)} %collective-permute-done.19.refs_3_) | copy-start | bytes 245764
  185.3 25.2 %collective-permute-start.26 = (bf16[192,3840]{1,0:T(8,128)(2,1)}, bf16[192,3840]{1,0:T(8,128)(2,1)}, u32[]{:S(2)}, u32[]{:S(2)}) collective-permute-start(bf16[192,3840]{1,0:T(8,128)(2,1)} %get-tuple-element.130), channel_id=1, source_target_pairs={{0,8},{8,0},{1,9},{9,1},{2,10},{10,2},{3,11},{11,3},{4,12},{12,4},... | collective-permute-start | bytes 4423688 | tf_op jit(solution)/shard_map/ppermute | solution.py:583
  185.8 8.4 %copy-start.19 = (bf16[2,160,128]{2,1,0:T(8,128)(2,1)}, bf16[2,160,128]{2,1,0:T(8,128)(2,1)S(1)}, u32[]{:S(2)}) copy-start(bf16[2,160,128]{2,1,0:T(8,128)(2,1)S(1)} %collective-permute-done.18.refs_2_) | copy-start | bytes 245764
  185.8 8.4 %copy-start.20 = (bf16[2,160,128]{2,1,0:T(8,128)(2,1)}, bf16[2,160,128]{2,1,0:T(8,128)(2,1)S(1)}, u32[]{:S(2)}) copy-start(bf16[2,160,128]{2,1,0:T(8,128)(2,1)S(1)} %collective-permute-done.17.refs_1_) | copy-start | bytes 245764
  188.9 39.2 %collective-permute-start.27 = (bf16[192,3840]{1,0:T(8,128)(2,1)S(1)}, bf16[192,3840]{1,0:T(8,128)(2,1)S(1)}, u32[]{:S(2)}, u32[]{:S(2)}) collective-permute-start(bf16[192,3840]{1,0:T(8,128)(2,1)S(1)} %add_convert_fusion), channel_id=1, source_target_pairs={{0,16},{16,0},{1,17},{17,1},{2,18},{18,2},{3,19},{19,3},{4,20},{20... | collective-permute-start | bytes 4423688 | tf_op jit(solution)/shard_map/ppermute | solution.py:583
  189.6 15.5 %collective-permute-start.21 = (bf16[4,320,128]{2,1,0:T(8,128)(2,1)S(1)}, bf16[4,320,128]{2,1,0:T(8,128)(2,1)S(1)}, u32[]{:S(2)}, u32[]{:S(2)}) collective-permute-start(bf16[4,320,128]{2,1,0:T(8,128)(2,1)S(1)} %copy-done.36), channel_id=1, source_target_pairs={{0,1},{1,0},{2,3},{3,2},{4,5},{5,4},{6,7},{7,6},{8,9},{9,8},{10,11... | collective-permute-start | bytes 983048 | tf_op jit(solution)/shard_map/ppermute | solution.py:583
  204.9 21.1 %collective-permute-start.25 = (bf16[4,320,128]{2,1,0:T(8,128)(2,1)}, bf16[4,320,128]{2,1,0:T(8,128)(2,1)}, u32[]{:S(2)}, u32[]{:S(2)}) collective-permute-start(bf16[4,320,128]{2,1,0:T(8,128)(2,1)} %get-tuple-element.127), channel_id=1, source_target_pairs={{0,1},{1,0},{2,3},{3,2},{4,5},{5,4},{6,7},{7,6},{8,9},{9,8},{10,11... | collective-permute-start | bytes 983048 | tf_op jit(solution)/shard_map/ppermute | solution.py:583
  207.9 15.1 %collective-permute-start.22 = (bf16[480,128]{1,0:T(8,128)(2,1)}, bf16[480,128]{1,0:T(8,128)(2,1)S(1)}, u32[]{:S(2)}, u32[]{:S(2)}) collective-permute-start(bf16[480,128]{1,0:T(8,128)(2,1)} %get-tuple-element.119.refs_7_), channel_id=1, source_target_pairs={{0,2},{2,4},{4,6},{6,0},{1,3},{3,5},{5,7},{7,1},{8,10},{10,12},{12... | collective-permute-start | bytes 368648 | tf_op jit(solution)/shard_map/ppermute | solution.py:583
  210.5 12.6 %collective-permute-start.23 = (bf16[480,128]{1,0:T(8,128)(2,1)}, bf16[480,128]{1,0:T(8,128)(2,1)S(1)}, u32[]{:S(2)}, u32[]{:S(2)}) collective-permute-start(bf16[480,128]{1,0:T(8,128)(2,1)} %get-tuple-element.120.refs_10_), channel_id=1, source_target_pairs={{0,4},{2,6},{4,0},{6,2},{1,5},{3,7},{5,1},{7,3},{8,12},{10,14},{12... | collective-permute-start | bytes 368648 | tf_op jit(solution)/shard_map/ppermute | solution.py:583
  210.5 15.5 %collective-permute-start.24 = (bf16[480,128]{1,0:T(8,128)(2,1)}, bf16[480,128]{1,0:T(8,128)(2,1)S(1)}, u32[]{:S(2)}, u32[]{:S(2)}) collective-permute-start(bf16[480,128]{1,0:T(8,128)(2,1)} %get-tuple-element.121.refs_13_), channel_id=1, source_target_pairs={{0,6},{2,0},{4,2},{6,4},{1,7},{3,1},{5,3},{7,5},{8,14},{10,8},{12,... | collective-permute-start | bytes 368648 | tf_op jit(solution)/shard_map/ppermute | solution.py:583
  223.0 16.9 %collective-permute-start.35 = (bf16[192,3072]{1,0:T(8,128)(2,1)}, bf16[192,3072]{1,0:T(8,128)(2,1)}, u32[]{:S(2)}, u32[]{:S(2)}) collective-permute-start(bf16[192,3072]{1,0:T(8,128)(2,1)} %get-tuple-element.145), channel_id=1, source_target_pairs={{0,8},{8,0},{1,9},{9,1},{2,10},{10,2},{3,11},{11,3},{4,12},{12,4},... | collective-permute-start | bytes 3538952 | tf_op jit(solution)/shard_map/ppermute | solution.py:583
  224.3 9.8 %collective-permute-start.28 = (bf16[4,320,128]{2,1,0:T(8,128)(2,1)}, bf16[4,320,128]{2,1,0:T(8,128)(2,1)S(1)}, u32[]{:S(2)}, u32[]{:S(2)}) collective-permute-start(bf16[4,320,128]{2,1,0:T(8,128)(2,1)} %get-tuple-element.139), channel_id=1, source_target_pairs={{0,1},{1,0},{2,3},{3,2},{4,5},{5,4},{6,7},{7,6},{8,9},{9,8},{10,11... | collective-permute-start | bytes 983048 | tf_op jit(solution)/shard_map/ppermute | solution.py:583
  234.1 14.7 %copy-start.16 = (bf16[4,320,128]{2,1,0:T(8,128)(2,1)}, bf16[4,320,128]{2,1,0:T(8,128)(2,1)S(1)}, u32[]{:S(2)}) copy-start(bf16[4,320,128]{2,1,0:T(8,128)(2,1)S(1)} %collective-permute-done.28.refs_0_) | copy-start | bytes 983044
  234.1 26.9 %collective-permute-start.38 = (bf16[4,24,3840]{2,1,0:T(8,128)(2,1)}, bf16[4,24,3840]{2,1,0:T(8,128)(2,1)}, u32[]{:S(2)}, u32[]{:S(2)}) collective-permute-start(bf16[4,24,3840]{2,1,0:T(8,128)(2,1)} %fusion.7), channel_id=1, source_target_pairs={{0,1},{1,0},{2,3},{3,2},{4,5},{5,4},{6,7},{7,6},{8,9},{9,8},{10,11... | collective-permute-start | bytes 2211848 | tf_op jit(solution)/shard_map/ppermute | solution.py:583
  235.7 32.1 %collective-permute-start.36 = (bf16[192,3072]{1,0:T(8,128)(2,1)}, bf16[192,3072]{1,0:T(8,128)(2,1)}, u32[]{:S(2)}, u32[]{:S(2)}) collective-permute-start(bf16[192,3072]{1,0:T(8,128)(2,1)} %add_convert_fusion.1), channel_id=1, source_target_pairs={{0,16},{16,0},{1,17},{17,1},{2,18},{18,2},{3,19},{19,3},{4,20},{20... | collective-permute-start | bytes 3538952 | tf_op jit(solution)/shard_map/ppermute | solution.py:583
  237.6 8.3 %collective-permute-start.29 = (bf16[480,128]{1,0:T(8,128)(2,1)}, bf16[480,128]{1,0:T(8,128)(2,1)S(1)}, u32[]{:S(2)}, u32[]{:S(2)}) collective-permute-start(bf16[480,128]{1,0:T(8,128)(2,1)} %get-tuple-element.132.refs_8_), channel_id=1, source_target_pairs={{0,2},{2,4},{4,6},{6,0},{1,3},{3,5},{5,7},{7,1},{8,10},{10,12},{12... | collective-permute-start | bytes 368648 | tf_op jit(solution)/shard_map/ppermute | solution.py:583
  237.6 11.2 %collective-permute-start.31 = (bf16[480,128]{1,0:T(8,128)(2,1)}, bf16[480,128]{1,0:T(8,128)(2,1)S(1)}, u32[]{:S(2)}, u32[]{:S(2)}) collective-permute-start(bf16[480,128]{1,0:T(8,128)(2,1)} %get-tuple-element.133.refs_11_), channel_id=1, source_target_pairs={{0,4},{2,6},{4,0},{6,2},{1,5},{3,7},{5,1},{7,3},{8,12},{10,14},{12... | collective-permute-start | bytes 368648 | tf_op jit(solution)/shard_map/ppermute | solution.py:583
  240.0 8.8 %collective-permute-start.33 = (bf16[480,128]{1,0:T(8,128)(2,1)}, bf16[480,128]{1,0:T(8,128)(2,1)}, u32[]{:S(2)}, u32[]{:S(2)}) collective-permute-start(bf16[480,128]{1,0:T(8,128)(2,1)} %get-tuple-element.134.refs_14_), channel_id=1, source_target_pairs={{0,6},{2,0},{4,2},{6,4},{1,7},{3,1},{5,3},{7,5},{8,14},{10,8},{12,... | collective-permute-start | bytes 368648 | tf_op jit(solution)/shard_map/ppermute | solution.py:583
  245.9 15.1 %copy-start.25 = (bf16[480,128]{1,0:T(8,128)(2,1)}, bf16[480,128]{1,0:T(8,128)(2,1)S(1)}, u32[]{:S(2)}) copy-start(bf16[480,128]{1,0:T(8,128)(2,1)S(1)} %collective-permute-done.29.refs_4_) | copy-start | bytes 368644
  248.8 12.2 %copy-start.26 = (bf16[480,128]{1,0:T(8,128)(2,1)}, bf16[480,128]{1,0:T(8,128)(2,1)S(1)}, u32[]{:S(2)}) copy-start(bf16[480,128]{1,0:T(8,128)(2,1)S(1)} %collective-permute-done.31.refs_7_) | copy-start | bytes 368644
  250.9 16.9 %collective-permute-start.30 = (bf16[480,128]{1,0:T(8,128)(2,1)}, bf16[480,128]{1,0:T(8,128)(2,1)}, u32[]{:S(2)}, u32[]{:S(2)}) collective-permute-start(bf16[480,128]{1,0:T(8,128)(2,1)} %get-tuple-element.141.refs_9_), channel_id=1, source_target_pairs={{0,2},{2,4},{4,6},{6,0},{1,3},{3,5},{5,7},{7,1},{8,10},{10,12},{12... | collective-permute-start | bytes 368648 | tf_op jit(solution)/shard_map/ppermute | solution.py:583
  253.1 14.7 %collective-permute-start.32 = (bf16[480,128]{1,0:T(8,128)(2,1)}, bf16[480,128]{1,0:T(8,128)(2,1)}, u32[]{:S(2)}, u32[]{:S(2)}) collective-permute-start(bf16[480,128]{1,0:T(8,128)(2,1)} %get-tuple-element.142.refs_12_), channel_id=1, source_target_pairs={{0,4},{2,6},{4,0},{6,2},{1,5},{3,7},{5,1},{7,3},{8,12},{10,14},{12... | collective-permute-start | bytes 368648 | tf_op jit(solution)/shard_map/ppermute | solution.py:583
  254.7 13.0 %collective-permute-start.34 = (bf16[480,128]{1,0:T(8,128)(2,1)}, bf16[480,128]{1,0:T(8,128)(2,1)}, u32[]{:S(2)}, u32[]{:S(2)}) collective-permute-start(bf16[480,128]{1,0:T(8,128)(2,1)} %get-tuple-element.143.refs_15_), channel_id=1, source_target_pairs={{0,6},{2,0},{4,2},{6,4},{1,7},{3,1},{5,3},{7,5},{8,14},{10,8},{12,... | collective-permute-start | bytes 368648 | tf_op jit(solution)/shard_map/ppermute | solution.py:583
  263.2 22.6 %all-to-all-start.1 = ((bf16[4,24,3840]{2,1,0:T(8,128)(2,1)}), bf16[4,24,3840]{2,1,0:T(8,128)(2,1)}, u32[]{:S(2)}, u32[]{:S(2)}) async-start(bf16[4,24,3840]{2,1,0:T(8,128)(2,1)} %fusion), calls=%async_computation.1 | async-start | bytes 1474560 | tf_op jit(solution)/shard_map/all_to_all | solution.py:761
  267.8 3.6 %collective-permute-start.39 = (bf16[2,192,576]{2,1,0:T(8,128)(2,1)}, bf16[2,192,576]{2,1,0:T(8,128)(2,1)S(1)}, u32[]{:S(2)}, u32[]{:S(2)}) collective-permute-start(bf16[2,192,576]{2,1,0:T(8,128)(2,1)} %get-tuple-element.152), channel_id=1, source_target_pairs={{0,8},{8,0},{1,9},{9,1},{2,10},{10,2},{3,11},{11,3},{4,12},{12,4},... | collective-permute-start | bytes 1327112 | tf_op jit(solution)/shard_map/ppermute | solution.py:583
  271.0 16.3 %collective-permute-start.37 = (bf16[4,24,3072]{2,1,0:T(8,128)(2,1)}, bf16[4,24,3072]{2,1,0:T(8,128)(2,1)}, u32[]{:S(2)}, u32[]{:S(2)}) collective-permute-start(bf16[4,24,3072]{2,1,0:T(8,128)(2,1)} %fusion.8), channel_id=1, source_target_pairs={{0,1},{1,0},{2,3},{3,2},{4,5},{5,4},{6,7},{7,6},{8,9},{9,8},{10,11... | collective-permute-start | bytes 1769480 | tf_op jit(solution)/shard_map/ppermute | solution.py:583
  272.3 8.7 %collective-permute-start.40 = (bf16[4,2,24,576]{3,2,0,1:T(8,128)(2,1)}, bf16[4,2,24,576]{3,2,0,1:T(8,128)(2,1)}, u32[]{:S(2)}, u32[]{:S(2)}) collective-permute-start(bf16[4,2,24,576]{3,2,0,1:T(8,128)(2,1)} %fusion.9), channel_id=1, source_target_pairs={{0,16},{16,0},{1,17},{17,1},{2,18},{18,2},{3,19},{19,3},{4,20},{20... | collective-permute-start | bytes 663560 | tf_op jit(solution)/shard_map/ppermute | solution.py:583
  282.7 9.0 %copy-start.4 = (f32[4,2,24,576]{3,2,0,1:T(8,128)S(1)}, f32[4,2,24,576]{3,2,0,1:T(8,128)}, u32[]{:S(2)}) copy-start(f32[4,2,24,576]{3,2,0,1:T(8,128)} %bitcast_add_fusion.2) | copy-start | bytes 1327108
  286.8 4.9 %collective-permute-start.41 = (bf16[4,24,576]{2,1,0:T(8,128)(2,1)S(1)}, bf16[4,24,576]{2,1,0:T(8,128)(2,1)S(1)}, u32[]{:S(2)}, u32[]{:S(2)}) collective-permute-start(bf16[4,24,576]{2,1,0:T(8,128)(2,1)S(1)} %fusion.11), channel_id=1, source_target_pairs={{0,1},{1,0},{2,3},{3,2},{4,5},{5,4},{6,7},{7,6},{8,9},{9,8},{10,11... | collective-permute-start | bytes 331784 | tf_op jit(solution)/shard_map/ppermute | solution.py:583
  292.6 21.1 %all-to-all-start.2 = ((bf16[4,24,3648]{2,1,0:T(8,128)(2,1)}), bf16[4,24,3648]{2,1,0:T(8,128)(2,1)}, u32[]{:S(2)}, u32[]{:S(2)}) async-start(bf16[4,24,3648]{2,1,0:T(8,128)(2,1)} %pad_maximum_fusion), calls=%async_computation.2 | async-start | bytes 1425408 | tf_op jit(solution)/shard_map/all_to_all | solution.py:766
  298.2 8.2 %copy-start.9 = (bf16[24,3072]{1,0:T(8,128)(2,1)S(1)}, bf16[24,3072]{1,0:T(8,128)(2,1)}, u32[]{:S(2)}) copy-start(bf16[24,3072]{1,0:T(8,128)(2,1)} %copy-done.8) | copy-start | bytes 442372
  (20 other events, 44.0 us)
Sparse Core Ops, SparseCore 0:
  12.9 115.8 all-gather.2
  131.7 62.3 all-gather.4

commit v3 on v2

--- a/solution.py
+++ b/solution.py
@@ -549,7 +549,11 @@
                 start = part * width + (g * heads + h) * HEAD
                 at = (h * 3 + part) * HEAD
                 qkv_ref[:, start : start + HEAD] = made[:, at : at + HEAD]
-    norm_ref[...] = norm / gain_ref[...]
+    row = lax.broadcasted_iota(jnp.int32, (share, share), 0)
+    column = lax.broadcasted_iota(jnp.int32, (share, share), 1)
+    norm_ref[...] = jnp.sum(
+        jnp.where(row == column, norm / gain_ref[...], 0.0), axis=0, keepdims=True
+    )
 
 
 def last_shares(got, weight, gain):
@@ -564,7 +568,7 @@
         out_shape=[
             jax.ShapeDtypeStruct((wide, share, width), F32),
             jax.ShapeDtypeStruct((share, 3 * width), F32),
-            jax.ShapeDtypeStruct((share, 1), F32),
+            jax.ShapeDtypeStruct((1, share), F32),
         ],
         compiler_params=pltpu.CompilerParams(vmem_limit_bytes=VMEM_LIMIT),
         name="last_shares",
@@ -781,7 +785,7 @@
         second, turned.swapaxes(0, 1), own_gain_one[:, None]
     )
     down_share = down_share.reshape(wide * share, width)
-    first_share = first_share[:, 0]
+    first_share = first_share.reshape(share)
     return (
         mixed,
         input_grad,

time: 329 us -> 328 us (level)
  no operation moved by 1% of the time
where the time goes in v3:
time: 328 us; the launch traced here: 323 us
  waiting for transfers between devices  99.2 us (30%)
  Pallas kernels  93.7 us (29%)
  starting transfers between devices  66.6 us (20%)
  local copies, waits for them, and re-layouts  25.4 us (8%)
  other arithmetic  22.4 us (7%)
  between operations  15.5 us (5%)
    ppermute x42, waiting for transfers between devices, shift(): return lax.ppermute(value, axis, [(i, (i + step) % n) for i in range(n)])  73 us
    ppermute x42, starting transfers between devices, shift(): return lax.ppermute(value, axis, [(i, (i + step) % n) for i in range(n)])  52.8 us
    pallas_call x3, Pallas kernels, attention_backward(): pl.pallas_call(functools.partial(attention_backward_kernel, rows, n_own),...  31.1 us
    pallas_call x1, Pallas kernels, middle(): pl.pallas_call(functools.partial(middle_kernel, (n_g, wide, width, rows,...  22.7 us
    all_to_all x1, waiting for transfers between devices, on_device(): parts = lax.all_to_all(parts, 'g', 0, 0)  21.3 us
    pallas_call x1, Pallas kernels, attention_forward(): pl.pallas_call(functools.partial(attention_forward_kernel, n_own), grid=(...  19.7 us
    add x4, other arithmetic, add_high(): total = total + term.astype(F32)  6.78 us
    convert_element_type x3, other arithmetic, add_low(): return add_high(*terms).astype(BF16)  6.72 us
  transfers between devices with their start and end apart: 47, of which 16 were waited for; matrix products, arithmetic and copies ran while one was open for 11% of the time, Pallas kernels for 28%

profile of v3, /device:TPU:0, one launch (start us, length us, event | category | flops | bytes accessed | tf_op | source)
XLA Modules:
  0.0 322.9 jit_solution(13940638430974191747)
XLA Ops:
  9.2 1.2 reshape.93
  10.6 1.3 reshape.94
  13.5 5.1 %collective-permute-start = (bf16[320,768]{1,0:T(8,128)(2,1)S(1)}, bf16[320,768]{1,0:T(8,128)(2,1)S(1)}, u32[]{:S(2)}, u32[]{:S(2)}) collective-permute-start(bf16[320,768]{1,0:T(8,128)(2,1)S(1)} %fusion.6.refs_0_), channel_id=1, source_target_pairs={{0,6},{2,0},{4,2},{6,4},{1,7},{3,1},{5,3},{7,5},{8,14},{10,8},{12,... | collective-permute-start | bytes 1474568 | tf_op jit(solution)/shard_map/ppermute | solution.py:587
  18.6 1.5 collective-permute-start.2
  21.3 5.1 %all-to-all-start = ((bf16[4,24,576]{2,1,0:T(8,128)(2,1)}), bf16[4,24,576]{2,1,0:T(8,128)(2,1)S(1)}, u32[]{:S(2)}, u32[]{:S(2)}) async-start(bf16[4,24,576]{2,1,0:T(8,128)(2,1)} %reshape.91), calls=%async_computation | async-start | bytes 245760 | tf_op jit(solution)/shard_map/all_to_all | solution.py:664
  27.6 21.3 %all-to-all-done = bf16[4,24,576]{2,1,0:T(8,128)(2,1)S(1)} async-done(((bf16[4,24,576]{2,1,0:T(8,128)(2,1)}), bf16[4,24,576]{2,1,0:T(8,128)(2,1)S(1)}, u32[]{:S(2)}, u32[]{:S(2)}) %all-to-all-start) | async-done | bytes 110624 | tf_op jit(solution)/shard_map/all_to_all | solution.py:664
  49.0 1.6 collective-permute-start.7
  50.6 4.9 %collective-permute-done.7 = bf16[4,24,576]{2,1,0:T(8,128)(2,1)S(1)} collective-permute-done((bf16[4,24,576]{2,1,0:T(8,128)(2,1)S(1)}, bf16[4,24,576]{2,1,0:T(8,128)(2,1)S(1)}, u32[]{:S(2)}, u32[]{:S(2)}) %collective-permute-start.7) | collective-permute-done | bytes 110624 | tf_op jit(solution)/shard_map/ppermute | solution.py:587
  55.6 4.1 %collective-permute-start.3 = (bf16[320,768]{1,0:T(8,128)(2,1)S(1)}, bf16[320,768]{1,0:T(8,128)(2,1)}, u32[]{:S(2)}, u32[]{:S(2)}) collective-permute-start(bf16[320,768]{1,0:T(8,128)(2,1)S(1)} %collective-permute-done.refs_1_), channel_id=1, source_target_pairs={{0,6},{2,0},{4,2},{6,4},{1,7},{3,1},{5,3},{7,5},{8,14},{10,8},{12,... | collective-permute-start | bytes 1474568 | tf_op jit(solution)/shard_map/ppermute | solution.py:587
  59.9 1.5 collective-permute-start.9
  61.4 2.5 collective-permute-start.4
  64.0 14.8 %collective-permute-done.3.refs_2_ = bf16[320,768]{1,0:T(8,128)(2,1)} collective-permute-done((bf16[320,768]{1,0:T(8,128)(2,1)S(1)}, bf16[320,768]{1,0:T(8,128)(2,1)}, u32[]{:S(2)}, u32[]{:S(2)}) %collective-permute-start.3) | collective-permute-done | bytes 491552 | tf_op jit(solution)/shard_map/ppermute | solution.py:587
  78.8 1.5 collective-permute-start.5
  81.8 1.2 maximum_bitcast_fusion
  83.0 1.2 copy.22
  84.3 2.6 collective-permute-done.6.refs_7_
  86.9 20.1 %collective-permute-done.5.refs_6_ = bf16[320,768]{1,0:T(8,128)(2,1)} collective-permute-done((bf16[320,768]{1,0:T(8,128)(2,1)}, bf16[320,768]{1,0:T(8,128)(2,1)}, u32[]{:S(2)}, u32[]{:S(2)}) %collective-permute-start.5) | collective-permute-done | bytes 491552 | tf_op jit(solution)/shard_map/ppermute | solution.py:587
  107.0 19.7 %attention_forward.1 = (bf16[4,3,160,128]{3,2,1,0:T(8,128)(2,1)}, bf16[3,1280,128]{2,1,0:T(8,128)(2,1)}, bf16[3,2560,128]{2,1,0:T(8,128)(2,1)}, bf16[3,2560,128]{2,1,0:T(8,128)(2,1)}) custom-call(s32[1]{0:T(128)S(6)} %copy.44.live_ref, bf16[320,768]{1,0:T(8,128)(2,1)} %copy-done.1, bf16[320,768]{1,0:T(8,128)(2,1)} %copy-done.2, ...), custom_call_target="tpu_custom_call" | custom-call | tf_op jit(solution)/shard_map/attention_forward/pallas_call | solution.py:110
  126.6 1.8 slice_bitcast_fusion
  128.4 4.3 %collective-permute-start.12 = (bf16[3,160,128]{2,1,0:T(8,128)(2,1)S(1)}, bf16[3,160,128]{2,1,0:T(8,128)(2,1)S(1)}, u32[]{:S(2)}, u32[]{:S(2)}) collective-permute-start(bf16[3,160,128]{2,1,0:T(8,128)(2,1)S(1)} %get-tuple-element.160), channel_id=1, source_target_pairs={{0,6},{2,0},{4,2},{6,4},{1,7},{3,1},{5,3},{7,5},{8,14},{10,8},{12,... | collective-permute-start | bytes 368648 | tf_op jit(solution)/shard_map/ppermute | solution.py:587
  133.8 1.3 collective-permute-done.10.refs_4_
  135.2 2.7 collective-permute-done.11.refs_5_
  138.6 22.7 %middle.1 = (bf16[320,768]{1,0:T(8,128)(2,1)}, f32[320,768]{1,0:T(8,128)}, bf16[160,128]{1,0:T(8,128)(2,1)}, bf16[160,128]{1,0:T(8,128)(2,1)}, bf16[160,128]{1,0...) custom-call(s32[4]{0:T(128)} %pad_add_fusion.scalar_ref, ...), custom_call_target="tpu_custom_call" | custom-call | tf_op jit(solution)/shard_map/middle/pallas_call | solution.py:394
  161.3 2.5 collective-permute-start.13
  164.7 1.7 collective-permute-done.13.refs_1_
  166.3 4.7 %collective-permute-done.14.refs_2_ = bf16[160,128]{1,0:T(8,128)(2,1)S(1)} collective-permute-done((bf16[160,128]{1,0:T(8,128)(2,1)}, bf16[160,128]{1,0:T(8,128)(2,1)S(1)}, u32[]{:S(2)}, u32[]{:S(2)}) %collective-permute-start.14) | collective-permute-done | bytes 40992 | tf_op jit(solution)/shard_map/ppermute | solution.py:587
  171.1 1.5 collective-permute-start.18
  172.6 2.3 collective-permute-start.17
  175.0 10.3 %attention_backward.3 = (f32[4,320,128]{2,1,0:T(8,128)}, bf16[4,320,128]{2,1,0:T(8,128)(2,1)}, bf16[4,160,128]{2,1,0:T(8,128)(2,1)}) custom-call(bf16[4,3,160,128]{3,2,1,0:T(8,128)(2,1)} %get-tuple-element.87.out_ref, bf16[3,1280,128]{2,1,0:T(8,128)(2,1)} %get-tuple-element.91.query_ref, bf16[3,2560,128]{2,1,0:T(8,128)(2,1)} %get-tuple-element.92.key_ref, ...), custom_call_target="tpu_custom_call" | custom-call | tf_op jit(solution)/shard_map/attention_backward/pallas_call | solution.py:204
  187.0 1.8 add_convert_fusion
  189.7 1.9 collective-permute-start.21
  191.6 2.7 add_convert_fusion.1
  194.3 10.6 %attention_backward.4 = (f32[4,320,128]{2,1,0:T(8,128)}, bf16[4,320,128]{2,1,0:T(8,128)(2,1)}, bf16[4,160,128]{2,1,0:T(8,128)(2,1)}) custom-call(bf16[4,3,160,128]{3,2,1,0:T(8,128)(2,1)} %get-tuple-element.87.out_ref, bf16[3,1280,128]{2,1,0:T(8,128)(2,1)} %get-tuple-element.91.query_ref, bf16[3,2560,128]{2,1,0:T(8,128)(2,1)} %get-tuple-element.92.key_ref, ...), custom_call_target="tpu_custom_call" | custom-call | tf_op jit(solution)/shard_map/attention_backward/pallas_call | solution.py:204
  205.9 2.1 combine.3
  208.0 2.5 collective-permute-start.22
  210.4 2.4 collective-permute-start.24
  212.8 10.2 %attention_backward.5 = (f32[4,320,128]{2,1,0:T(8,128)}, bf16[4,320,128]{2,1,0:T(8,128)(2,1)}, bf16[4,160,128]{2,1,0:T(8,128)(2,1)}) custom-call(bf16[4,3,160,128]{3,2,1,0:T(8,128)(2,1)} %get-tuple-element.87.out_ref, bf16[3,1280,128]{2,1,0:T(8,128)(2,1)} %get-tuple-element.91.query_ref, bf16[3,2560,128]{2,1,0:T(8,128)(2,1)} %get-tuple-element.92.key_ref, ...), custom_call_target="tpu_custom_call" | custom-call | tf_op jit(solution)/shard_map/attention_backward/pallas_call | solution.py:204
  224.3 1.7 collective-permute-start.28
  226.0 2.1 combine.4
  229.2 2.7 convert_add_fusion
  234.1 1.7 collective-permute-start.38
  235.7 1.9 collective-permute-start.36
  237.6 2.4 collective-permute-start.31
  240.0 1.5 collective-permute-start.33
  241.5 4.4 %collective-permute-done.29.refs_4_ = bf16[480,128]{1,0:T(8,128)(2,1)S(1)} collective-permute-done((bf16[480,128]{1,0:T(8,128)(2,1)}, bf16[480,128]{1,0:T(8,128)(2,1)S(1)}, u32[]{:S(2)}, u32[]{:S(2)}) %collective-permute-start.29) | collective-permute-done | bytes 122912 | tf_op jit(solution)/shard_map/ppermute | solution.py:587
  245.9 2.9 collective-permute-done.31.refs_7_
  248.8 2.1 combine.5
  250.9 2.2 collective-permute-start.30
  253.1 1.7 collective-permute-start.32
  255.4 5.6 %group_grad.1 = (f32[2,192,576]{2,1,0:T(8,128)}, bf16[2,192,576]{2,1,0:T(8,128)(2,1)}) custom-call(s32[4]{0:T(128)} %pad_add_fusion.scalar_ref, bf16[320,768]{1,0:T(8,128)(2,1)} %copy-done.1, bf16[320,768]{1,0:T(8,128)(2,1)} %copy-done.2, bf16[320,768]{1,0:T(8,128)(2,1)} %collective-permute-done.3.refs_2_, bf16[320,768]{1,0:T(8,128)(2,1)} %copy-done.3, ...), custom_call_target="tpu_custom_call" | custom-call | tf_op jit(solution)/shard_map/group_grad/pallas_call | solution.py:478
  261.0 2.2 fusion
  263.2 4.5 %all-to-all-start.1 = ((bf16[4,24,3840]{2,1,0:T(8,128)(2,1)}), bf16[4,24,3840]{2,1,0:T(8,128)(2,1)}, u32[]{:S(2)}, u32[]{:S(2)}) async-start(bf16[4,24,3840]{2,1,0:T(8,128)(2,1)} %fusion), calls=%async_computation.1 | async-start | bytes 1474560 | tf_op jit(solution)/shard_map/all_to_all | solution.py:765
  267.8 2.2 convert_add_fusion.1
  272.5 8.4 %collective-permute-done.40 = bf16[4,2,24,576]{3,2,0,1:T(8,128)(2,1)} collective-permute-done((bf16[4,2,24,576]{3,2,0,1:T(8,128)(2,1)}, bf16[4,2,24,576]{3,2,0,1:T(8,128)(2,1)}, u32[]{:S(2)}, u32[]{:S(2)}) %collective-permute-start.40) | collective-permute-done | bytes 221216 | tf_op jit(solution)/shard_map/ppermute | solution.py:587
  280.9 1.8 bitcast_add_fusion.2
  282.7 3.1 all-to-all-done.1
  288.4 3.3 %collective-permute-done.41 = bf16[4,24,576]{2,1,0:T(8,128)(2,1)S(1)} collective-permute-done((bf16[4,24,576]{2,1,0:T(8,128)(2,1)S(1)}, bf16[4,24,576]{2,1,0:T(8,128)(2,1)S(1)}, u32[]{:S(2)}, u32[]{:S(2)}) %collective-permute-start.41) | collective-permute-done | bytes 110624 | tf_op jit(solution)/shard_map/ppermute | solution.py:587
  292.6 4.2 %all-to-all-start.2 = ((bf16[4,24,3648]{2,1,0:T(8,128)(2,1)}), bf16[4,24,3648]{2,1,0:T(8,128)(2,1)}, u32[]{:S(2)}, u32[]{:S(2)}) async-start(bf16[4,24,3648]{2,1,0:T(8,128)(2,1)} %pad_maximum_fusion), calls=%async_computation.2 | async-start | bytes 1425408 | tf_op jit(solution)/shard_map/all_to_all | solution.py:770
  298.1 6.3 %input_gradient.1 = f32[320,768]{1,0:T(8,128)} custom-call(s32[4]{0:T(128)} %pad_add_fusion.scalar_ref, bf16[320,768]{1,0:T(8,128)(2,1)} %token_ref.1, f32[320,768]{1,0:T(8,128)} %get-tuple-element.89.resid_ref, f32[1,768]{1,0:T(1,128)} %broadcast_in_dim.13.gain_ref, bf16[768,2560]{1,0:T(8,128)(2,1)} %all-gather.5.cloned.1.call-done.weight_ref, ...), custom_call_target="tpu_custom_call" | custom-call | tf_op jit(solution)/shard_map/input_gradient/pallas_call | solution.py:522
  304.4 1.3 convert_reduce_fusion
  307.5 1.2 copy.30
  308.8 2.6 reshape.101
  311.9 1.8 all-to-all-done.2.got_ref
  313.7 2.2 last_shares.1
  (178 shorter events, 28.7 us)
Async XLA Ops:
  7.2 130.7 %all-gather.3.cloned.1.call-start = ((), (), s32[]{:S(2)}) async-start(), calls=%async_computation.3 | async-start | bytes 10948608 | tf_op jit(solution)/shard_map/all_gather | solution.py:682
  11.9 8.2 %copy-start.21 = (f32[24,2304]{1,0:T(8,128)S(1)}, f32[24,2304]{1,0:T(8,128)}, u32[]{:S(2)}) copy-start(f32[24,2304]{1,0:T(8,128)} %param.12) | copy-start | bytes 663556
  13.5 13.3 %copy-start.1 = (bf16[320,768]{1,0:T(8,128)(2,1)}, bf16[320,768]{1,0:T(8,128)(2,1)S(1)}, u32[]{:S(2)}) copy-start(bf16[320,768]{1,0:T(8,128)(2,1)S(1)} %fusion.6.refs_0_) | copy-start | bytes 1474564
  13.5 35.4 %collective-permute-start = (bf16[320,768]{1,0:T(8,128)(2,1)S(1)}, bf16[320,768]{1,0:T(8,128)(2,1)S(1)}, u32[]{:S(2)}, u32[]{:S(2)}) collective-permute-start(bf16[320,768]{1,0:T(8,128)(2,1)S(1)} %fusion.6.refs_0_), channel_id=1, source_target_pairs={{0,6},{2,0},{4,2},{6,4},{1,7},{3,1},{5,3},{7,5},{8,14},{10,8},{12,... | collective-permute-start | bytes 1474568 | tf_op jit(solution)/shard_map/ppermute | solution.py:587
  18.6 30.4 %collective-permute-start.1 = (bf16[320,768]{1,0:T(8,128)(2,1)S(1)}, bf16[320,768]{1,0:T(8,128)(2,1)S(1)}, u32[]{:S(2)}, u32[]{:S(2)}) collective-permute-start(bf16[320,768]{1,0:T(8,128)(2,1)S(1)} %fusion.6.refs_0_), channel_id=1, source_target_pairs={{0,2},{2,4},{4,6},{6,0},{1,3},{3,5},{5,7},{7,1},{8,10},{10,12},{12... | collective-permute-start | bytes 1474568 | tf_op jit(solution)/shard_map/ppermute | solution.py:587
  18.6 30.4 %collective-permute-start.2 = (bf16[320,768]{1,0:T(8,128)(2,1)S(1)}, bf16[320,768]{1,0:T(8,128)(2,1)S(1)}, u32[]{:S(2)}, u32[]{:S(2)}) collective-permute-start(bf16[320,768]{1,0:T(8,128)(2,1)S(1)} %fusion.6.refs_0_), channel_id=1, source_target_pairs={{0,1},{1,0},{2,3},{3,2},{4,5},{5,4},{6,7},{7,6},{8,9},{9,8},{10,11... | collective-permute-start | bytes 1474568 | tf_op jit(solution)/shard_map/ppermute | solution.py:587
  21.3 27.6 %all-to-all-start = ((bf16[4,24,576]{2,1,0:T(8,128)(2,1)}), bf16[4,24,576]{2,1,0:T(8,128)(2,1)S(1)}, u32[]{:S(2)}, u32[]{:S(2)}) async-start(bf16[4,24,576]{2,1,0:T(8,128)(2,1)} %reshape.91), calls=%async_computation | async-start | bytes 245760 | tf_op jit(solution)/shard_map/all_to_all | solution.py:664
  26.4 186.4 %all-gather.5.cloned.1.call-start = ((), (), s32[]{:S(2)}) async-start(), calls=%async_computation.4 | async-start | bytes 4055040 | tf_op jit(solution)/shard_map/all_gather | solution.py:706
  26.8 33.1 %copy-start.12 = (bf16[24,4,576]{2,0,1:T(8,128)(2,1)}, bf16[24,4,576]{2,0,1:T(8,128)(2,1)S(1)}, u32[]{:S(2)}) copy-start(bf16[24,4,576]{2,0,1:T(8,128)(2,1)S(1)} %reshape.95) | copy-start | bytes 331780
  48.9 12.5 %copy-start.2 = (bf16[320,768]{1,0:T(8,128)(2,1)}, bf16[320,768]{1,0:T(8,128)(2,1)S(1)}, u32[]{:S(2)}) copy-start(bf16[320,768]{1,0:T(8,128)(2,1)S(1)} %collective-permute-done.refs_1_) | copy-start | bytes 1474564
  48.9 15.0 %copy-start.3 = (bf16[320,768]{1,0:T(8,128)(2,1)}, bf16[320,768]{1,0:T(8,128)(2,1)S(1)}, u32[]{:S(2)}) copy-start(bf16[320,768]{1,0:T(8,128)(2,1)S(1)} %collective-permute-done.1.refs_3_) | copy-start | bytes 1474564
  49.0 10.8 %copy-start.14 = (bf16[320,768]{1,0:T(8,128)(2,1)}, bf16[320,768]{1,0:T(8,128)(2,1)S(1)}, u32[]{:S(2)}) copy-start(bf16[320,768]{1,0:T(8,128)(2,1)S(1)} %collective-permute-done.2.refs_4_) | copy-start | bytes 1474564
  49.0 6.5 %collective-permute-start.7 = (bf16[4,24,576]{2,1,0:T(8,128)(2,1)S(1)}, bf16[4,24,576]{2,1,0:T(8,128)(2,1)S(1)}, u32[]{:S(2)}, u32[]{:S(2)}) collective-permute-start(bf16[4,24,576]{2,1,0:T(8,128)(2,1)S(1)} %all-to-all-done), channel_id=1, source_target_pairs={{0,1},{1,0},{2,3},{3,2},{4,5},{5,4},{6,7},{7,6},{8,9},{9,8},{10,11... | collective-permute-start | bytes 331784 | tf_op jit(solution)/shard_map/ppermute | solution.py:587
  55.6 4.2 %collective-permute-start.8 = (bf16[2,4,24,576]{3,2,1,0:T(8,128)(2,1)S(1)}, bf16[2,4,24,576]{3,2,1,0:T(8,128)(2,1)S(1)}, u32[]{:S(2)}, u32[]{:S(2)}) collective-permute-start(bf16[2,4,24,576]{3,2,1,0:T(8,128)(2,1)S(1)} %pad_maximum_fusion.2), channel_id=1, source_target_pairs={{0,8},{8,0},{1,9},{9,1},{2,10},{10,2},{3,11},{11,3},{4,12},{12,4},... | collective-permute-start | bytes 663560 | tf_op jit(solution)/shard_map/ppermute | solution.py:587
  55.6 23.2 %collective-permute-start.3 = (bf16[320,768]{1,0:T(8,128)(2,1)S(1)}, bf16[320,768]{1,0:T(8,128)(2,1)}, u32[]{:S(2)}, u32[]{:S(2)}) collective-permute-start(bf16[320,768]{1,0:T(8,128)(2,1)S(1)} %collective-permute-done.refs_1_), channel_id=1, source_target_pairs={{0,6},{2,0},{4,2},{6,4},{1,7},{3,1},{5,3},{7,5},{8,14},{10,8},{12,... | collective-permute-start | bytes 1474568 | tf_op jit(solution)/shard_map/ppermute | solution.py:587
  59.9 21.0 %collective-permute-start.9 = (bf16[2,2,4,24,576]{4,3,2,1,0:T(8,128)(2,1)S(1)}, bf16[2,2,4,24,576]{4,3,2,1,0:T(8,128)(2,1)S(1)}, u32[]{:S(2)}, u32[]{:S(2)}) collective-permute-start(bf16[2,2,4,24,576]{4,3,2,1,0:T(8,128)(2,1)S(1)} %pad_maximum_fusion.1), channel_id=1, source_target_pairs={{0,16},{16,0},{1,17},{17,1},{2,18},{18,2},{3,19},{19,3},{4,20},{20... | collective-permute-start | bytes 1327112 | tf_op jit(solution)/shard_map/ppermute | solution.py:587
  61.4 22.8 %collective-permute-start.4 = (bf16[320,768]{1,0:T(8,128)(2,1)S(1)}, bf16[320,768]{1,0:T(8,128)(2,1)}, u32[]{:S(2)}, u32[]{:S(2)}) collective-permute-start(bf16[320,768]{1,0:T(8,128)(2,1)S(1)} %collective-permute-done.refs_1_), channel_id=1, source_target_pairs={{0,1},{1,0},{2,3},{3,2},{4,5},{5,4},{6,7},{7,6},{8,9},{9,8},{10,11... | collective-permute-start | bytes 1474568 | tf_op jit(solution)/shard_map/ppermute | solution.py:587
  63.9 23.0 %collective-permute-start.6 = (bf16[320,768]{1,0:T(8,128)(2,1)S(1)}, bf16[320,768]{1,0:T(8,128)(2,1)}, u32[]{:S(2)}, u32[]{:S(2)}) collective-permute-start(bf16[320,768]{1,0:T(8,128)(2,1)S(1)} %collective-permute-done.1.refs_3_), channel_id=1, source_target_pairs={{0,1},{1,0},{2,3},{3,2},{4,5},{5,4},{6,7},{7,6},{8,9},{9,8},{10,11... | collective-permute-start | bytes 1474568 | tf_op jit(solution)/shard_map/ppermute | solution.py:587
  78.8 28.1 %collective-permute-start.5 = (bf16[320,768]{1,0:T(8,128)(2,1)}, bf16[320,768]{1,0:T(8,128)(2,1)}, u32[]{:S(2)}, u32[]{:S(2)}) collective-permute-start(bf16[320,768]{1,0:T(8,128)(2,1)} %collective-permute-done.3.refs_2_), channel_id=1, source_target_pairs={{0,1},{1,0},{2,3},{3,2},{4,5},{5,4},{6,7},{7,6},{8,9},{9,8},{10,11... | collective-permute-start | bytes 1474568 | tf_op jit(solution)/shard_map/ppermute | solution.py:587
  107.0 25.7 %copy-start.35 = (f32[768]{0:T(1024)S(1)}, f32[768]{0:T(1024)}, u32[]{:S(2)}) copy-start(f32[768]{0:T(1024)} %param.17) | copy-start | bytes 9220
  128.4 6.8 %collective-permute-start.10 = (bf16[3,160,128]{2,1,0:T(8,128)(2,1)S(1)}, bf16[3,160,128]{2,1,0:T(8,128)(2,1)S(1)}, u32[]{:S(2)}, u32[]{:S(2)}) collective-permute-start(bf16[3,160,128]{2,1,0:T(8,128)(2,1)S(1)} %get-tuple-element.162), channel_id=1, source_target_pairs={{0,2},{2,4},{4,6},{6,0},{1,3},{3,5},{5,7},{7,1},{8,10},{10,12},{12... | collective-permute-start | bytes 368648 | tf_op jit(solution)/shard_map/ppermute | solution.py:587
  128.4 9.5 %collective-permute-start.11 = (bf16[3,160,128]{2,1,0:T(8,128)(2,1)S(1)}, bf16[3,160,128]{2,1,0:T(8,128)(2,1)S(1)}, u32[]{:S(2)}, u32[]{:S(2)}) collective-permute-start(bf16[3,160,128]{2,1,0:T(8,128)(2,1)S(1)} %get-tuple-element.161), channel_id=1, source_target_pairs={{0,4},{2,6},{4,0},{6,2},{1,5},{3,7},{5,1},{7,3},{8,12},{10,14},{12... | collective-permute-start | bytes 368648 | tf_op jit(solution)/shard_map/ppermute | solution.py:587
  128.4 9.5 %collective-permute-start.12 = (bf16[3,160,128]{2,1,0:T(8,128)(2,1)S(1)}, bf16[3,160,128]{2,1,0:T(8,128)(2,1)S(1)}, u32[]{:S(2)}, u32[]{:S(2)}) collective-permute-start(bf16[3,160,128]{2,1,0:T(8,128)(2,1)S(1)} %get-tuple-element.160), channel_id=1, source_target_pairs={{0,6},{2,0},{4,2},{6,4},{1,7},{3,1},{5,3},{7,5},{8,14},{10,8},{12,... | collective-permute-start | bytes 368648 | tf_op jit(solution)/shard_map/ppermute | solution.py:587
  161.3 24.6 %collective-permute-start.16 = (bf16[192,3840]{1,0:T(8,128)(2,1)}, bf16[192,3840]{1,0:T(8,128)(2,1)S(1)}, u32[]{:S(2)}, u32[]{:S(2)}) collective-permute-start(bf16[192,3840]{1,0:T(8,128)(2,1)} %get-tuple-element.102), channel_id=1, source_target_pairs={{0,8},{8,0},{1,9},{9,1},{2,10},{10,2},{3,11},{11,3},{4,12},{12,4},... | collective-permute-start | bytes 4423688 | tf_op jit(solution)/shard_map/ppermute | solution.py:587
  161.3 5.0 %collective-permute-start.13 = (bf16[160,128]{1,0:T(8,128)(2,1)}, bf16[160,128]{1,0:T(8,128)(2,1)S(1)}, u32[]{:S(2)}, u32[]{:S(2)}) collective-permute-start(bf16[160,128]{1,0:T(8,128)(2,1)} %get-tuple-element.95), channel_id=1, source_target_pairs={{0,6},{2,0},{4,2},{6,4},{1,7},{3,1},{5,3},{7,5},{8,14},{10,8},{12,... | collective-permute-start | bytes 122888 | tf_op jit(solution)/shard_map/ppermute | solution.py:587
  163.9 7.2 %collective-permute-start.14 = (bf16[160,128]{1,0:T(8,128)(2,1)}, bf16[160,128]{1,0:T(8,128)(2,1)S(1)}, u32[]{:S(2)}, u32[]{:S(2)}) collective-permute-start(bf16[160,128]{1,0:T(8,128)(2,1)} %get-tuple-element.96), channel_id=1, source_target_pairs={{0,4},{2,6},{4,0},{6,2},{1,5},{3,7},{5,1},{7,3},{8,12},{10,14},{12... | collective-permute-start | bytes 122888 | tf_op jit(solution)/shard_map/ppermute | solution.py:587
  164.7 6.4 %collective-permute-start.15 = (bf16[160,128]{1,0:T(8,128)(2,1)}, bf16[160,128]{1,0:T(8,128)(2,1)S(1)}, u32[]{:S(2)}, u32[]{:S(2)}) collective-permute-start(bf16[160,128]{1,0:T(8,128)(2,1)} %get-tuple-element.97), channel_id=1, source_target_pairs={{0,2},{2,4},{4,6},{6,0},{1,3},{3,5},{5,7},{7,1},{8,10},{10,12},{12... | collective-permute-start | bytes 122888 | tf_op jit(solution)/shard_map/ppermute | solution.py:587
  166.3 8.6 %copy-start.31 = (bf16[160,128]{1,0:T(8,128)(2,1)}, bf16[160,128]{1,0:T(8,128)(2,1)S(1)}, u32[]{:S(2)}) copy-start(bf16[160,128]{1,0:T(8,128)(2,1)S(1)} %collective-permute-done.13.refs_1_) | copy-start | bytes 122884
  171.1 14.2 %collective-permute-start.19 = (bf16[2,160,128]{2,1,0:T(8,128)(2,1)}, bf16[2,160,128]{2,1,0:T(8,128)(2,1)S(1)}, u32[]{:S(2)}, u32[]{:S(2)}) collective-permute-start(bf16[2,160,128]{2,1,0:T(8,128)(2,1)} %get-tuple-element.108), channel_id=1, source_target_pairs={{0,2},{2,4},{4,6},{6,0},{1,3},{3,5},{5,7},{7,1},{8,10},{10,12},{12... | collective-permute-start | bytes 245768 | tf_op jit(solution)/shard_map/ppermute | solution.py:587
  171.1 14.7 %collective-permute-start.18 = (bf16[2,160,128]{2,1,0:T(8,128)(2,1)}, bf16[2,160,128]{2,1,0:T(8,128)(2,1)S(1)}, u32[]{:S(2)}, u32[]{:S(2)}) collective-permute-start(bf16[2,160,128]{2,1,0:T(8,128)(2,1)} %get-tuple-element.106), channel_id=1, source_target_pairs={{0,4},{2,6},{4,0},{6,2},{1,5},{3,7},{5,1},{7,3},{8,12},{10,14},{12... | collective-permute-start | bytes 245768 | tf_op jit(solution)/shard_map/ppermute | solution.py:587
  172.6 13.2 %collective-permute-start.17 = (bf16[2,160,128]{2,1,0:T(8,128)(2,1)}, bf16[2,160,128]{2,1,0:T(8,128)(2,1)S(1)}, u32[]{:S(2)}, u32[]{:S(2)}) collective-permute-start(bf16[2,160,128]{2,1,0:T(8,128)(2,1)} %get-tuple-element.104), channel_id=1, source_target_pairs={{0,6},{2,0},{4,2},{6,4},{1,7},{3,1},{5,3},{7,5},{8,14},{10,8},{12,... | collective-permute-start | bytes 245768 | tf_op jit(solution)/shard_map/ppermute | solution.py:587
  174.9 16.6 %collective-permute-start.20 = (bf16[192,3072]{1,0:T(8,128)(2,1)}, bf16[192,3072]{1,0:T(8,128)(2,1)}, u32[]{:S(2)}, u32[]{:S(2)}) collective-permute-start(bf16[192,3072]{1,0:T(8,128)(2,1)} %get-tuple-element.111), channel_id=1, source_target_pairs={{0,8},{8,0},{1,9},{9,1},{2,10},{10,2},{3,11},{11,3},{4,12},{12,4},... | collective-permute-start | bytes 3538952 | tf_op jit(solution)/shard_map/ppermute | solution.py:587
  175.0 12.1 %copy-start.6 = (bf16[192,3840]{1,0:T(8,128)(2,1)S(1)}, bf16[192,3840]{1,0:T(8,128)(2,1)}, u32[]{:S(2)}) copy-start(bf16[192,3840]{1,0:T(8,128)(2,1)} %get-tuple-element.101) | copy-start | bytes 4423684
  185.3 9.0 %copy-start.18 = (bf16[2,160,128]{2,1,0:T(8,128)(2,1)}, bf16[2,160,128]{2,1,0:T(8,128)(2,1)S(1)}, u32[]{:S(2)}) copy-start(bf16[2,160,128]{2,1,0:T(8,128)(2,1)S(1)} %collective-permute-done.19.refs_3_) | copy-start | bytes 245764
  185.3 25.2 %collective-permute-start.26 = (bf16[192,3840]{1,0:T(8,128)(2,1)}, bf16[192,3840]{1,0:T(8,128)(2,1)}, u32[]{:S(2)}, u32[]{:S(2)}) collective-permute-start(bf16[192,3840]{1,0:T(8,128)(2,1)} %get-tuple-element.130), channel_id=1, source_target_pairs={{0,8},{8,0},{1,9},{9,1},{2,10},{10,2},{3,11},{11,3},{4,12},{12,4},... | collective-permute-start | bytes 4423688 | tf_op jit(solution)/shard_map/ppermute | solution.py:587
  185.8 8.4 %copy-start.19 = (bf16[2,160,128]{2,1,0:T(8,128)(2,1)}, bf16[2,160,128]{2,1,0:T(8,128)(2,1)S(1)}, u32[]{:S(2)}) copy-start(bf16[2,160,128]{2,1,0:T(8,128)(2,1)S(1)} %collective-permute-done.18.refs_2_) | copy-start | bytes 245764
  185.8 8.4 %copy-start.20 = (bf16[2,160,128]{2,1,0:T(8,128)(2,1)}, bf16[2,160,128]{2,1,0:T(8,128)(2,1)S(1)}, u32[]{:S(2)}) copy-start(bf16[2,160,128]{2,1,0:T(8,128)(2,1)S(1)} %collective-permute-done.17.refs_1_) | copy-start | bytes 245764
  188.9 39.2 %collective-permute-start.27 = (bf16[192,3840]{1,0:T(8,128)(2,1)S(1)}, bf16[192,3840]{1,0:T(8,128)(2,1)S(1)}, u32[]{:S(2)}, u32[]{:S(2)}) collective-permute-start(bf16[192,3840]{1,0:T(8,128)(2,1)S(1)} %add_convert_fusion), channel_id=1, source_target_pairs={{0,16},{16,0},{1,17},{17,1},{2,18},{18,2},{3,19},{19,3},{4,20},{20... | collective-permute-start | bytes 4423688 | tf_op jit(solution)/shard_map/ppermute | solution.py:587
  189.7 15.5 %collective-permute-start.21 = (bf16[4,320,128]{2,1,0:T(8,128)(2,1)S(1)}, bf16[4,320,128]{2,1,0:T(8,128)(2,1)S(1)}, u32[]{:S(2)}, u32[]{:S(2)}) collective-permute-start(bf16[4,320,128]{2,1,0:T(8,128)(2,1)S(1)} %copy-done.36), channel_id=1, source_target_pairs={{0,1},{1,0},{2,3},{3,2},{4,5},{5,4},{6,7},{7,6},{8,9},{9,8},{10,11... | collective-permute-start | bytes 983048 | tf_op jit(solution)/shard_map/ppermute | solution.py:587
  204.9 21.1 %collective-permute-start.25 = (bf16[4,320,128]{2,1,0:T(8,128)(2,1)}, bf16[4,320,128]{2,1,0:T(8,128)(2,1)}, u32[]{:S(2)}, u32[]{:S(2)}) collective-permute-start(bf16[4,320,128]{2,1,0:T(8,128)(2,1)} %get-tuple-element.127), channel_id=1, source_target_pairs={{0,1},{1,0},{2,3},{3,2},{4,5},{5,4},{6,7},{7,6},{8,9},{9,8},{10,11... | collective-permute-start | bytes 983048 | tf_op jit(solution)/shard_map/ppermute | solution.py:587
  208.0 15.0 %collective-permute-start.22 = (bf16[480,128]{1,0:T(8,128)(2,1)}, bf16[480,128]{1,0:T(8,128)(2,1)S(1)}, u32[]{:S(2)}, u32[]{:S(2)}) collective-permute-start(bf16[480,128]{1,0:T(8,128)(2,1)} %get-tuple-element.119.refs_7_), channel_id=1, source_target_pairs={{0,2},{2,4},{4,6},{6,0},{1,3},{3,5},{5,7},{7,1},{8,10},{10,12},{12... | collective-permute-start | bytes 368648 | tf_op jit(solution)/shard_map/ppermute | solution.py:587
  210.4 12.6 %collective-permute-start.23 = (bf16[480,128]{1,0:T(8,128)(2,1)}, bf16[480,128]{1,0:T(8,128)(2,1)S(1)}, u32[]{:S(2)}, u32[]{:S(2)}) collective-permute-start(bf16[480,128]{1,0:T(8,128)(2,1)} %get-tuple-element.120.refs_10_), channel_id=1, source_target_pairs={{0,4},{2,6},{4,0},{6,2},{1,5},{3,7},{5,1},{7,3},{8,12},{10,14},{12... | collective-permute-start | bytes 368648 | tf_op jit(solution)/shard_map/ppermute | solution.py:587
  210.4 15.5 %collective-permute-start.24 = (bf16[480,128]{1,0:T(8,128)(2,1)}, bf16[480,128]{1,0:T(8,128)(2,1)S(1)}, u32[]{:S(2)}, u32[]{:S(2)}) collective-permute-start(bf16[480,128]{1,0:T(8,128)(2,1)} %get-tuple-element.121.refs_13_), channel_id=1, source_target_pairs={{0,6},{2,0},{4,2},{6,4},{1,7},{3,1},{5,3},{7,5},{8,14},{10,8},{12,... | collective-permute-start | bytes 368648 | tf_op jit(solution)/shard_map/ppermute | solution.py:587
  223.0 17.0 %collective-permute-start.35 = (bf16[192,3072]{1,0:T(8,128)(2,1)}, bf16[192,3072]{1,0:T(8,128)(2,1)}, u32[]{:S(2)}, u32[]{:S(2)}) collective-permute-start(bf16[192,3072]{1,0:T(8,128)(2,1)} %get-tuple-element.145), channel_id=1, source_target_pairs={{0,8},{8,0},{1,9},{9,1},{2,10},{10,2},{3,11},{11,3},{4,12},{12,4},... | collective-permute-start | bytes 3538952 | tf_op jit(solution)/shard_map/ppermute | solution.py:587
  224.3 9.8 %collective-permute-start.28 = (bf16[4,320,128]{2,1,0:T(8,128)(2,1)}, bf16[4,320,128]{2,1,0:T(8,128)(2,1)S(1)}, u32[]{:S(2)}, u32[]{:S(2)}) collective-permute-start(bf16[4,320,128]{2,1,0:T(8,128)(2,1)} %get-tuple-element.139), channel_id=1, source_target_pairs={{0,1},{1,0},{2,3},{3,2},{4,5},{5,4},{6,7},{7,6},{8,9},{9,8},{10,11... | collective-permute-start | bytes 983048 | tf_op jit(solution)/shard_map/ppermute | solution.py:587
  234.1 14.7 %copy-start.16 = (bf16[4,320,128]{2,1,0:T(8,128)(2,1)}, bf16[4,320,128]{2,1,0:T(8,128)(2,1)S(1)}, u32[]{:S(2)}) copy-start(bf16[4,320,128]{2,1,0:T(8,128)(2,1)S(1)} %collective-permute-done.28.refs_0_) | copy-start | bytes 983044
  234.1 27.0 %collective-permute-start.38 = (bf16[4,24,3840]{2,1,0:T(8,128)(2,1)}, bf16[4,24,3840]{2,1,0:T(8,128)(2,1)}, u32[]{:S(2)}, u32[]{:S(2)}) collective-permute-start(bf16[4,24,3840]{2,1,0:T(8,128)(2,1)} %fusion.7), channel_id=1, source_target_pairs={{0,1},{1,0},{2,3},{3,2},{4,5},{5,4},{6,7},{7,6},{8,9},{9,8},{10,11... | collective-permute-start | bytes 2211848 | tf_op jit(solution)/shard_map/ppermute | solution.py:587
  235.7 32.1 %collective-permute-start.36 = (bf16[192,3072]{1,0:T(8,128)(2,1)}, bf16[192,3072]{1,0:T(8,128)(2,1)}, u32[]{:S(2)}, u32[]{:S(2)}) collective-permute-start(bf16[192,3072]{1,0:T(8,128)(2,1)} %add_convert_fusion.1), channel_id=1, source_target_pairs={{0,16},{16,0},{1,17},{17,1},{2,18},{18,2},{3,19},{19,3},{4,20},{20... | collective-permute-start | bytes 3538952 | tf_op jit(solution)/shard_map/ppermute | solution.py:587
  237.6 8.3 %collective-permute-start.29 = (bf16[480,128]{1,0:T(8,128)(2,1)}, bf16[480,128]{1,0:T(8,128)(2,1)S(1)}, u32[]{:S(2)}, u32[]{:S(2)}) collective-permute-start(bf16[480,128]{1,0:T(8,128)(2,1)} %get-tuple-element.132.refs_8_), channel_id=1, source_target_pairs={{0,2},{2,4},{4,6},{6,0},{1,3},{3,5},{5,7},{7,1},{8,10},{10,12},{12... | collective-permute-start | bytes 368648 | tf_op jit(solution)/shard_map/ppermute | solution.py:587
  237.6 11.2 %collective-permute-start.31 = (bf16[480,128]{1,0:T(8,128)(2,1)}, bf16[480,128]{1,0:T(8,128)(2,1)S(1)}, u32[]{:S(2)}, u32[]{:S(2)}) collective-permute-start(bf16[480,128]{1,0:T(8,128)(2,1)} %get-tuple-element.133.refs_11_), channel_id=1, source_target_pairs={{0,4},{2,6},{4,0},{6,2},{1,5},{3,7},{5,1},{7,3},{8,12},{10,14},{12... | collective-permute-start | bytes 368648 | tf_op jit(solution)/shard_map/ppermute | solution.py:587
  240.0 8.8 %collective-permute-start.33 = (bf16[480,128]{1,0:T(8,128)(2,1)}, bf16[480,128]{1,0:T(8,128)(2,1)}, u32[]{:S(2)}, u32[]{:S(2)}) collective-permute-start(bf16[480,128]{1,0:T(8,128)(2,1)} %get-tuple-element.134.refs_14_), channel_id=1, source_target_pairs={{0,6},{2,0},{4,2},{6,4},{1,7},{3,1},{5,3},{7,5},{8,14},{10,8},{12,... | collective-permute-start | bytes 368648 | tf_op jit(solution)/shard_map/ppermute | solution.py:587
  245.9 15.1 %copy-start.25 = (bf16[480,128]{1,0:T(8,128)(2,1)}, bf16[480,128]{1,0:T(8,128)(2,1)S(1)}, u32[]{:S(2)}) copy-start(bf16[480,128]{1,0:T(8,128)(2,1)S(1)} %collective-permute-done.29.refs_4_) | copy-start | bytes 368644
  248.8 12.2 %copy-start.26 = (bf16[480,128]{1,0:T(8,128)(2,1)}, bf16[480,128]{1,0:T(8,128)(2,1)S(1)}, u32[]{:S(2)}) copy-start(bf16[480,128]{1,0:T(8,128)(2,1)S(1)} %collective-permute-done.31.refs_7_) | copy-start | bytes 368644
  250.9 16.8 %collective-permute-start.30 = (bf16[480,128]{1,0:T(8,128)(2,1)}, bf16[480,128]{1,0:T(8,128)(2,1)}, u32[]{:S(2)}, u32[]{:S(2)}) collective-permute-start(bf16[480,128]{1,0:T(8,128)(2,1)} %get-tuple-element.141.refs_9_), channel_id=1, source_target_pairs={{0,2},{2,4},{4,6},{6,0},{1,3},{3,5},{5,7},{7,1},{8,10},{10,12},{12... | collective-permute-start | bytes 368648 | tf_op jit(solution)/shard_map/ppermute | solution.py:587
  253.1 14.6 %collective-permute-start.32 = (bf16[480,128]{1,0:T(8,128)(2,1)}, bf16[480,128]{1,0:T(8,128)(2,1)}, u32[]{:S(2)}, u32[]{:S(2)}) collective-permute-start(bf16[480,128]{1,0:T(8,128)(2,1)} %get-tuple-element.142.refs_12_), channel_id=1, source_target_pairs={{0,4},{2,6},{4,0},{6,2},{1,5},{3,7},{5,1},{7,3},{8,12},{10,14},{12... | collective-permute-start | bytes 368648 | tf_op jit(solution)/shard_map/ppermute | solution.py:587
  254.7 12.9 %collective-permute-start.34 = (bf16[480,128]{1,0:T(8,128)(2,1)}, bf16[480,128]{1,0:T(8,128)(2,1)}, u32[]{:S(2)}, u32[]{:S(2)}) collective-permute-start(bf16[480,128]{1,0:T(8,128)(2,1)} %get-tuple-element.143.refs_15_), channel_id=1, source_target_pairs={{0,6},{2,0},{4,2},{6,4},{1,7},{3,1},{5,3},{7,5},{8,14},{10,8},{12,... | collective-permute-start | bytes 368648 | tf_op jit(solution)/shard_map/ppermute | solution.py:587
  263.2 22.5 %all-to-all-start.1 = ((bf16[4,24,3840]{2,1,0:T(8,128)(2,1)}), bf16[4,24,3840]{2,1,0:T(8,128)(2,1)}, u32[]{:S(2)}, u32[]{:S(2)}) async-start(bf16[4,24,3840]{2,1,0:T(8,128)(2,1)} %fusion), calls=%async_computation.1 | async-start | bytes 1474560 | tf_op jit(solution)/shard_map/all_to_all | solution.py:765
  267.7 3.6 %collective-permute-start.39 = (bf16[2,192,576]{2,1,0:T(8,128)(2,1)}, bf16[2,192,576]{2,1,0:T(8,128)(2,1)S(1)}, u32[]{:S(2)}, u32[]{:S(2)}) collective-permute-start(bf16[2,192,576]{2,1,0:T(8,128)(2,1)} %get-tuple-element.152), channel_id=1, source_target_pairs={{0,8},{8,0},{1,9},{9,1},{2,10},{10,2},{3,11},{11,3},{4,12},{12,4},... | collective-permute-start | bytes 1327112 | tf_op jit(solution)/shard_map/ppermute | solution.py:587
  270.9 16.3 %collective-permute-start.37 = (bf16[4,24,3072]{2,1,0:T(8,128)(2,1)}, bf16[4,24,3072]{2,1,0:T(8,128)(2,1)}, u32[]{:S(2)}, u32[]{:S(2)}) collective-permute-start(bf16[4,24,3072]{2,1,0:T(8,128)(2,1)} %fusion.8), channel_id=1, source_target_pairs={{0,1},{1,0},{2,3},{3,2},{4,5},{5,4},{6,7},{7,6},{8,9},{9,8},{10,11... | collective-permute-start | bytes 1769480 | tf_op jit(solution)/shard_map/ppermute | solution.py:587
  272.2 8.7 %collective-permute-start.40 = (bf16[4,2,24,576]{3,2,0,1:T(8,128)(2,1)}, bf16[4,2,24,576]{3,2,0,1:T(8,128)(2,1)}, u32[]{:S(2)}, u32[]{:S(2)}) collective-permute-start(bf16[4,2,24,576]{3,2,0,1:T(8,128)(2,1)} %fusion.9), channel_id=1, source_target_pairs={{0,16},{16,0},{1,17},{17,1},{2,18},{18,2},{3,19},{19,3},{4,20},{20... | collective-permute-start | bytes 663560 | tf_op jit(solution)/shard_map/ppermute | solution.py:587
  282.7 9.0 %copy-start.4 = (f32[4,2,24,576]{3,2,0,1:T(8,128)S(1)}, f32[4,2,24,576]{3,2,0,1:T(8,128)}, u32[]{:S(2)}) copy-start(f32[4,2,24,576]{3,2,0,1:T(8,128)} %bitcast_add_fusion.2) | copy-start | bytes 1327108
  286.7 4.9 %collective-permute-start.41 = (bf16[4,24,576]{2,1,0:T(8,128)(2,1)S(1)}, bf16[4,24,576]{2,1,0:T(8,128)(2,1)S(1)}, u32[]{:S(2)}, u32[]{:S(2)}) collective-permute-start(bf16[4,24,576]{2,1,0:T(8,128)(2,1)S(1)} %fusion.11), channel_id=1, source_target_pairs={{0,1},{1,0},{2,3},{3,2},{4,5},{5,4},{6,7},{7,6},{8,9},{9,8},{10,11... | collective-permute-start | bytes 331784 | tf_op jit(solution)/shard_map/ppermute | solution.py:587
  292.6 21.1 %all-to-all-start.2 = ((bf16[4,24,3648]{2,1,0:T(8,128)(2,1)}), bf16[4,24,3648]{2,1,0:T(8,128)(2,1)}, u32[]{:S(2)}, u32[]{:S(2)}) async-start(bf16[4,24,3648]{2,1,0:T(8,128)(2,1)} %pad_maximum_fusion), calls=%async_computation.2 | async-start | bytes 1425408 | tf_op jit(solution)/shard_map/all_to_all | solution.py:770
  298.1 8.2 %copy-start.9 = (bf16[24,3072]{1,0:T(8,128)(2,1)S(1)}, bf16[24,3072]{1,0:T(8,128)(2,1)}, u32[]{:S(2)}) copy-start(bf16[24,3072]{1,0:T(8,128)(2,1)} %copy-done.8) | copy-start | bytes 442372
  (20 other events, 44.0 us)
Sparse Core Ops, SparseCore 0:
  12.9 115.8 all-gather.2
  131.7 62.4 all-gather.4
